TPU v7x, 128 devices: a whole 4x4x4 slice. The times are simulated.
128 devices in a mesh: dom: 32 (over y, x, core), rep: 4 (over z).
Axes of the slice: x: 4, y: 4, z: 4, core: 2. Of those that a mesh axis runs over, the one named last changes fastest.
Arguments:
- features: bfloat16 [131072, 512], P('dom', 'rep'), may hold values from -6 to 6
- tile_values: bfloat16 [1024, 8, 128, 128], P('dom'), may hold values from -0.1875 to 0.1875
- tile_columns: int32 [1024, 8], P('dom'), may hold values from 0 to 63
- boundary_rows: int32 [32, 128], P('dom'), may hold values from 0 to 4095
- train_rows: int32 [32, 4096], P('dom'), may hold values from 0 to 4095
- shuffle: int32 [32, 4096], P('dom'), may hold values from 0 to 4095, each once within a row
- labels: int32 [131072], P(('dom', 'rep')), may hold values from 0 to 152
- first_weight: bfloat16 [4, 512, 1024], replicated, may hold values from -0.125 to 0.125
- mid_weight: bfloat16 [1024, 1024], replicated, may hold values from -0.1875 to 0.1875
- out_weight: bfloat16 [1024, 153], replicated, may hold values from -0.1875 to 0.1875
Outputs:
- first_grad: float32 [4, 512, 1024], P('rep', 'dom')
- mid_grad: float32 [1024, 1024], P(('dom', 'rep'))
- out_grad: float32 [1024, 153], P(('dom', 'rep'))
Inputs may be any that keep to these rules, and one draw needn't show every extreme that they name: `tile_columns`: an entry below 32 names a block of the partition's own rows, an entry c of 32 or more names block c - 32 of the gathered boundary rows. `train_rows`: indices may repeat. `shuffle`: each row is a permutation of 0 to 4095.
All inputs are finite; a program needn't handle non-finite values.
Results may differ from a plain program's by a relative error of at most 0.02.
Values may be sent and summed in bfloat16 or wider, within the bound.
No kernel may reach another device: no remote copies, remote signals or barrier semaphores. Data moves between devices by JAX's collectives and lax.ppermute only.
A program may use at most 128 MiB of HBM per device.

v0:
```python
import math

import jax
import jax.numpy as jnp
from jax import lax
from jax.sharding import PartitionSpec as P

HOPS = 3


root_two_pi = 0.7978845608028654
cubic_term = 0.044715


def gelu_pair(values):
    inner_arg = root_two_pi * (values + cubic_term * values * values * values)
    tanh_part = jnp.tanh(inner_arg)
    output = 0.5 * values * (1.0 + tanh_part)
    slope_out = 0.5 * (1.0 + tanh_part) + 0.5 * values * (
        1.0 - tanh_part * tanh_part
    ) * root_two_pi * (1.0 + 3.0 * cubic_term * values * values)
    return (output, slope_out)


def outer_rows(left_side, right_side):
    return lax.dot_general(
        left_side, right_side, (((0,), (0,)), ((), ())), preferred_element_type=jnp.float32
    )


def inner_cols(left_side, right_side):
    return lax.dot_general(
        left_side, right_side, (((1,), (1,)), ((), ())), preferred_element_type=jnp.float32
    )


def propagate(hop_now, bound_local, tile_columns, tile_values):
    exported = hop_now[bound_local]
    halo_rows = lax.all_gather(exported, "dom", axis=0, tiled=True)
    joined = jnp.concatenate([hop_now, halo_rows], axis=0)
    blocks = joined.reshape(-1, tile_values.shape[2], hop_now.shape[1])
    picked = blocks[tile_columns]
    summed = jnp.einsum("bkij,bkjf->bif", tile_values, picked, preferred_element_type=jnp.float32)
    return summed.reshape(hop_now.shape).astype(jnp.bfloat16)


def per_device(
    features,
    tile_values,
    tile_columns,
    boundary_rows,
    train_rows,
    shuffle,
    labels,
    first_weight,
    mid_weight,
    out_weight,
):
    hop_list = [features]
    bound_local = boundary_rows[0]
    for hop_index in range(HOPS):
        hop_list.append(propagate(hop_list[-1], bound_local, tile_columns, tile_values))
    picked_rows = train_rows[0][shuffle[0]]
    chosen = jnp.stack([hop[picked_rows] for hop in hop_list], axis=1)
    train_dev = chosen.shape[0]
    slab_width = chosen.shape[2]
    n_dom = lax.axis_size("dom")
    n_rep = lax.axis_size("rep")
    batch_rows = train_dev // n_rep
    hop_count = len(hop_list)
    quarter = hop_count * slab_width // n_dom
    hidden_width = mid_weight.shape[0]
    chosen = chosen.reshape(train_dev, 1, hop_count * slab_width)
    relayed = lax.all_to_all(
        lax.all_to_all(chosen, "dom", split_axis=0, concat_axis=0, tiled=True),
        "rep",
        split_axis=0,
        concat_axis=1,
        tiled=True,
    )
    inputs = relayed.reshape(batch_rows, n_rep * hop_count * slab_width)
    pre_first = jnp.dot(
        inputs,
        first_weight.reshape(n_rep * hop_count * slab_width, hidden_width),
        preferred_element_type=jnp.float32,
    )
    act_first, slope_first = gelu_pair(pre_first)
    act_first = act_first.astype(jnp.bfloat16)
    pre_mid = jnp.dot(act_first, mid_weight, preferred_element_type=jnp.float32)
    act_mid, slope_mid = gelu_pair(pre_mid)
    act_mid = act_mid.astype(jnp.bfloat16)
    logits = jnp.dot(act_mid, out_weight, preferred_element_type=jnp.float32)
    exp_logits = jnp.exp(logits)
    softmax_out = exp_logits / jnp.sum(exp_logits, axis=1, keepdims=True)
    classes = out_weight.shape[1]
    onehot = (labels[:, None] == jnp.arange(classes, dtype=jnp.int32)[None, :]).astype(jnp.float32)
    grad_logits = ((softmax_out - onehot) * (1.0 / math.sqrt(n_dom * train_dev))).astype(
        jnp.bfloat16
    )
    grad_mid = (inner_cols(grad_logits, out_weight) * slope_mid).astype(jnp.bfloat16)
    grad_first = (inner_cols(grad_mid, mid_weight) * slope_first).astype(jnp.bfloat16)
    columns = act_mid
    out_grad = lax.psum_scatter(
        outer_rows(columns, grad_logits), ("dom", "rep"), scatter_dimension=0, tiled=True
    )
    columns = act_first
    mid_grad = lax.psum_scatter(
        outer_rows(columns, grad_mid), ("dom", "rep"), scatter_dimension=0, tiled=True
    )
    permuted = (
        inputs.reshape(batch_rows, n_rep, n_dom, quarter)
        .transpose(0, 2, 1, 3)
        .reshape(batch_rows, n_rep * hop_count * slab_width)
    )
    columns = permuted
    first_share = lax.psum_scatter(
        outer_rows(columns, grad_first), ("dom", "rep"), scatter_dimension=0, tiled=True
    )
    return (first_share.reshape(1, quarter, hidden_width), mid_grad, out_grad)


def solution(mesh):
    placed = (
        P("dom", "rep"),
        P("dom", None, None, None),
        P("dom", None),
        P("dom", None),
        P("dom", None),
        P("dom", None),
        P(("dom", "rep")),
        P(),
        P(),
        P(),
    )
    return jax.shard_map(
        per_device,
        mesh=mesh,
        in_specs=placed,
        out_specs=(P("rep", "dom", None), P(("dom", "rep"), None), P(("dom", "rep"), None)),
        check_vma=False,
    )
```

profile of v0, /device:TPU:0, one launch (start us, length us, event | category | flops | bytes accessed | tf_op | source)
XLA Modules:
  0.0 2415.3 jit_solution(373140161364106574)
XLA Ops:
  11.6 44.4 %all-gather.7.cloned.1.call-done = bf16[4096,128]{1,0:T(8,128)(2,1)} async-done(((bf16[128,128]{1,0:T(8,128)(2,1)}), bf16[4096,128]{1,0:T(8,128)(2,1)}) %all-gather.7.cloned.1.call-update) | async-done | bytes 1048592 | tf_op jit(solution)/shard_map/all_gather | solution.py:39
  59.0 10.2 gather_fusion.3
  69.2 8.1 bitcast_convert_fusion.2
  78.7 42.1 %all-gather.9.cloned.1.call-done = bf16[4096,128]{1,0:T(8,128)(2,1)} async-done(((bf16[128,128]{1,0:T(8,128)(2,1)}), bf16[4096,128]{1,0:T(8,128)(2,1)}) %all-gather.9.cloned.1.call-update) | async-done | bytes 1048592 | tf_op jit(solution)/shard_map/all_gather | solution.py:39
  123.6 10.2 gather_fusion.6
  133.8 9.2 bitcast_convert_fusion.1
  146.2 23.0 gather_fusion
  169.3 15.6 gather_fusion.1
  184.9 14.9 gather_fusion.4
  199.7 15.7 gather_fusion.7
  218.2 10.2 gather_fusion.9
  228.4 8.1 bitcast_convert_fusion
  236.5 14.9 gather_fusion.10
  255.0 6.5 copy.20
  262.1 6.7 reduce
  268.8 6.5 copy.29
  275.3 7.8 reshape.217
  283.1 56.6 %all_to_all.20 = bf16[32,2,32768]{2,1,0:T(2,128)(2,1)} all-to-all(bf16[32,2,32768]{2,1,0:T(2,128)(2,1)} %reshape.217), channel_id=1, replica_groups=mesh['dom'=32,'rep'=4] {'dom'}, dimensions={0} | all-to-all | bytes 8388608 | tf_op jit(solution)/shard_map/all_to_all | solution.py:75
  339.6 19.7 reshape.218
  359.4 28.5 %reduce.1 = bf16[4096,512]{1,0:T(8,128)(2,1)} reduce(bf16[4096,1,512]{2,1,0:T(2,128)(2,1)} %reshape.218, bf16[]{:T(256)} %broadcast.170), dimensions={1}, to_apply=%reshape.218.reduce_sub_computation | reduce | bytes 8388610
  387.9 6.3 reshape.219
  394.1 55.1 %all_to_all.21 = bf16[4,2,262144]{2,1,0:T(2,128)(2,1)} all-to-all(bf16[4,2,262144]{2,1,0:T(2,128)(2,1)} %reshape.219), channel_id=1, replica_groups=mesh['dom'=32,'rep'=4] {'rep'}, dimensions={0} | all-to-all | bytes 8388608 | tf_op jit(solution)/shard_map/all_to_all | solution.py:74
  449.2 7.4 reshape.220
  456.6 6.6 copy.28
  463.2 6.3 copy.22
  469.5 7.6 fusion.25
  477.1 5.0 multiply_convert_fusion
  496.0 5.0 copy.23
  500.9 14.4 fusion.14
  515.3 604.9 %reduce-scatter.8.cloned.1.call-done = f32[8,153]{1,0:T(8,128)} async-done(((f32[1024,153]{1,0:T(8,128)}), f32[8,153]{1,0:T(8,128)}) %reduce-scatter.8.cloned.1.call-update) | async-done | bytes 4912 | tf_op jit(solution)/shard_map/reduce_scatter | solution.py:103
  1120.2 640.0 %reduce-scatter.6.cloned.1.call-done = f32[8,1024]{1,0:T(8,128)} async-done(((f32[1024,1024]{1,0:T(8,128)}), f32[8,1024]{1,0:T(8,128)}) %reduce-scatter.6.cloned.1.call-update) | async-done | bytes 32784 | tf_op jit(solution)/shard_map/reduce_scatter | solution.py:107
  1760.3 648.0 %reduce-scatter.4.cloned.1.call-done = f32[16,1024]{1,0:T(8,128)} async-done(((f32[2048,1024]{1,0:T(8,128)}), f32[16,1024]{1,0:T(8,128)}) %reduce-scatter.4.cloned.1.call-update) | async-done | bytes 65552 | tf_op jit(solution)/shard_map/reduce_scatter | solution.py:116
  (53 shorter events, 35.4 us)
Async XLA Ops:
  7.2 469.9 %copy-start = (bf16[1024,1024]{1,0:T(8,128)(2,1)S(1)}, bf16[1024,1024]{1,0:T(8,128)(2,1)}, u32[]{:S(2)}) copy-start(bf16[1024,1024]{1,0:T(8,128)(2,1)} %param.18) | copy-start | bytes 6291460
  7.2 48.8 %all-gather.7.cloned.1.call-start = ((), (), s32[]{:S(2)}) async-start(), calls=%async_computation.8 | async-start | bytes 1081344 | tf_op jit(solution)/shard_map/all_gather | solution.py:39
  10.7 110.2 %all-gather.9.cloned.1.call-start = ((), (), s32[]{:S(2)}) async-start(), calls=%async_computation.9 | async-start | bytes 1081344 | tf_op jit(solution)/shard_map/all_gather | solution.py:39
  78.7 136.7 %all-gather.11.cloned.1.call-start = ((), (), s32[]{:S(2)}) async-start(), calls=%async_computation.10 | async-start | bytes 1081344 | tf_op jit(solution)/shard_map/all_gather | solution.py:39
  133.8 12.4 copy-start.4
  143.0 3.2 copy-start.1
  145.6 974.6 %reduce-scatter.8.cloned.1.call-start = ((), (), s32[]{:S(2)}) async-start(), calls=%async_computation.7 | async-start | bytes 1056768 | tf_op jit(solution)/shard_map/reduce_scatter | solution.py:103
  199.7 15.7 copy-start.2
  477.1 5.1 copy-start.6
  477.1 5.1 copy-start.3
  477.1 5.9 copy-start.5
  484.8 1275.4 %reduce-scatter.6.cloned.1.call-start = ((), (), s32[]{:S(2)}) async-start(), calls=%async_computation.6 | async-start | bytes 4227072 | tf_op jit(solution)/shard_map/reduce_scatter | solution.py:107
  485.1 6.0 copy-start.7
  489.8 1.3 copy-start.8
  495.9 1912.3 %reduce-scatter.4.cloned.1.call-start = ((), (), s32[]{:S(2)}) async-start(), calls=%async_computation.5 | async-start | bytes 8454144 | tf_op jit(solution)/shard_map/reduce_scatter | solution.py:116
Sparse Core Ops, SparseCore 0:
  10.9 45.0 all-gather.6
  78.8 41.9 all-gather.8
  145.7 41.9 all-gather.10
  485.0 635.2 reduce-scatter.7
  1123.1 637.0 reduce-scatter.5
  1763.0 645.1 reduce-scatter.3
where the time goes:
time: 2430 us; the launch traced here: 2420 us
  waiting for transfers between devices  1980 us (81%)
  local copies, waits for them, and re-layouts  195 us (8%)
  blocking collectives  112 us (5%)
  matrix products  64.4 us (3%)
  other arithmetic  49 us (2%)
    reduce_scatter x1, waiting for transfers between devices, per_device(): lax.psum_scatter(outer_rows(columns, grad_first), ('dom', 'rep'), scatter...  648 us
    reduce_scatter x1, waiting for transfers between devices, per_device(): lax.psum_scatter(outer_rows(columns, grad_mid), ('dom', 'rep'), scatter_d...  640 us
    reduce_scatter x1, waiting for transfers between devices, per_device(): lax.psum_scatter(outer_rows(columns, grad_logits), ('dom', 'rep'), scatte...  605 us
    all_gather x3, waiting for transfers between devices, propagate(): halo_rows = lax.all_gather(exported, 'dom', axis=0, tiled=True)  86.5 us
    gather x4, local copies, waits for them, and re-layouts, per_device(): chosen = jnp.stack([hop[picked_rows] for hop in hop_list], axis=1)  61 us
    all_to_all x1, blocking collectives, per_device(): lax.all_to_all(chosen, 'dom', split_axis=0, concat_axis=0, tiled=True)  56.6 us
    unnamed x24, local copies, waits for them, and re-layouts  55.7 us
    all_to_all x1, blocking collectives, per_device(): lax.all_to_all(lax.all_to_all(chosen, 'dom', split_axis=0, concat_axis=0,...  55.1 us
  transfers between devices with their start and end apart: 6, of which 5 were waited for; matrix products, arithmetic and copies ran while one was open for 4% of the time, Pallas kernels for 0%

commit v1 on v0

v1 whole, which is shorter than its diff:
```python
import functools
import math

import jax
import jax.numpy as jnp
from jax import lax
from jax.experimental import pallas as pl
from jax.experimental.pallas import tpu as pltpu
from jax.sharding import Mesh, PartitionSpec as P

HOPS = 3
TILE = 128
NB = 32
K = 8
R = 4096
HID = 1024
C = 153
CP = 256
Y, X, CORE, REP = 4, 4, 2, 4
DOM = Y * X * CORE
ROWS = R // REP
N_TRAIN = DOM * R
BF = jnp.bfloat16
F32 = jnp.float32
VM = 56 * 2**20

root_two_pi = 0.7978845608028654
cubic_term = 0.044715


def gelu_pair(v):
    sq = v * v
    t = jnp.tanh(root_two_pi * (v + cubic_term * sq * v))
    half = 0.5 * (1.0 + t)
    slope = half + (0.5 * root_two_pi) * v * (1.0 - t * t) * (
        1.0 + (3.0 * cubic_term) * sq
    )
    return v * half, slope


def dot(a, b, ca, cb):
    return lax.dot_general(a, b, (((ca,), (cb,)), ((), ())), preferred_element_type=F32)


def params():
    return pltpu.CompilerParams(vmem_limit_bytes=VM)


def whole(memory_space=pltpu.VMEM):
    return pl.BlockSpec(memory_space=memory_space)


def struct(shape, dtype=BF):
    return jax.ShapeDtypeStruct(shape, dtype)


def export_kernel(pos, hop, brow, export, q0, q1, q2, q3):
    row = lax.broadcasted_iota(jnp.int32, (TILE, R), 1)
    mask = (row == brow[...]).astype(BF)
    export[...] = dot(mask, hop[...], 1, 0).astype(BF)
    for d, q in enumerate((q0, q1, q2, q3)):
        start = pl.multiple_of(lax.rem(pos[0] + d, REP) * ROWS, ROWS)
        q[...] = hop[pl.ds(start, ROWS), :]


def export_first(pos, hop, brow):
    return pl.pallas_call(
        export_kernel,
        in_specs=[whole(pltpu.SMEM), whole(), whole()],
        out_specs=[whole()] * 5,
        out_shape=[struct((TILE, TILE))] + [struct((ROWS, TILE))] * 4,
        compiler_params=params(),
        name="export_first",
        cost_estimate=pl.CostEstimate(
            flops=2 * TILE * TILE * R, bytes_accessed=4 * 2**20, transcendentals=0
        ),
    )(pos, hop, brow)


STEP = 4


def prop_kernel(last, cols, tiles, hop, near, far, brow, *rest):
    if last:
        q0, q1, q2, q3, joined, out = rest
    else:
        out, export, q0, q1, q2, q3, joined, acc = rest
    i = pl.program_id(0)

    @pl.when(i == 0)
    def _():
        joined[:R] = hop[...]
        joined[R : R + R // 2] = near[...]
        joined[R + R // 2 :] = far[...]
        if not last:
            acc[...] = jnp.zeros_like(acc)

    for s in range(STEP):
        b = i * STEP + s
        parts = []
        for k in range(K):
            at = pl.multiple_of(cols[b * K + k] * TILE, TILE)
            parts.append(joined[pl.ds(at, TILE), :])
        left = jnp.concatenate([tiles[s, k] for k in range(K)], axis=1)
        got = dot(left, jnp.concatenate(parts, axis=0), 1, 0).astype(BF)
        out[pl.ds(pl.multiple_of(b * TILE, TILE), TILE), :] = got
        if not last:
            row = lax.broadcasted_iota(jnp.int32, (TILE, TILE), 1) + b * TILE
            mask = (row == brow[...]).astype(BF)
            acc[...] += dot(mask, got, 1, 0)

    @pl.when(i == NB // STEP - 1)
    def _():
        if not last:
            export[...] = acc[...].astype(BF)
        r = cols[NB * K]
        for d, q in enumerate((q0, q1, q2, q3)):
            start = pl.multiple_of(lax.rem(r + d, REP) * ROWS, ROWS)
            q[...] = out[pl.ds(start, ROWS), :]


def propagate(last, cols, tiles, hop, near, far, brow):
    def fixed(shape):
        return pl.BlockSpec(shape, lambda i, c: (0,) * len(shape))

    outs = [] if last else [(R, TILE), (TILE, TILE)]
    outs += [(ROWS, TILE)] * 4
    scratch = [pltpu.VMEM((2 * R, TILE), BF)]
    scratch += [pltpu.VMEM((R, TILE), BF) if last else pltpu.VMEM((TILE, TILE), F32)]
    return pl.pallas_call(
        functools.partial(prop_kernel, last),
        grid_spec=pltpu.PrefetchScalarGridSpec(
            num_scalar_prefetch=1,
            grid=(NB // STEP,),
            in_specs=[
                pl.BlockSpec((STEP, K, TILE, TILE), lambda i, c: (i, 0, 0, 0)),
                fixed((R, TILE)),
                fixed((R // 2, TILE)),
                fixed((R // 2, TILE)),
                fixed((TILE, TILE)),
            ],
            out_specs=[fixed(s) for s in outs],
            scratch_shapes=scratch,
        ),
        out_shape=[struct(s) for s in outs],
        compiler_params=params(),
        name="propagate_last" if last else "propagate",
        cost_estimate=pl.CostEstimate(
            flops=2 * NB * K * TILE**3, bytes_accessed=12 * 2**20, transcendentals=0
        ),
    )(cols, tiles, hop, near, far, brow)


def count_kernel(pos, labels, shuffle, train, out):
    first = lax.broadcasted_iota(jnp.int32, (DOM, TILE), 0)
    second = lax.broadcasted_iota(jnp.int32, (TILE, TILE), 0)
    slots = jnp.zeros((DOM, TILE), F32)
    for lo in range(0, DOM, 8):
        a, b = [], []
        for e in range(lo, lo + 8):
            slot = shuffle[e : e + 1, :]
            label = labels[e : e + 1, :].astype(F32)
            a.append(jnp.where(first == slot // TILE, label, 0.0).astype(BF))
            b.append((second == lax.rem(slot, TILE)).astype(BF))
        slots += dot(jnp.concatenate(a, axis=1), jnp.concatenate(b, axis=1), 1, 1)
    slots = slots.astype(jnp.int32)
    paper = lax.broadcasted_iota(jnp.int32, (ROWS, TILE), 0) + pos[0] * ROWS
    kind = lax.broadcasted_iota(jnp.int32, (CP, TILE), 0)
    total = jnp.zeros((ROWS, CP), F32)
    for lo in range(0, DOM, 8):
        a, b = [], []
        for e in range(lo, lo + 8):
            a.append((paper == train[e : e + 1, :]).astype(BF))
            b.append((kind == slots[e : e + 1, :]).astype(BF))
        total += dot(jnp.concatenate(a, axis=1), jnp.concatenate(b, axis=1), 1, 1)
    out[...] = total


def count_labels(pos, labels, shuffle, train):
    return pl.pallas_call(
        count_kernel,
        in_specs=[whole(pltpu.SMEM), whole(), whole(), whole()],
        out_specs=whole(),
        out_shape=struct((ROWS, CP), F32),
        compiler_params=params(),
        name="count_labels",
        cost_estimate=pl.CostEstimate(
            flops=2 * ROWS * R * CP, bytes_accessed=2 * 2**20, transcendentals=0
        ),
    )(pos, labels, shuffle, train)


MLP_ROWS = 256


def mlp_kernel(pos, *refs):
    pieces, (counts, w1, w2, w3, act1, act2, gl, gm, gf) = refs[:16], refs[16:]
    r = pos[0]
    pre1 = jnp.zeros((MLP_ROWS, HID), F32)
    for d in range(REP):
        slab = lax.rem(r + REP - d, REP)
        x = jnp.concatenate([pieces[4 * d + h][...] for h in range(HOPS + 1)], axis=1)
        pre1 += dot(x, w1[slab], 1, 0)
    a1, slope1 = gelu_pair(pre1)
    a1 = a1.astype(BF)
    act1[...] = a1
    a2, slope2 = gelu_pair(dot(a1, w2[...], 1, 0))
    a2 = a2.astype(BF)
    act2[...] = a2
    logits = dot(a2, w3[...], 1, 0)
    kind = lax.broadcasted_iota(jnp.int32, (MLP_ROWS, CP), 1)
    ex = jnp.where(kind < C, jnp.exp(logits), 0.0)
    probs = ex / jnp.sum(ex, axis=1, keepdims=True)
    drawn = counts[...]
    many = jnp.sum(drawn, axis=1, keepdims=True)
    g3 = ((probs * many - drawn) * (1.0 / math.sqrt(N_TRAIN))).astype(BF)
    gl[...] = g3
    g2 = (dot(g3, w3[...], 1, 1) * slope2).astype(BF)
    gm[...] = g2
    gf[...] = (dot(g2, w2[...], 1, 1) * slope1).astype(BF)


def mlp(pos, pieces, counts, w1, w2, w3):
    def fixed(shape):
        return pl.BlockSpec(shape, lambda i, c: (0,) * len(shape))

    def rows(width):
        return pl.BlockSpec((MLP_ROWS, width), lambda i, c: (i, 0))

    widths = (HID, HID, CP, HID, HID)
    return pl.pallas_call(
        mlp_kernel,
        grid_spec=pltpu.PrefetchScalarGridSpec(
            num_scalar_prefetch=1,
            grid=(ROWS // MLP_ROWS,),
            in_specs=[rows(TILE)] * 16
            + [rows(CP), fixed(w1.shape), fixed(w2.shape), fixed(w3.shape)],
            out_specs=[rows(w) for w in widths],
        ),
        out_shape=[struct((ROWS, w)) for w in widths],
        compiler_params=params(),
        name="mlp",
        cost_estimate=pl.CostEstimate(
            flops=2 * ROWS * HID * (4 * HID + 2 * CP),
            bytes_accessed=20 * 2**20,
            transcendentals=2 * ROWS * HID,
        ),
    )(pos, *pieces, counts, w1, w2, w3)


WIDE = (HID + CP) // 2


def outer_kernel(pos, act1, act2, gl, gm, keep, send):
    own = pos[1] == 0
    width = HID // Y
    for y in range(Y):
        cut = slice(y * width, (y + 1) * width)
        mid = dot(act1[:, cut], gm[...], 0, 0)
        out = dot(act2[:, cut], gl[...], 0, 0)
        both = jnp.concatenate([mid, out], axis=1).reshape(X, CORE, REP, 8, HID + CP)
        both = jnp.concatenate([both[..., :WIDE], both[..., WIDE:]], axis=3)
        zero, one = both[:, 0], both[:, 1]
        keep[y] = jnp.where(own, zero, one).astype(BF)
        send[y] = jnp.where(own, one, zero).astype(BF)


def outer_grads(pos, act1, act2, gl, gm):
    shape = (Y, X, REP, 16, WIDE)
    return pl.pallas_call(
        outer_kernel,
        in_specs=[whole(pltpu.SMEM)] + [whole()] * 4,
        out_specs=[whole()] * 2,
        out_shape=[struct(shape)] * 2,
        compiler_params=params(),
        name="outer_grads",
        cost_estimate=pl.CostEstimate(
            flops=2 * ROWS * HID * (HID + CP), bytes_accessed=8 * 2**20, transcendentals=0
        ),
    )(pos, act1, act2, gl, gm)


def first_kernel(pos, *refs):
    pieces, (gf, keep, send) = refs[:16], refs[16:]
    own = pos[1] == 0
    for d in range(REP):
        slab = lax.rem(pos[0] + REP - d, REP)
        for y in range(0, Y, 2):
            x = jnp.concatenate([pieces[4 * d + y][...], pieces[4 * d + y + 1][...]], axis=1)
            got = dot(x, gf[...], 0, 0).reshape(2, X, CORE, 16, HID)
            zero, one = got[:, :, 0], got[:, :, 1]
            kept = jnp.where(own, zero, one).astype(BF)
            sent = jnp.where(own, one, zero).astype(BF)
            for u in range(2):
                for v in range(X):
                    keep[y + u, v, slab] = kept[u, v]
                    send[y + u, v, slab] = sent[u, v]


def first_grads(pos, pieces, gf):
    shape = (Y, X, REP, 16, HID)
    return pl.pallas_call(
        first_kernel,
        in_specs=[whole(pltpu.SMEM)] + [whole()] * 17,
        out_specs=[whole()] * 2,
        out_shape=[struct(shape)] * 2,
        compiler_params=params(),
        name="first_grads",
        cost_estimate=pl.CostEstimate(
            flops=4 * ROWS * HID * HID, bytes_accessed=10 * 2**20, transcendentals=0
        ),
    )(pos, *pieces, gf)


def join_kernel(keep_f, got_f, keep_m, got_m, out):
    out[:, :, :HID] = (keep_f[...].astype(F32) + got_f[...].astype(F32)).astype(BF)
    out[:, :, HID:] = (keep_m[...].astype(F32) + got_m[...].astype(F32)).astype(BF)


def join_cores(keep_f, got_f, keep_m, got_m):
    n = Y * X * REP
    flat = [v.reshape(n, 16, v.shape[-1]) for v in (keep_f, got_f, keep_m, got_m)]

    def spec(width):
        return pl.BlockSpec((8, 16, width), lambda i: (i, 0, 0))

    return pl.pallas_call(
        join_kernel,
        grid=(n // 8,),
        in_specs=[spec(v.shape[-1]) for v in flat],
        out_specs=spec(HID + WIDE),
        out_shape=struct((n, 16, HID + WIDE)),
        compiler_params=params(),
        name="join_cores",
    )(*flat)


def total_kernel(parts, first, mid, out):
    total = jnp.sum(parts[...].astype(F32), axis=0)
    first[0] = total[:, :HID]
    rest = jnp.concatenate([total[:8, HID:], total[8:, HID:]], axis=1)
    mid[...] = rest[:, :HID]
    out[...] = rest[:, HID : HID + C]


def total_grads(parts):
    return pl.pallas_call(
        total_kernel,
        in_specs=[whole()],
        out_specs=[whole()] * 3,
        out_shape=[struct((1, 16, HID), F32), struct((8, HID), F32), struct((8, C), F32)],
        compiler_params=params(),
        name="total_grads",
    )(parts)


def shift(value, axis, by):
    size = lax.axis_size(axis)
    return lax.ppermute(value, axis, [(i, (i + by) % size) for i in range(size)])


def spread(export):
    for axis in ("y", "x"):
        export = jnp.concatenate([export] + [shift(export, axis, d) for d in (1, 2, 3)])
    return export, shift(export, "core", 1)


def per_device(
    features,
    tile_values,
    tile_columns,
    boundary_rows,
    train_rows,
    shuffle,
    labels,
    first_weight,
    mid_weight,
    out_weight,
):
    y, x, core, rep = (lax.axis_index(a) for a in ("y", "x", "core", "rep"))
    pos = jnp.stack([rep, core]).astype(jnp.int32)

    part = tile_columns - NB
    far = lax.rem(core + CORE - part % CORE, CORE)
    along_x = lax.rem(x + X - part // CORE % X, X)
    along_y = lax.rem(y + Y - part // (CORE * X), Y)
    halo_at = NB + (far * X + along_x) * Y + along_y
    cols = jnp.where(tile_columns < NB, tile_columns, halo_at).reshape(-1)
    cols = jnp.concatenate([cols, rep[None]]).astype(jnp.int32)
    brow = jnp.broadcast_to(boundary_rows.reshape(TILE, 1), (TILE, TILE))

    all_labels = lax.all_gather(labels, "rep", axis=0, tiled=True)
    all_labels = lax.all_gather(all_labels, ("y", "x", "core"), axis=0, tiled=True)
    dom = (y * X + x) * CORE + core
    own_labels = lax.dynamic_slice_in_dim(
        all_labels.reshape(DOM, DOM * TILE), dom * TILE, TILE, axis=1
    )
    counts = count_labels(
        pos, own_labels, shuffle.reshape(DOM, TILE), train_rows.reshape(DOM, TILE)
    )

    export, *quarters = export_first(pos, features, boundary_rows.reshape(TILE, 1))
    pieces = [[quarters[0]] + [shift(quarters[d], "rep", d) for d in (1, 2, 3)]]
    hop = features
    for h in range(HOPS):
        near, other = spread(export)
        last = h == HOPS - 1
        got = propagate(last, cols, tile_values, hop, near, other, brow)
        quarters = got[-4:]
        pieces.append([quarters[0]] + [shift(quarters[d], "rep", d) for d in (1, 2, 3)])
        if not last:
            hop, export = got[0], got[1]
    pieces = [pieces[h][d] for d in range(REP) for h in range(HOPS + 1)]

    w3 = jnp.pad(out_weight, ((0, 0), (0, CP - C)))
    act1, act2, gl, gm, gf = mlp(pos, pieces, counts, first_weight, mid_weight, w3)
    keep_m, send_m = outer_grads(pos, act1, act2, gl, gm)
    got_m = shift(send_m, "core", 1)
    keep_f, send_f = first_grads(pos, pieces, gf)
    got_f = shift(send_f, "core", 1)
    parts = join_cores(keep_f, got_f, keep_m, got_m)
    parts = lax.all_to_all(parts, ("y", "x", "rep"), split_axis=0, concat_axis=0, tiled=True)
    first, mid, out = total_grads(parts)
    return first, mid, out


def solution(mesh):
    fine = Mesh(mesh.devices.reshape(Y, X, CORE, REP), ("y", "x", "core", "rep"))
    dom = ("y", "x", "core")
    every = dom + ("rep",)
    placed = (
        P(dom, "rep"),
        P(dom, None, None, None),
        P(dom, None),
        P(dom, None),
        P(dom, None),
        P(dom, None),
        P(every),
        P(),
        P(),
        P(),
    )
    return jax.shard_map(
        per_device,
        mesh=fine,
        in_specs=placed,
        out_specs=(P("rep", dom, None), P(every, None), P(every, None)),
        check_vma=False,
    )
```

time: 2430 us -> 296 us (0.12)
  waiting for transfers between devices: 1980 us -> 43.2 us
  local copies, waits for them, and re-layouts: 195 us -> 10.3 us
  Pallas kernels: 0 us -> 88.7 us
  matrix products: 64.4 us -> 0 us
  starting transfers between devices: 0.92 us -> 55.2 us
  other arithmetic: 49 us -> 1.21 us
    reduce_scatter x3 -> x0, waiting for transfers between devices: 1890 us -> none  [the longest x1 648 us: per_device(): lax.psum_scatter(outer_rows(columns, grad_first), ('dom', 'rep'), scatter...]
    gather x11 -> x0, local copies, waits for them, and re-layouts: 121 us -> none  [the longest x4 61 us: per_device(): chosen = jnp.stack([hop[picked_rows] for hop in hop_list], axis=1)]
    pallas_call x0 -> x10, Pallas kernels: none -> 88.7 us  [the longest x3 35.6 us: propagate(): pl.pallas_call(functools.partial(prop_kernel, last), grid_spec=pltpu.Pref...]
    all_gather x3 -> x0, waiting for transfers between devices: 86.5 us -> none  [propagate(): halo_rows = lax.all_gather(exported, 'dom', axis=0, tiled=True)]
    dot_general x10 -> x0, matrix products: 64.4 us -> none  [the longest x3 25.4 us: propagate(): jnp.einsum('bkij,bkjf->bif', tile_values, picked, preferred_element_type=...]
    all_to_all x2 -> x1, blocking collectives: 112 us -> 52.1 us  [per_device(): lax.all_to_all(parts, ('y', 'x', 'rep'), split_axis=0, concat_axis=0, til...]
    ppermute x0 -> x35, starting transfers between devices: none -> 55.2 us  [shift(): lax.ppermute(value, axis, [(i, (i + by) % size) for i in range(size)])]
    unnamed x24 -> x70, local copies, waits for them, and re-layouts: 55.7 us -> 6.18 us
  transfers between devices with their start and end apart: 6 -> 35, of which waited for: 5 -> 24; matrix products, arithmetic and copies ran while one was open for 4% -> 2% of each run, Pallas kernels for 0% -> 8%
where the time goes in v1:
time: 296 us; the launch traced here: 295 us
  blocking collectives  95.6 us (32%)
  Pallas kernels  88.7 us (30%)
  starting transfers between devices  55.2 us (19%)
  waiting for transfers between devices  43.2 us (15%)
  local copies, waits for them, and re-layouts  10.3 us (3%)
    ppermute x35, starting transfers between devices, shift(): lax.ppermute(value, axis, [(i, (i + by) % size) for i in range(size)])  55.2 us
    all_to_all x1, blocking collectives, per_device(): lax.all_to_all(parts, ('y', 'x', 'rep'), split_axis=0, concat_axis=0, til...  52.1 us
    ppermute x35, waiting for transfers between devices, shift(): lax.ppermute(value, axis, [(i, (i + by) % size) for i in range(size)])  43.2 us
    pallas_call x3, Pallas kernels, propagate(): pl.pallas_call(functools.partial(prop_kernel, last), grid_spec=pltpu.Pref...  35.6 us
    all_gather x1, blocking collectives, per_device(): lax.all_gather(all_labels, ('y', 'x', 'core'), axis=0, tiled=True)  24.4 us
    all_gather x1, blocking collectives, per_device(): all_labels = lax.all_gather(labels, 'rep', axis=0, tiled=True)  19.1 us
    pallas_call x1, Pallas kernels, mlp(): pl.pallas_call(mlp_kernel, grid_spec=pltpu.PrefetchScalarGridSpec(num_sca...  18.2 us
    pallas_call x1, Pallas kernels, first_grads(): pl.pallas_call(first_kernel, in_specs=[whole(pltpu.SMEM)] + [whole()] * 1...  9.48 us
  transfers between devices with their start and end apart: 35, of which 24 were waited for; matrix products, arithmetic and copies ran while one was open for 2% of the time, Pallas kernels for 8%

profile of v1, /device:TPU:0, one launch (start us, length us, event | category | flops | bytes accessed | tf_op | source)
XLA Modules:
  0.0 295.1 jit_solution(7676398154538886984)
XLA Ops:
  2.7 2.7 export_first.1
  7.0 2.9 collective-permute-start.1
  15.6 2.7 collective-permute-start.4
  26.1 12.7 %propagate.2 = (bf16[4096,128]{1,0:T(8,128)(2,1)}, bf16[128,128]{1,0:T(8,128)(2,1)}, bf16[1024,128]{1,0:T(8,128)(2,1)}, bf16[1024,128]{1,0:T(8,128)(2,1)}, bf16[...) custom-call(s32[257]{0:T(512)} %pad_add_fusion.cols, bf16[32,8,128,128]{3,2,1,0:T(8,128)(2,1)} %tiles.5, ...), custom_call_target="tpu_custom_call" | custom-call | flops 1073741824 | bytes 12582912 | tf_op jit(solution)/shard_map/propagate/pallas_call | solution.py:130
  39.9 3.9 %collective-permute-start.8 = (bf16[128,128]{1,0:T(8,128)(2,1)}, bf16[128,128]{1,0:T(8,128)(2,1)S(1)}, u32[]{:S(2)}, u32[]{:S(2)}) collective-permute-start(bf16[128,128]{1,0:T(8,128)(2,1)} %get-tuple-element.37), channel_id=1, source_target_pairs={{0,64},{32,96},{64,0},{96,32},{1,65},{33,97},{65,1},{97,33},{2,66}... | collective-permute-start | bytes 98312 | tf_op jit(solution)/shard_map/ppermute | solution.py:359
  45.9 2.0 collective-permute-done.9
  49.3 2.8 collective-permute-start.11
  52.9 2.4 collective-permute-done.10
  59.9 12.9 %propagate.3 = (bf16[4096,128]{1,0:T(8,128)(2,1)}, bf16[128,128]{1,0:T(8,128)(2,1)}, bf16[1024,128]{1,0:T(8,128)(2,1)}, bf16[1024,128]{1,0:T(8,128)(2,1)}, bf16[...) custom-call(s32[257]{0:T(512)} %pad_add_fusion.cols, bf16[32,8,128,128]{3,2,1,0:T(8,128)(2,1)} %tiles.5, ...), custom_call_target="tpu_custom_call" | custom-call | flops 1073741824 | bytes 12582912 | tf_op jit(solution)/shard_map/propagate/pallas_call | solution.py:130
  73.7 2.8 collective-permute-start.15
  82.0 2.8 collective-permute-start.18
  85.2 3.0 %collective-permute-done.17 = bf16[512,128]{1,0:T(8,128)(2,1)S(1)} collective-permute-done((bf16[512,128]{1,0:T(8,128)(2,1)S(1)}, bf16[512,128]{1,0:T(8,128)(2,1)S(1)}, u32[]{:S(2)}, u32[]{:S(2)}) %collective-permute-start.17) | collective-permute-done | bytes 131104 | tf_op jit(solution)/shard_map/ppermute | solution.py:359
  89.9 2.0 collective-permute-start.21
  91.8 3.6 %collective-permute-start.25 = (bf16[1024,128]{1,0:T(8,128)(2,1)S(1)}, bf16[1024,128]{1,0:T(8,128)(2,1)S(1)}, u32[]{:S(2)}, u32[]{:S(2)}) collective-permute-start(bf16[1024,128]{1,0:T(8,128)(2,1)S(1)} %copy-done.13), channel_id=1, source_target_pairs={{0,2},{1,3},{2,0},{3,1},{4,6},{5,7},{6,4},{7,5},{8,10},{9,11},{10,... | collective-permute-start | bytes 786440 | tf_op jit(solution)/shard_map/ppermute | solution.py:359
  97.5 3.7 %collective-permute-done.21.refs_4_ = bf16[1024,128]{1,0:T(8,128)(2,1)S(1)} collective-permute-done((bf16[1024,128]{1,0:T(8,128)(2,1)S(1)}, bf16[1024,128]{1,0:T(8,128)(2,1)S(1)}, u32[]{:S(2)}, u32[]{:S(2)}) %collective-permute-start.21) | collective-permute-done | bytes 262176 | tf_op jit(solution)/shard_map/ppermute | solution.py:359
  101.1 7.4 %collective-permute-start.26 = (bf16[1024,128]{1,0:T(8,128)(2,1)S(1)}, bf16[1024,128]{1,0:T(8,128)(2,1)}, u32[]{:S(2)}, u32[]{:S(2)}) collective-permute-start(bf16[1024,128]{1,0:T(8,128)(2,1)S(1)} %copy-done.16), channel_id=1, source_target_pairs={{0,2},{1,3},{2,0},{3,1},{4,6},{5,7},{6,4},{7,5},{8,10},{9,11},{10,... | collective-permute-start | bytes 786440 | tf_op jit(solution)/shard_map/ppermute | solution.py:359
  108.8 2.0 collective-permute-start.23
  110.8 19.1 %all_gather.6 = s32[4096]{0:T(1024)S(1)} all-gather(s32[1024]{0:T(1024)S(1)} %copy-done.9), channel_id=1, replica_groups=mesh['y'=4,'x'=4,'core'=2,'rep'=4] {'rep'}, dimensions={0}, use_global_device_ids=true | all-gather | bytes 20480 | tf_op jit(solution)/shard_map/all_gather | solution.py:392
  129.9 24.4 %all_gather.7 = s32[131072]{0:T(1024)S(1)} all-gather(s32[4096]{0:T(1024)S(1)} %all_gather.6), channel_id=1, replica_groups=mesh['y'=4,'x'=4,'core'=2,'rep'=4] {'y','x','core'}, dimensions={0}, use_global_device_ids=true | all-gather | bytes 540672 | tf_op jit(solution)/shard_map/all_gather | solution.py:393
  155.5 10.0 %propagate_last.1 = (bf16[1024,128]{1,0:T(8,128)(2,1)}, bf16[1024,128]{1,0:T(8,128)(2,1)}, bf16[1024,128]{1,0:T(8,128)(2,1)}, bf16[1024,128]{1,0:T(8,128)(2,1)}) custom-call(s32[257]{0:T(512)} %pad_add_fusion.cols, bf16[32,8,128,128]{3,2,1,0:T(8,128)(2,1)} %tiles.5, bf16[4096,128]{1,0:T(8,128)(2,1)} %get-tuple-element.39.hop, bf16[2048,128]{1,0:T(8,128)(2,1)} %copy-done.3, ...), custom_call_target="tpu_custom_call" | custom-call | flops 1073741824 | bytes 12582912 | tf_op jit(solution)/shard_map/propagate_last/pallas_call | solution.py:130
  169.1 2.1 collective-permute-start.28
  173.7 5.1 %count_labels.1.refs_16_ = f32[1024,256]{1,0:T(8,128)} custom-call(s32[2]{0:T(128)} %pad_add_fusion.1.pos, s32[32,128]{1,0:T(8,128)} %constant_dynamic-slice_fusion.labels, s32[32,128]{1,0:T(8,128)} %bitcast.16, s32[32,128]{1,0:T(8,128)} %bitcast.17), custom_call_target="tpu_custom_call" | custom-call | flops 2147483648 | bytes 2097152 | tf_op jit(solution)/shard_map/count_labels/pallas_call | solution.py:180
  178.7 2.3 collective-permute-done.31.refs_14_
  181.8 5.1 %collective-permute-done.28.refs_11_ = bf16[1024,128]{1,0:T(8,128)(2,1)S(1)} collective-permute-done((bf16[1024,128]{1,0:T(8,128)(2,1)}, bf16[1024,128]{1,0:T(8,128)(2,1)S(1)}, u32[]{:S(2)}, u32[]{:S(2)}) %collective-permute-start.28) | collective-permute-done | bytes 262176 | tf_op jit(solution)/shard_map/ppermute | solution.py:359
  187.0 4.8 %collective-permute-done.32.refs_15_ = bf16[1024,128]{1,0:T(8,128)(2,1)S(1)} collective-permute-done((bf16[1024,128]{1,0:T(8,128)(2,1)}, bf16[1024,128]{1,0:T(8,128)(2,1)S(1)}, u32[]{:S(2)}, u32[]{:S(2)}) %collective-permute-start.32) | collective-permute-done | bytes 262176 | tf_op jit(solution)/shard_map/ppermute | solution.py:359
  192.5 18.2 %mlp.1 = (bf16[1024,1024]{1,0:T(8,128)(2,1)}, bf16[1024,1024]{1,0:T(8,128)(2,1)}, bf16[1024,256]{1,0:T(8,128)(2,1)}, bf16[1024,1024]{1,0:T(8,128)(2,1)}, bf16[1024,1024]{1,0:T(8,128)(2,1)}) custom-call(s32[2]{0:T(128)} %pad_add_fusion.1.pos, bf16[1024,128]{1,0:T(8,128)(2,1)} %get-tuple-element.33.refs_0_, bf16[1024,128]{1,0:T(8,128)(2,1)} %get-tuple-element.35.refs_1_, ...), custom_call_target="tpu_custom_call" | custom-call | flops 9663676416 | bytes 20971520 | tf_op jit(solution)/shard_map/mlp/pallas_call | solution.py:231
  210.7 9.5 %first_grads.1 = (bf16[4,4,4,16,1024]{4,3,2,1,0:T(8,128)(2,1)}, bf16[4,4,4,16,1024]{4,3,2,1,0:T(8,128)(2,1)}) custom-call(s32[2]{0:T(128)} %pad_add_fusion.1.pos, bf16[1024,128]{1,0:T(8,128)(2,1)} %get-tuple-element.33.refs_0_, bf16[1024,128]{1,0:T(8,128)(2,1)} %get-tuple-element.35.refs_1_, bf16[1024,128]{1,0:T(8,128)(2,1)} %get-tuple-element.38.refs_2_, ...), custom_call_target="tpu_custom_call" | custom-call | flops 4294967296 | bytes 10485760 | tf_op jit(solution)/shard_map/first_grads/pallas_call | solution.py:302
  220.2 7.5 %outer_grads.1 = (bf16[4,4,4,16,640]{4,3,2,1,0:T(8,128)(2,1)}, bf16[4,4,4,16,640]{4,3,2,1,0:T(8,128)(2,1)}) custom-call(s32[2]{0:T(128)} %pad_add_fusion.1.pos, bf16[1024,1024]{1,0:T(8,128)(2,1)} %get-tuple-element.57.act1, bf16[1024,1024]{1,0:T(8,128)(2,1)} %get-tuple-element.58.act2, bf16[1024,256]{1,0:T(8,128)(2,1)} %get-tuple-element.59.gl, ...), custom_call_target="tpu_custom_call" | custom-call | flops 2684354560 | bytes 8388608 | tf_op jit(solution)/shard_map/outer_grads/pallas_call | solution.py:270
  228.2 2.9 collective-permute-done.34
  232.9 7.1 %join_cores.1 = bf16[64,16,1664]{2,1,0:T(8,128)(2,1)} custom-call(bf16[64,16,1024]{2,1,0:T(8,128)(2,1)} %bitcast.10, bf16[64,16,1024]{2,1,0:T(8,128)(2,1)} %bitcast.11, bf16[64,16,640]{2,1,0:T(8,128)(2,1)} %bitcast.12, bf16[64,16,640]{2,1,0:T(8,128)(2,1)} %bitcast.13), custom_call_target="tpu_custom_call" | custom-call | tf_op jit(solution)/shard_map/join_cores/pallas_call | solution.py:327
  239.9 52.1 %all_to_all.5.parts = bf16[64,16,1664]{2,1,0:T(8,128)(2,1)} all-to-all(bf16[64,16,1664]{2,1,0:T(8,128)(2,1)} %join_cores.1), channel_id=1, replica_groups=mesh['y'=4,'x'=4,'core'=2,'rep'=4] {'y','x','rep'}, dimensions={0} | all-to-all | bytes 6815744 | tf_op jit(solution)/shard_map/all_to_all | solution.py:422
  292.1 3.0 %total_grads.1 = (f32[1,16,1024]{2,1,0:T(8,128)}, f32[8,1024]{1,0:T(8,128)}, f32[8,153]{1,0:T(8,128)}) custom-call(bf16[64,16,1664]{2,1,0:T(8,128)(2,1)} %all_to_all.5.parts), custom_call_target="tpu_custom_call" | custom-call | tf_op jit(solution)/shard_map/total_grads/pallas_call | solution.py:347
  (137 shorter events, 48.7 us)
Async XLA Ops:
  5.3 6.7 %collective-permute-start = (bf16[128,128]{1,0:T(8,128)(2,1)}, bf16[128,128]{1,0:T(8,128)(2,1)S(1)}, u32[]{:S(2)}, u32[]{:S(2)}) collective-permute-start(bf16[128,128]{1,0:T(8,128)(2,1)} %get-tuple-element.34), channel_id=1, source_target_pairs={{0,32},{32,64},{64,96},{96,0},{1,33},{33,65},{65,97},{97,1},{2,34}... | collective-permute-start | bytes 98312 | tf_op jit(solution)/shard_map/ppermute | solution.py:359
  7.0 5.6 %collective-permute-start.1 = (bf16[128,128]{1,0:T(8,128)(2,1)}, bf16[128,128]{1,0:T(8,128)(2,1)S(1)}, u32[]{:S(2)}, u32[]{:S(2)}) collective-permute-start(bf16[128,128]{1,0:T(8,128)(2,1)} %get-tuple-element.34), channel_id=1, source_target_pairs={{0,64},{32,96},{64,0},{96,32},{1,65},{33,97},{65,1},{97,33},{2,66}... | collective-permute-start | bytes 98312 | tf_op jit(solution)/shard_map/ppermute | solution.py:359
  9.9 4.1 %collective-permute-start.2 = (bf16[128,128]{1,0:T(8,128)(2,1)}, bf16[128,128]{1,0:T(8,128)(2,1)S(1)}, u32[]{:S(2)}, u32[]{:S(2)}) collective-permute-start(bf16[128,128]{1,0:T(8,128)(2,1)} %get-tuple-element.34), channel_id=1, source_target_pairs={{0,96},{32,0},{64,32},{96,64},{1,97},{33,1},{65,33},{97,65},{2,98}... | collective-permute-start | bytes 98312 | tf_op jit(solution)/shard_map/ppermute | solution.py:359
  14.0 7.5 %collective-permute-start.3 = (bf16[512,128]{1,0:T(8,128)(2,1)S(1)}, bf16[512,128]{1,0:T(8,128)(2,1)S(1)}, u32[]{:S(2)}, u32[]{:S(2)}) collective-permute-start(bf16[512,128]{1,0:T(8,128)(2,1)S(1)} %get-tuple-element.79), channel_id=1, source_target_pairs={{0,8},{8,16},{16,24},{24,0},{1,9},{9,17},{17,25},{25,1},{2,10},{10... | collective-permute-start | bytes 393224 | tf_op jit(solution)/shard_map/ppermute | solution.py:359
  15.6 7.3 %collective-permute-start.4 = (bf16[512,128]{1,0:T(8,128)(2,1)S(1)}, bf16[512,128]{1,0:T(8,128)(2,1)S(1)}, u32[]{:S(2)}, u32[]{:S(2)}) collective-permute-start(bf16[512,128]{1,0:T(8,128)(2,1)S(1)} %get-tuple-element.79), channel_id=1, source_target_pairs={{0,16},{8,24},{16,0},{24,8},{1,17},{9,25},{17,1},{25,9},{2,18},{10... | collective-permute-start | bytes 393224 | tf_op jit(solution)/shard_map/ppermute | solution.py:359
  18.3 5.0 %collective-permute-start.5 = (bf16[512,128]{1,0:T(8,128)(2,1)S(1)}, bf16[512,128]{1,0:T(8,128)(2,1)S(1)}, u32[]{:S(2)}, u32[]{:S(2)}) collective-permute-start(bf16[512,128]{1,0:T(8,128)(2,1)S(1)} %get-tuple-element.79), channel_id=1, source_target_pairs={{0,24},{8,0},{16,8},{24,16},{1,25},{9,1},{17,9},{25,17},{2,26},{10... | collective-permute-start | bytes 393224 | tf_op jit(solution)/shard_map/ppermute | solution.py:359
  38.9 5.3 %collective-permute-start.7 = (bf16[128,128]{1,0:T(8,128)(2,1)}, bf16[128,128]{1,0:T(8,128)(2,1)S(1)}, u32[]{:S(2)}, u32[]{:S(2)}) collective-permute-start(bf16[128,128]{1,0:T(8,128)(2,1)} %get-tuple-element.37), channel_id=1, source_target_pairs={{0,32},{32,64},{64,96},{96,0},{1,33},{33,65},{65,97},{97,1},{2,34}... | collective-permute-start | bytes 98312 | tf_op jit(solution)/shard_map/ppermute | solution.py:359
  39.9 6.0 %collective-permute-start.8 = (bf16[128,128]{1,0:T(8,128)(2,1)}, bf16[128,128]{1,0:T(8,128)(2,1)S(1)}, u32[]{:S(2)}, u32[]{:S(2)}) collective-permute-start(bf16[128,128]{1,0:T(8,128)(2,1)} %get-tuple-element.37), channel_id=1, source_target_pairs={{0,64},{32,96},{64,0},{96,32},{1,65},{33,97},{65,1},{97,33},{2,66}... | collective-permute-start | bytes 98312 | tf_op jit(solution)/shard_map/ppermute | solution.py:359
  43.8 4.1 %collective-permute-start.9 = (bf16[128,128]{1,0:T(8,128)(2,1)}, bf16[128,128]{1,0:T(8,128)(2,1)S(1)}, u32[]{:S(2)}, u32[]{:S(2)}) collective-permute-start(bf16[128,128]{1,0:T(8,128)(2,1)} %get-tuple-element.37), channel_id=1, source_target_pairs={{0,96},{32,0},{64,32},{96,64},{1,97},{33,1},{65,33},{97,65},{2,98}... | collective-permute-start | bytes 98312 | tf_op jit(solution)/shard_map/ppermute | solution.py:359
  47.9 7.4 %collective-permute-start.10 = (bf16[512,128]{1,0:T(8,128)(2,1)S(1)}, bf16[512,128]{1,0:T(8,128)(2,1)S(1)}, u32[]{:S(2)}, u32[]{:S(2)}) collective-permute-start(bf16[512,128]{1,0:T(8,128)(2,1)S(1)} %get-tuple-element.71), channel_id=1, source_target_pairs={{0,8},{8,16},{16,24},{24,0},{1,9},{9,17},{17,25},{25,1},{2,10},{10... | collective-permute-start | bytes 393224 | tf_op jit(solution)/shard_map/ppermute | solution.py:359
  49.3 7.4 %collective-permute-start.11 = (bf16[512,128]{1,0:T(8,128)(2,1)S(1)}, bf16[512,128]{1,0:T(8,128)(2,1)S(1)}, u32[]{:S(2)}, u32[]{:S(2)}) collective-permute-start(bf16[512,128]{1,0:T(8,128)(2,1)S(1)} %get-tuple-element.71), channel_id=1, source_target_pairs={{0,16},{8,24},{16,0},{24,8},{1,17},{9,25},{17,1},{25,9},{2,18},{10... | collective-permute-start | bytes 393224 | tf_op jit(solution)/shard_map/ppermute | solution.py:359
  52.1 5.0 %collective-permute-start.12 = (bf16[512,128]{1,0:T(8,128)(2,1)S(1)}, bf16[512,128]{1,0:T(8,128)(2,1)S(1)}, u32[]{:S(2)}, u32[]{:S(2)}) collective-permute-start(bf16[512,128]{1,0:T(8,128)(2,1)S(1)} %get-tuple-element.71), channel_id=1, source_target_pairs={{0,24},{8,0},{16,8},{24,16},{1,25},{9,1},{17,9},{25,17},{2,26},{10... | collective-permute-start | bytes 393224 | tf_op jit(solution)/shard_map/ppermute | solution.py:359
  72.8 5.3 %collective-permute-start.14 = (bf16[128,128]{1,0:T(8,128)(2,1)}, bf16[128,128]{1,0:T(8,128)(2,1)S(1)}, u32[]{:S(2)}, u32[]{:S(2)}) collective-permute-start(bf16[128,128]{1,0:T(8,128)(2,1)} %get-tuple-element.40), channel_id=1, source_target_pairs={{0,32},{32,64},{64,96},{96,0},{1,33},{33,65},{65,97},{97,1},{2,34}... | collective-permute-start | bytes 98312 | tf_op jit(solution)/shard_map/ppermute | solution.py:359
  73.7 5.7 %collective-permute-start.15 = (bf16[128,128]{1,0:T(8,128)(2,1)}, bf16[128,128]{1,0:T(8,128)(2,1)S(1)}, u32[]{:S(2)}, u32[]{:S(2)}) collective-permute-start(bf16[128,128]{1,0:T(8,128)(2,1)} %get-tuple-element.40), channel_id=1, source_target_pairs={{0,64},{32,96},{64,0},{96,32},{1,65},{33,97},{65,1},{97,33},{2,66}... | collective-permute-start | bytes 98312 | tf_op jit(solution)/shard_map/ppermute | solution.py:359
  76.5 4.1 %collective-permute-start.16 = (bf16[128,128]{1,0:T(8,128)(2,1)}, bf16[128,128]{1,0:T(8,128)(2,1)S(1)}, u32[]{:S(2)}, u32[]{:S(2)}) collective-permute-start(bf16[128,128]{1,0:T(8,128)(2,1)} %get-tuple-element.40), channel_id=1, source_target_pairs={{0,96},{32,0},{64,32},{96,64},{1,97},{33,1},{65,33},{97,65},{2,98}... | collective-permute-start | bytes 98312 | tf_op jit(solution)/shard_map/ppermute | solution.py:359
  80.7 7.6 %collective-permute-start.17 = (bf16[512,128]{1,0:T(8,128)(2,1)S(1)}, bf16[512,128]{1,0:T(8,128)(2,1)S(1)}, u32[]{:S(2)}, u32[]{:S(2)}) collective-permute-start(bf16[512,128]{1,0:T(8,128)(2,1)S(1)} %get-tuple-element.63), channel_id=1, source_target_pairs={{0,8},{8,16},{16,24},{24,0},{1,9},{9,17},{17,25},{25,1},{2,10},{10... | collective-permute-start | bytes 393224 | tf_op jit(solution)/shard_map/ppermute | solution.py:359
  82.0 7.7 %collective-permute-start.18 = (bf16[512,128]{1,0:T(8,128)(2,1)S(1)}, bf16[512,128]{1,0:T(8,128)(2,1)S(1)}, u32[]{:S(2)}, u32[]{:S(2)}) collective-permute-start(bf16[512,128]{1,0:T(8,128)(2,1)S(1)} %get-tuple-element.63), channel_id=1, source_target_pairs={{0,16},{8,24},{16,0},{24,8},{1,17},{9,25},{17,1},{25,9},{2,18},{10... | collective-permute-start | bytes 393224 | tf_op jit(solution)/shard_map/ppermute | solution.py:359
  84.8 5.0 %collective-permute-start.19 = (bf16[512,128]{1,0:T(8,128)(2,1)S(1)}, bf16[512,128]{1,0:T(8,128)(2,1)S(1)}, u32[]{:S(2)}, u32[]{:S(2)}) collective-permute-start(bf16[512,128]{1,0:T(8,128)(2,1)S(1)} %get-tuple-element.63), channel_id=1, source_target_pairs={{0,24},{8,0},{16,8},{24,16},{1,25},{9,1},{17,9},{25,17},{2,26},{10... | collective-permute-start | bytes 393224 | tf_op jit(solution)/shard_map/ppermute | solution.py:359
  89.8 19.1 %collective-permute-start.20 = (bf16[2048,128]{1,0:T(8,128)(2,1)S(1)}, bf16[2048,128]{1,0:T(8,128)(2,1)S(1)}, u32[]{:S(2)}, u32[]{:S(2)}) collective-permute-start(bf16[2048,128]{1,0:T(8,128)(2,1)S(1)} %constant_dynamic-update-slice_fusion.26.near), channel_id=1, source_target_pairs={{0,4},{4,0},{1,5},{5,1},{2,6},{6,2},{3,7},{7,3},{8,12},{12,8},{9,1... | collective-permute-start | bytes 1572872 | tf_op jit(solution)/shard_map/ppermute | solution.py:359
  89.9 11.3 %collective-permute-start.21 = (bf16[1024,128]{1,0:T(8,128)(2,1)S(1)}, bf16[1024,128]{1,0:T(8,128)(2,1)S(1)}, u32[]{:S(2)}, u32[]{:S(2)}) collective-permute-start(bf16[1024,128]{1,0:T(8,128)(2,1)S(1)} %copy-done.14), channel_id=1, source_target_pairs={{0,1},{1,2},{2,3},{3,0},{4,5},{5,6},{6,7},{7,4},{8,9},{9,10},{10,1... | collective-permute-start | bytes 786440 | tf_op jit(solution)/shard_map/ppermute | solution.py:359
  91.8 16.7 %collective-permute-start.25 = (bf16[1024,128]{1,0:T(8,128)(2,1)S(1)}, bf16[1024,128]{1,0:T(8,128)(2,1)S(1)}, u32[]{:S(2)}, u32[]{:S(2)}) collective-permute-start(bf16[1024,128]{1,0:T(8,128)(2,1)S(1)} %copy-done.13), channel_id=1, source_target_pairs={{0,2},{1,3},{2,0},{3,1},{4,6},{5,7},{6,4},{7,5},{8,10},{9,11},{10,... | collective-permute-start | bytes 786440 | tf_op jit(solution)/shard_map/ppermute | solution.py:359
  95.4 70.1 %collective-permute-start.29 = (bf16[1024,128]{1,0:T(8,128)(2,1)S(1)}, bf16[1024,128]{1,0:T(8,128)(2,1)}, u32[]{:S(2)}, u32[]{:S(2)}) collective-permute-start(bf16[1024,128]{1,0:T(8,128)(2,1)S(1)} %copy-done.12), channel_id=1, source_target_pairs={{0,3},{1,0},{2,1},{3,2},{4,7},{5,4},{6,5},{7,6},{8,11},{9,8},{10,9... | collective-permute-start | bytes 786440 | tf_op jit(solution)/shard_map/ppermute | solution.py:359
  96.4 70.6 %collective-permute-start.22 = (bf16[1024,128]{1,0:T(8,128)(2,1)S(1)}, bf16[1024,128]{1,0:T(8,128)(2,1)}, u32[]{:S(2)}, u32[]{:S(2)}) collective-permute-start(bf16[1024,128]{1,0:T(8,128)(2,1)S(1)} %copy-done.17), channel_id=1, source_target_pairs={{0,1},{1,2},{2,3},{3,0},{4,5},{5,6},{6,7},{7,4},{8,9},{9,10},{10,1... | collective-permute-start | bytes 786440 | tf_op jit(solution)/shard_map/ppermute | solution.py:359
  101.1 67.8 %collective-permute-start.26 = (bf16[1024,128]{1,0:T(8,128)(2,1)S(1)}, bf16[1024,128]{1,0:T(8,128)(2,1)}, u32[]{:S(2)}, u32[]{:S(2)}) collective-permute-start(bf16[1024,128]{1,0:T(8,128)(2,1)S(1)} %copy-done.16), channel_id=1, source_target_pairs={{0,2},{1,3},{2,0},{3,1},{4,6},{5,7},{6,4},{7,5},{8,10},{9,11},{10,... | collective-permute-start | bytes 786440 | tf_op jit(solution)/shard_map/ppermute | solution.py:359
  108.6 60.6 %collective-permute-start.30 = (bf16[1024,128]{1,0:T(8,128)(2,1)S(1)}, bf16[1024,128]{1,0:T(8,128)(2,1)}, u32[]{:S(2)}, u32[]{:S(2)}) collective-permute-start(bf16[1024,128]{1,0:T(8,128)(2,1)S(1)} %copy-done.15), channel_id=1, source_target_pairs={{0,3},{1,0},{2,1},{3,2},{4,7},{5,4},{6,5},{7,6},{8,11},{9,8},{10,9... | collective-permute-start | bytes 786440 | tf_op jit(solution)/shard_map/ppermute | solution.py:359
  108.8 62.4 %collective-permute-start.23 = (bf16[1024,128]{1,0:T(8,128)(2,1)}, bf16[1024,128]{1,0:T(8,128)(2,1)}, u32[]{:S(2)}, u32[]{:S(2)}) collective-permute-start(bf16[1024,128]{1,0:T(8,128)(2,1)} %get-tuple-element.44), channel_id=1, source_target_pairs={{0,1},{1,2},{2,3},{3,0},{4,5},{5,6},{6,7},{7,4},{8,9},{9,10},{10,1... | collective-permute-start | bytes 786440 | tf_op jit(solution)/shard_map/ppermute | solution.py:359
  165.5 13.2 %collective-permute-start.27 = (bf16[1024,128]{1,0:T(8,128)(2,1)S(1)}, bf16[1024,128]{1,0:T(8,128)(2,1)S(1)}, u32[]{:S(2)}, u32[]{:S(2)}) collective-permute-start(bf16[1024,128]{1,0:T(8,128)(2,1)S(1)} %copy-done.19), channel_id=1, source_target_pairs={{0,2},{1,3},{2,0},{3,1},{4,6},{5,7},{6,4},{7,5},{8,10},{9,11},{10,... | collective-permute-start | bytes 786440 | tf_op jit(solution)/shard_map/ppermute | solution.py:359
  167.1 14.0 %collective-permute-start.31 = (bf16[1024,128]{1,0:T(8,128)(2,1)S(1)}, bf16[1024,128]{1,0:T(8,128)(2,1)S(1)}, u32[]{:S(2)}, u32[]{:S(2)}) collective-permute-start(bf16[1024,128]{1,0:T(8,128)(2,1)S(1)} %copy-done.18), channel_id=1, source_target_pairs={{0,3},{1,0},{2,1},{3,2},{4,7},{5,4},{6,5},{7,6},{8,11},{9,8},{10,9... | collective-permute-start | bytes 786440 | tf_op jit(solution)/shard_map/ppermute | solution.py:359
  168.9 12.9 %collective-permute-start.24 = (bf16[1024,128]{1,0:T(8,128)(2,1)}, bf16[1024,128]{1,0:T(8,128)(2,1)S(1)}, u32[]{:S(2)}, u32[]{:S(2)}) collective-permute-start(bf16[1024,128]{1,0:T(8,128)(2,1)} %get-tuple-element.45), channel_id=1, source_target_pairs={{0,1},{1,2},{2,3},{3,0},{4,5},{5,6},{6,7},{7,4},{8,9},{9,10},{10,1... | collective-permute-start | bytes 786440 | tf_op jit(solution)/shard_map/ppermute | solution.py:359
  169.1 17.8 %collective-permute-start.28 = (bf16[1024,128]{1,0:T(8,128)(2,1)}, bf16[1024,128]{1,0:T(8,128)(2,1)S(1)}, u32[]{:S(2)}, u32[]{:S(2)}) collective-permute-start(bf16[1024,128]{1,0:T(8,128)(2,1)} %get-tuple-element.49), channel_id=1, source_target_pairs={{0,2},{1,3},{2,0},{3,1},{4,6},{5,7},{6,4},{7,5},{8,10},{9,11},{10,... | collective-permute-start | bytes 786440 | tf_op jit(solution)/shard_map/ppermute | solution.py:359
  171.2 20.6 %collective-permute-start.32 = (bf16[1024,128]{1,0:T(8,128)(2,1)}, bf16[1024,128]{1,0:T(8,128)(2,1)S(1)}, u32[]{:S(2)}, u32[]{:S(2)}) collective-permute-start(bf16[1024,128]{1,0:T(8,128)(2,1)} %get-tuple-element.53), channel_id=1, source_target_pairs={{0,3},{1,0},{2,1},{3,2},{4,7},{5,4},{6,5},{7,6},{8,11},{9,8},{10,9... | collective-permute-start | bytes 786440 | tf_op jit(solution)/shard_map/ppermute | solution.py:359
  220.2 10.9 %collective-permute-start.33 = (bf16[4,4,4,16,1024]{4,3,2,1,0:T(8,128)(2,1)}, bf16[4,4,4,16,1024]{4,3,2,1,0:T(8,128)(2,1)S(1)}, u32[]{:S(2)}, u32[]{:S(2)}) collective-permute-start(bf16[4,4,4,16,1024]{4,3,2,1,0:T(8,128)(2,1)} %get-tuple-element.56), channel_id=1, source_target_pairs={{0,4},{4,0},{1,5},{5,1},{2,6},{6,2},{3,7},{7,3},{8,12},{12,8},{9,1... | collective-permute-start | bytes 6291464 | tf_op jit(solution)/shard_map/ppermute | solution.py:359
  (30 other events, 624.9 us)

commit v2 on v1

v2 whole, which is shorter than its diff:
```python
import functools
import math

import jax
import jax.numpy as jnp
from jax import lax
from jax.experimental import pallas as pl
from jax.experimental.pallas import tpu as pltpu
from jax.sharding import Mesh, PartitionSpec as P

HOPS = 3
TILE = 128
NB = 32
K = 8
R = 4096
HID = 1024
C = 153
CP = 256
Y, X, CORE, REP = 4, 4, 2, 4
DOM = Y * X * CORE
ROWS = R // REP
N_TRAIN = DOM * R
BF = jnp.bfloat16
F32 = jnp.float32
LAB = 16
MIB = 2**20

root_two_pi = 0.7978845608028654
cubic_term = 0.044715


def gelu_pair(v):
    sq = v * v
    t = jnp.tanh(root_two_pi * (v + cubic_term * sq * v))
    half = 0.5 * (1.0 + t)
    slope = half + (0.5 * root_two_pi) * v * (1.0 - t * t) * (
        1.0 + (3.0 * cubic_term) * sq
    )
    return v * half, slope


def dot(a, b, ca, cb):
    return lax.dot_general(a, b, (((ca,), (cb,)), ((), ())), preferred_element_type=F32)


def params(mib):
    return pltpu.CompilerParams(vmem_limit_bytes=mib * MIB)


def whole(memory_space=pltpu.VMEM):
    return pl.BlockSpec(memory_space=memory_space)


def struct(shape, dtype=BF):
    return jax.ShapeDtypeStruct(shape, dtype)


def export_rows(hop, brow):
    row = lax.broadcasted_iota(jnp.int32, (TILE, R), 1)
    return dot((row == brow[...]).astype(BF), hop[...], 1, 0).astype(BF)


def take_quarters(rep, hop, quarters):
    for d, q in enumerate(quarters):
        start = pl.multiple_of(lax.rem(rep + d, REP) * ROWS, ROWS)
        q[:ROWS] = hop[pl.ds(start, ROWS), :]


def export_kernel(pos, hop, brow, labels, export, *quarters):
    got = export_rows(hop, brow)
    extra = jnp.concatenate([labels[...].astype(F32), jnp.zeros((8, TILE), F32)])
    extra = extra.astype(BF)
    for t in range(Y * X):
        export[t, :TILE] = got
        export[t, TILE:] = extra
    take_quarters(pos[0], hop, quarters)


def export_first(pos, hop, brow, labels):
    return pl.pallas_call(
        export_kernel,
        in_specs=[whole(pltpu.SMEM)] + [whole()] * 3,
        out_specs=[whole()] * 5,
        out_shape=[struct((Y * X, TILE + LAB, TILE))] + [struct((ROWS, TILE))] * 4,
        compiler_params=params(16),
        name="export_first",
        cost_estimate=pl.CostEstimate(
            flops=2 * TILE * TILE * R, bytes_accessed=2 * MIB, transcendentals=0
        ),
    )(pos, hop, brow, labels)


CUTS = 8
STEP = NB // CUTS


def prop_kernel(h, cols, tiles, hop, near, far, brow, *rest):
    last = h == HOPS - 1
    if last:
        q0, q1, q2, q3, joined, held, sem, out = rest
    else:
        out, export, q0, q1, q2, q3, joined, held, sem = rest
    r, core, inner = cols[NB * K], cols[NB * K + 1], cols[NB * K + 2]
    copies = [
        pltpu.make_async_copy(
            tiles.at[pl.ds(c * STEP, STEP)], held.at[pl.ds(c * STEP, STEP)], sem.at[c]
        )
        for c in range(CUTS)
    ]
    for copy in copies:
        copy.start()
    joined[:R] = hop[...]
    for t in range(Y * X):
        at = R + t * TILE
        joined[at : at + TILE] = near[t, :TILE]
        joined[at + R // 2 : at + R // 2 + TILE] = far[t, :TILE]
    for c in range(CUTS):
        copies[c].wait()

        @pl.loop(c * STEP, (c + 1) * STEP)
        def _(b):
            parts = []
            for k in range(K):
                at = pl.multiple_of(cols[b * K + k] * TILE, TILE)
                parts.append(joined[pl.ds(at, TILE), :])
            left = jnp.concatenate([held[b, k] for k in range(K)], axis=1)
            got = dot(left, jnp.concatenate(parts, axis=0), 1, 0).astype(BF)
            out[pl.ds(pl.multiple_of(b * TILE, TILE), TILE), :] = got

    if not last:
        got = export_rows(out, brow)
        for t in range(Y * X):
            export[t] = got
    quarters = (q0, q1, q2, q3)
    take_quarters(r, out, quarters)
    if h == 0:
        pick = lax.broadcasted_iota(jnp.int32, (LAB, TILE), 0) == inner
        labs = []
        for t in range(Y * X):
            two = [
                jnp.sum(jnp.where(pick, v[t, TILE:].astype(F32), 0.0), axis=0, keepdims=True)
                for v in (near, far)
            ]
            labs.append(jnp.where(core == 0, two[0], two[1]))
            labs.append(jnp.where(core == 0, two[1], two[0]))
        labs = jnp.concatenate(labs, axis=0).astype(BF)
        for q in quarters:
            q[ROWS:] = labs


def propagate(h, cols, tiles, hop, near, far, brow):
    last = h == HOPS - 1
    outs = [] if last else [(R, TILE), (Y * X, TILE, TILE)]
    outs += [(ROWS + DOM if h == 0 else ROWS, TILE)] * 4
    scratch = [
        pltpu.VMEM((2 * R, TILE), BF),
        pltpu.VMEM((NB, K, TILE, TILE), BF),
        pltpu.SemaphoreType.DMA((CUTS,)),
    ]
    scratch += [pltpu.VMEM((R, TILE), BF)] if last else []
    return pl.pallas_call(
        functools.partial(prop_kernel, h),
        in_specs=[whole(pltpu.SMEM), whole(pltpu.HBM)] + [whole()] * 4,
        out_specs=[whole()] * len(outs),
        scratch_shapes=scratch,
        out_shape=[struct(s) for s in outs],
        compiler_params=params(54),
        name="propagate_" + str(h),
        cost_estimate=pl.CostEstimate(
            flops=2 * NB * K * TILE**3, bytes_accessed=12 * MIB, transcendentals=0
        ),
    )(cols, tiles, hop, near, far, brow)


def count_kernel(pos, lab0, lab1, lab2, lab3, shuffle, train, out):
    labels = jnp.zeros((DOM, TILE), F32)
    for d, v in enumerate((lab0, lab1, lab2, lab3)):
        labels = jnp.where(pos[2] == d, v[...].astype(F32), labels)
    first = lax.broadcasted_iota(jnp.int32, (DOM, TILE), 0)
    second = lax.broadcasted_iota(jnp.int32, (TILE, TILE), 0)
    slots = jnp.zeros((DOM, TILE), F32)
    for lo in range(0, DOM, 8):
        a, b = [], []
        for e in range(lo, lo + 8):
            slot = shuffle[e : e + 1, :]
            label = labels[e : e + 1, :]
            a.append(jnp.where(first == slot // TILE, label, 0.0).astype(BF))
            b.append((second == lax.rem(slot, TILE)).astype(BF))
        slots += dot(jnp.concatenate(a, axis=1), jnp.concatenate(b, axis=1), 1, 1)
    slots = slots.astype(jnp.int32)
    paper = lax.broadcasted_iota(jnp.int32, (ROWS, TILE), 0) + pos[0] * ROWS
    kind = lax.broadcasted_iota(jnp.int32, (CP, TILE), 0)
    total = jnp.zeros((ROWS, CP), F32)
    for lo in range(0, DOM, 8):
        a, b = [], []
        for e in range(lo, lo + 8):
            a.append((paper == train[e : e + 1, :]).astype(BF))
            b.append((kind == slots[e : e + 1, :]).astype(BF))
        total += dot(jnp.concatenate(a, axis=1), jnp.concatenate(b, axis=1), 1, 1)
    out[...] = total


def count_labels(pos, both, shuffle, train):
    def fixed(shape):
        return pl.BlockSpec(shape, lambda i, c: (0, 0))

    tail = pl.BlockSpec((DOM, TILE), lambda i, c: (ROWS // DOM, 0))
    return pl.pallas_call(
        count_kernel,
        grid_spec=pltpu.PrefetchScalarGridSpec(
            num_scalar_prefetch=1,
            grid=(1,),
            in_specs=[tail] * 4 + [fixed((DOM, TILE))] * 2,
            out_specs=fixed((ROWS, CP)),
        ),
        out_shape=struct((ROWS, CP), F32),
        compiler_params=params(24),
        name="count_labels",
        cost_estimate=pl.CostEstimate(
            flops=2 * ROWS * R * CP, bytes_accessed=2 * MIB, transcendentals=0
        ),
    )(pos, *both, shuffle, train)


MLP_ROWS = 256


def slab_of(rep, d):
    return lax.rem(rep + REP - d, REP)


def early_kernel(pos, *refs):
    pieces, (w1, out) = refs[:12], refs[12:]
    total = jnp.zeros((MLP_ROWS, HID), F32)
    for d in range(REP):
        x = jnp.concatenate([pieces[3 * d + h][...] for h in range(HOPS)], axis=1)
        total += dot(x, w1[slab_of(pos[0], d), : HOPS * TILE], 1, 0)
    out[...] = total


def mlp_kernel(pos, *refs):
    pieces, (early, counts, w1, w2, w3, act1, act2, gl, gm, gf) = refs[:4], refs[4:]
    pre1 = early[...]
    for d in range(REP):
        pre1 += dot(pieces[d][...], w1[slab_of(pos[0], d), HOPS * TILE :], 1, 0)
    a1, slope1 = gelu_pair(pre1)
    a1 = a1.astype(BF)
    act1[...] = a1
    a2, slope2 = gelu_pair(dot(a1, w2[...], 1, 0))
    a2 = a2.astype(BF)
    act2[...] = a2
    logits = dot(a2, w3[...], 1, 0)
    kind = lax.broadcasted_iota(jnp.int32, (MLP_ROWS, CP), 1)
    ex = jnp.where(kind < C, jnp.exp(logits), 0.0)
    probs = ex / jnp.sum(ex, axis=1, keepdims=True)
    drawn = counts[...]
    many = jnp.sum(drawn, axis=1, keepdims=True)
    g3 = ((probs * many - drawn) * (1.0 / math.sqrt(N_TRAIN))).astype(BF)
    gl[...] = g3
    g2 = (dot(g3, w3[...], 1, 1) * slope2).astype(BF)
    gm[...] = g2
    gf[...] = (dot(g2, w2[...], 1, 1) * slope1).astype(BF)


def fixed_block(shape):
    return pl.BlockSpec(shape, lambda i, c: (0,) * len(shape))


def row_block(width):
    return pl.BlockSpec((MLP_ROWS, width), lambda i, c: (i, 0))


def first_layer_early(pos, pieces, w1):
    return pl.pallas_call(
        early_kernel,
        grid_spec=pltpu.PrefetchScalarGridSpec(
            num_scalar_prefetch=1,
            grid=(ROWS // MLP_ROWS,),
            in_specs=[row_block(TILE)] * 12 + [fixed_block(w1.shape)],
            out_specs=row_block(HID),
        ),
        out_shape=struct((ROWS, HID), F32),
        compiler_params=params(20),
        name="first_layer_early",
        cost_estimate=pl.CostEstimate(
            flops=2 * ROWS * HID * 3 * 512, bytes_accessed=11 * MIB, transcendentals=0
        ),
    )(pos, *pieces, w1)


def mlp(pos, pieces, early, counts, w1, w2, w3):
    widths = (HID, HID, CP, HID, HID)
    return pl.pallas_call(
        mlp_kernel,
        grid_spec=pltpu.PrefetchScalarGridSpec(
            num_scalar_prefetch=1,
            grid=(ROWS // MLP_ROWS,),
            in_specs=[row_block(TILE)] * 4
            + [row_block(HID), row_block(CP)]
            + [fixed_block(w.shape) for w in (w1, w2, w3)],
            out_specs=[row_block(w) for w in widths],
        ),
        out_shape=[struct((ROWS, w)) for w in widths],
        compiler_params=params(36),
        name="mlp",
        cost_estimate=pl.CostEstimate(
            flops=2 * ROWS * HID * (2 * HID + 512 + 2 * CP),
            bytes_accessed=20 * MIB,
            transcendentals=2 * ROWS * HID,
        ),
    )(pos, *pieces, early, counts, w1, w2, w3)


WIDE = (HID + CP) // 2


def outer_kernel(pos, act1, act2, gl, gm, keep, send):
    own = pos[1] == 0
    width = HID // Y
    for y in range(Y):
        cut = slice(y * width, (y + 1) * width)
        mid = dot(act1[:, cut], gm[...], 0, 0)
        out = dot(act2[:, cut], gl[...], 0, 0)
        both = jnp.concatenate([mid, out], axis=1).reshape(X, CORE, REP, 8, HID + CP)
        both = jnp.concatenate([both[..., :WIDE], both[..., WIDE:]], axis=3)
        zero, one = both[:, 0], both[:, 1]
        keep[y] = jnp.where(own, zero, one).astype(BF)
        send[y] = jnp.where(own, one, zero).astype(BF)


def outer_grads(pos, act1, act2, gl, gm):
    shape = (Y, X, REP, 16, WIDE)
    return pl.pallas_call(
        outer_kernel,
        in_specs=[whole(pltpu.SMEM)] + [whole()] * 4,
        out_specs=[whole()] * 2,
        out_shape=[struct(shape)] * 2,
        compiler_params=params(30),
        name="outer_grads",
        cost_estimate=pl.CostEstimate(
            flops=2 * ROWS * HID * (HID + CP), bytes_accessed=8 * MIB, transcendentals=0
        ),
    )(pos, act1, act2, gl, gm)


def first_kernel(pos, *refs):
    pieces, (gf, keep, send) = refs[:16], refs[16:]
    own = pos[1] == 0
    for d in range(REP):
        slab = lax.rem(pos[0] + REP - d, REP)
        for y in range(0, Y, 2):
            two = [pieces[4 * u + d][:ROWS] for u in (y, y + 1)]
            x = jnp.concatenate(two, axis=1)
            got = dot(x, gf[...], 0, 0).reshape(2, X, CORE, 16, HID)
            zero, one = got[:, :, 0], got[:, :, 1]
            kept = jnp.where(own, zero, one).astype(BF)
            sent = jnp.where(own, one, zero).astype(BF)
            for u in range(2):
                for v in range(X):
                    keep[y + u, v, slab] = kept[u, v]
                    send[y + u, v, slab] = sent[u, v]


def first_grads(pos, pieces, gf):
    shape = (Y, X, REP, 16, HID)
    return pl.pallas_call(
        first_kernel,
        in_specs=[whole(pltpu.SMEM)] + [whole()] * 17,
        out_specs=[whole()] * 2,
        out_shape=[struct(shape)] * 2,
        compiler_params=params(36),
        name="first_grads",
        cost_estimate=pl.CostEstimate(
            flops=4 * ROWS * HID * HID, bytes_accessed=10 * MIB, transcendentals=0
        ),
    )(pos, *pieces, gf)


def join_kernel(keep_f, got_f, keep_m, got_m, out):
    out[:, :, :HID] = (keep_f[...].astype(F32) + got_f[...].astype(F32)).astype(BF)
    out[:, :, HID:] = (keep_m[...].astype(F32) + got_m[...].astype(F32)).astype(BF)


def join_cores(keep_f, got_f, keep_m, got_m):
    n = Y * X * REP
    flat = [v.reshape(n, 16, v.shape[-1]) for v in (keep_f, got_f, keep_m, got_m)]

    def spec(width):
        return pl.BlockSpec((8, 16, width), lambda i: (i, 0, 0))

    return pl.pallas_call(
        join_kernel,
        grid=(n // 8,),
        in_specs=[spec(v.shape[-1]) for v in flat],
        out_specs=spec(HID + WIDE),
        out_shape=struct((n, 16, HID + WIDE)),
        compiler_params=params(8),
        name="join_cores",
    )(*flat)


def total_kernel(parts, first, mid, out):
    total = jnp.sum(parts[...].astype(F32), axis=0)
    first[0] = total[:, :HID]
    rest = jnp.concatenate([total[:8, HID:], total[8:, HID:]], axis=1)
    mid[...] = rest[:, :HID]
    out[...] = rest[:, HID : HID + C]


def total_grads(parts):
    return pl.pallas_call(
        total_kernel,
        in_specs=[whole()],
        out_specs=[whole()] * 3,
        out_shape=[struct((1, 16, HID), F32), struct((8, HID), F32), struct((8, C), F32)],
        compiler_params=params(16),
        name="total_grads",
    )(parts)


def shift(value, axis, by):
    size = lax.axis_size(axis)
    return lax.ppermute(value, axis, [(i, (i + by) % size) for i in range(size)])


def spread(export):
    return lax.all_to_all(export, ("y", "x"), split_axis=0, concat_axis=0, tiled=True)


def exchange(quarters):
    return [quarters[0]] + [shift(quarters[d], "rep", d) for d in (1, 2, 3)]


def per_device(
    features,
    tile_values,
    tile_columns,
    boundary_rows,
    train_rows,
    shuffle,
    labels,
    first_weight,
    mid_weight,
    out_weight,
):
    y, x, core, rep = (lax.axis_index(a) for a in ("y", "x", "core", "rep"))
    pos = jnp.stack([rep, core, lax.rem(rep + REP - y, REP)]).astype(jnp.int32)

    part = tile_columns - NB
    halo_at = NB + (part + core) % CORE * (NB // CORE) + part // CORE
    cols = jnp.where(tile_columns < NB, tile_columns, halo_at).reshape(-1)
    inner = lax.rem((y * X + x) * CORE + core, DOM // REP)
    cols = jnp.concatenate([cols, jnp.stack([rep, core, inner])]).astype(jnp.int32)
    brow = boundary_rows.reshape(TILE, 1)

    export, *quarters = export_first(pos, features, brow, labels.reshape(8, TILE))
    hop, pieces, counts = features, [], None
    for h in range(HOPS):
        got = exchange(quarters)
        if h == HOPS - 1:
            counts = count_labels(
                pos, pieces[1], shuffle.reshape(DOM, TILE), train_rows.reshape(DOM, TILE)
            )
        near, got, counts = lax.optimization_barrier((spread(export), got, counts))
        far = shift(near, "core", 1)
        pieces.append(got)
        made = propagate(h, cols, tile_values, hop, near, far, brow)
        hop, export, quarters = made[0], made[1], made[-4:]
    early = first_layer_early(
        pos, [pieces[h][d] for d in range(REP) for h in range(HOPS)], first_weight
    )
    pieces.append(exchange(quarters))

    w3 = jnp.pad(out_weight, ((0, 0), (0, CP - C)))
    act1, act2, gl, gm, gf = mlp(
        pos, pieces[3], early, counts, first_weight, mid_weight, w3
    )
    pieces = [v for got in pieces for v in got]
    keep_f, send_f = first_grads(pos, pieces, gf)
    got_f = shift(send_f, "core", 1)
    keep_m, send_m = outer_grads(pos, act1, act2, gl, gm)
    got_m = shift(send_m, "core", 1)
    parts = join_cores(keep_f, got_f, keep_m, got_m)
    parts = lax.all_to_all(parts, ("y", "x", "rep"), split_axis=0, concat_axis=0, tiled=True)
    first, mid, out = total_grads(parts)
    return first, mid, out


def solution(mesh):
    fine = Mesh(mesh.devices.reshape(Y, X, CORE, REP), ("y", "x", "core", "rep"))
    dom = ("y", "x", "core")
    every = dom + ("rep",)
    placed = (
        P(dom, "rep"),
        P(dom, None, None, None),
        P(dom, None),
        P(dom, None),
        P(dom, None),
        P(dom, None),
        P(every),
        P(),
        P(),
        P(),
    )
    return jax.shard_map(
        per_device,
        mesh=fine,
        in_specs=placed,
        out_specs=(P("rep", dom, None), P(every, None), P(every, None)),
        check_vma=False,
    )
```

time: 296 us -> 219 us (0.74)
  blocking collectives: 95.6 us -> 54 us
  Pallas kernels: 88.7 us -> 71.2 us
  starting transfers between devices: 55.2 us -> 42.8 us
  waiting for transfers between devices: 43.2 us -> 39.9 us
    all_gather x2 -> x0, blocking collectives: 43.4 us -> none  [the longest x1 24.4 us: per_device(): lax.all_gather(all_labels, ('y', 'x', 'core'), axis=0, tiled=True)]
    ppermute x35 -> x17, starting transfers between devices: 55.2 us -> 21.9 us  [shift(): lax.ppermute(value, axis, [(i, (i + by) % size) for i in range(size)])]
    all_to_all x0 -> x3, starting transfers between devices: none -> 20.9 us  [spread(): lax.all_to_all(export, ('y', 'x'), split_axis=0, concat_axis=0, tiled=True)]
    pallas_call x1, Pallas kernels: 7.08 us -> 0.89 us  [join_cores(): pl.pallas_call(join_kernel, grid=(n // 8,), in_specs=[spec(v.shape[-1]) f...]
    pallas_call x1, Pallas kernels: 9.48 us -> 5.15 us  [first_grads(): pl.pallas_call(first_kernel, in_specs=[whole(pltpu.SMEM)] + [whole()] * 1...]
    pallas_call x1, Pallas kernels: 18.2 us -> 14 us  [mlp(): pl.pallas_call(mlp_kernel, grid_spec=pltpu.PrefetchScalarGridSpec(num_sca...]
    pallas_call x1, Pallas kernels: 7.47 us -> 3.59 us  [outer_grads(): pl.pallas_call(outer_kernel, in_specs=[whole(pltpu.SMEM)] + [whole()] * 4...]
    ppermute x35 -> x17, waiting for transfers between devices: 43.2 us -> 39.9 us  [shift(): lax.ppermute(value, axis, [(i, (i + by) % size) for i in range(size)])]
  transfers between devices with their start and end apart: 35 -> 20, of which waited for: 24 -> 11; matrix products, arithmetic and copies ran while one was open for 2% -> 2% of each run, Pallas kernels for 8% -> 6%
where the time goes in v2:
time: 219 us; the launch traced here: 218 us
  Pallas kernels  71.2 us (33%)
  blocking collectives  54 us (25%)
  starting transfers between devices  42.8 us (20%)
  waiting for transfers between devices  39.9 us (18%)
  local copies, waits for them, and re-layouts  8.58 us (4%)
    all_to_all x1, blocking collectives, per_device(): lax.all_to_all(parts, ('y', 'x', 'rep'), split_axis=0, concat_axis=0, til...  54 us
    ppermute x17, waiting for transfers between devices, shift(): lax.ppermute(value, axis, [(i, (i + by) % size) for i in range(size)])  39.9 us
    pallas_call x3, Pallas kernels, propagate(): pl.pallas_call(functools.partial(prop_kernel, h), in_specs=[whole(pltpu.S...  35.2 us
    ppermute x17, starting transfers between devices, shift(): lax.ppermute(value, axis, [(i, (i + by) % size) for i in range(size)])  21.9 us
    all_to_all x3, starting transfers between devices, spread(): lax.all_to_all(export, ('y', 'x'), split_axis=0, concat_axis=0, tiled=True)  20.9 us
    pallas_call x1, Pallas kernels, mlp(): pl.pallas_call(mlp_kernel, grid_spec=pltpu.PrefetchScalarGridSpec(num_sca...  14 us
    unnamed x35, local copies, waits for them, and re-layouts  6.53 us
    pallas_call x1, Pallas kernels, first_layer_early(): pl.pallas_call(early_kernel, grid_spec=pltpu.PrefetchScalarGridSpec(num_s...  5.61 us
  transfers between devices with their start and end apart: 20, of which 11 were waited for; matrix products, arithmetic and copies ran while one was open for 2% of the time, Pallas kernels for 6%

profile of v2, /device:TPU:0, one launch (start us, length us, event | category | flops | bytes accessed | tf_op | source)
XLA Modules:
  0.0 218.1 jit_solution(13508603624948819465)
XLA Ops:
  1.5 1.2 copy-done
  3.4 1.9 export_first.1
  5.3 7.1 %all-to-all-start = ((bf16[16,144,128]{2,1,0:T(8,128)(2,1)}), bf16[16,144,128]{2,1,0:T(8,128)(2,1)S(1)}, u32[]{:S(2)}, u32[]{:S(2)}) async-start(bf16[16,144,128]{2,1,0:T(8,128)(2,1)} %get-tuple-element.49), calls=%async_computation | async-start | bytes 1179648 | tf_op jit(solution)/shard_map/all_to_all | solution.py:427
  12.4 2.0 collective-permute-start
  14.4 3.6 %collective-permute-start.1 = (bf16[1024,128]{1,0:T(8,128)(2,1)S(1)}, bf16[1024,128]{1,0:T(8,128)(2,1)S(1)}, u32[]{:S(2)}, u32[]{:S(2)}) collective-permute-start(bf16[1024,128]{1,0:T(8,128)(2,1)S(1)} %get-tuple-element.52), channel_id=1, source_target_pairs={{0,2},{1,3},{2,0},{3,1},{4,6},{5,7},{6,4},{7,5},{8,10},{9,11},{10,... | collective-permute-start | bytes 786440 | tf_op jit(solution)/shard_map/ppermute | solution.py:423
  19.0 3.8 %collective-permute-done.refs_3_.refs_1_ = bf16[1024,128]{1,0:T(8,128)(2,1)S(1)} collective-permute-done((bf16[1024,128]{1,0:T(8,128)(2,1)S(1)}, bf16[1024,128]{1,0:T(8,128)(2,1)S(1)}, u32[]{:S(2)}, u32[]{:S(2)}) %collective-permute-start) | collective-permute-done | bytes 262176 | tf_op jit(solution)/shard_map/ppermute | solution.py:423
  22.8 6.5 %collective-permute-done.1.refs_6_.refs_2_ = bf16[1024,128]{1,0:T(8,128)(2,1)S(1)} collective-permute-done((bf16[1024,128]{1,0:T(8,128)(2,1)S(1)}, bf16[1024,128]{1,0:T(8,128)(2,1)S(1)}, u32[]{:S(2)}, u32[]{:S(2)}) %collective-permute-start.1) | collective-permute-done | bytes 262176 | tf_op jit(solution)/shard_map/ppermute | solution.py:423
  32.2 11.8 %propagate_0.1 = (bf16[4096,128]{1,0:T(8,128)(2,1)}, bf16[16,128,128]{2,1,0:T(8,128)(2,1)}, bf16[1056,128]{1,0:T(8,128)(2,1)}, bf16[1056,128]{1,0:T(8,128)(2,1)}...) custom-call(s32[259]{0:T(512)} %pad_add_fusion.cols, bf16[32,8,128,128]{3,2,1,0:T(8,128)(2,1)} %tiles.5, ...), custom_call_target="tpu_custom_call" | custom-call | flops 1073741824 | bytes 12582912 | tf_op jit(solution)/shard_map/propagate_0/pallas_call | solution.py:161
  44.1 6.9 %all-to-all-start.1 = ((bf16[16,128,128]{2,1,0:T(8,128)(2,1)}), bf16[16,128,128]{2,1,0:T(8,128)(2,1)S(1)}, u32[]{:S(2)}, u32[]{:S(2)}) async-start(bf16[16,128,128]{2,1,0:T(8,128)(2,1)} %get-tuple-element.59), calls=%async_computation.1 | async-start | bytes 1048576 | tf_op jit(solution)/shard_map/all_to_all | solution.py:427
  51.0 1.2 collective-permute-start.4
  52.2 2.4 %collective-permute-start.5 = (bf16[1056,128]{1,0:T(8,128)(2,1)}, bf16[1056,128]{1,0:T(8,128)(2,1)S(1)}, u32[]{:S(2)}, u32[]{:S(2)}) collective-permute-start(bf16[1056,128]{1,0:T(8,128)(2,1)} %get-tuple-element.62), channel_id=1, source_target_pairs={{0,2},{1,3},{2,0},{3,1},{4,6},{5,7},{6,4},{7,5},{8,10},{9,11},{10,... | collective-permute-start | bytes 811016 | tf_op jit(solution)/shard_map/ppermute | solution.py:423
  54.6 1.2 collective-permute-start.6
  55.8 5.7 %collective-permute-done.4.lab1.refs_4_.refs_5_ = bf16[1056,128]{1,0:T(8,128)(2,1)S(1)} collective-permute-done((bf16[1056,128]{1,0:T(8,128)(2,1)}, bf16[1056,128]{1,0:T(8,128)(2,1)S(1)}, u32[]{:S(2)}, u32[]{:S(2)}) %collective-permute-start.4) | collective-permute-done | bytes 270368 | tf_op jit(solution)/shard_map/ppermute | solution.py:423
  61.5 5.3 %collective-permute-done.5.lab2.refs_7_.refs_6_ = bf16[1056,128]{1,0:T(8,128)(2,1)S(1)} collective-permute-done((bf16[1056,128]{1,0:T(8,128)(2,1)}, bf16[1056,128]{1,0:T(8,128)(2,1)S(1)}, u32[]{:S(2)}, u32[]{:S(2)}) %collective-permute-start.5) | collective-permute-done | bytes 270368 | tf_op jit(solution)/shard_map/ppermute | solution.py:423
  67.1 1.9 collective-permute-done.7.far
  69.8 11.8 %propagate_1.1 = (bf16[4096,128]{1,0:T(8,128)(2,1)}, bf16[16,128,128]{2,1,0:T(8,128)(2,1)}, bf16[1024,128]{1,0:T(8,128)(2,1)}, bf16[1024,128]{1,0:T(8,128)(2,1)}...) custom-call(s32[259]{0:T(512)} %pad_add_fusion.cols, bf16[32,8,128,128]{3,2,1,0:T(8,128)(2,1)} %tiles.5, ...), custom_call_target="tpu_custom_call" | custom-call | flops 1073741824 | bytes 12582912 | tf_op jit(solution)/shard_map/propagate_1/pallas_call | solution.py:161
  81.6 6.9 %all-to-all-start.2 = ((bf16[16,128,128]{2,1,0:T(8,128)(2,1)}), bf16[16,128,128]{2,1,0:T(8,128)(2,1)}, u32[]{:S(2)}, u32[]{:S(2)}) async-start(bf16[16,128,128]{2,1,0:T(8,128)(2,1)} %get-tuple-element.70), calls=%async_computation.2 | async-start | bytes 1048576 | tf_op jit(solution)/shard_map/all_to_all | solution.py:427
  88.5 1.6 collective-permute-start.8
  90.1 2.6 %collective-permute-start.9 = (bf16[1024,128]{1,0:T(8,128)(2,1)}, bf16[1024,128]{1,0:T(8,128)(2,1)S(1)}, u32[]{:S(2)}, u32[]{:S(2)}) collective-permute-start(bf16[1024,128]{1,0:T(8,128)(2,1)} %get-tuple-element.73), channel_id=1, source_target_pairs={{0,2},{1,3},{2,0},{3,1},{4,6},{5,7},{6,4},{7,5},{8,10},{9,11},{10,... | collective-permute-start | bytes 786440 | tf_op jit(solution)/shard_map/ppermute | solution.py:423
  93.4 3.8 %count_labels.1.refs_5_ = f32[1024,256]{1,0:T(8,128)S(1)} custom-call(s32[3]{0:T(128)S(1)} %pad_add_fusion.1.pos, bf16[1056,128]{1,0:T(8,128)(2,1)S(1)} %copy-done.5, bf16[1056,128]{1,0:T(8,128)(2,1)S(1)} %collective-permute-done.4.lab1.refs_4_.refs_5_, bf16[1056,128]{1,0:T(8,128)(2,1)S(1)} %collective-permute-done.5.lab2.refs_7_.refs_6_, ...), custom_call_target="tpu_custom_call" | custom-call | flops 2147483648 | bytes 2097152 | tf_op jit(solution)/shard_map/count_labels/pallas_call | solution.py:208
  98.4 6.2 %collective-permute-done.9.refs_8_.refs_10_ = bf16[1024,128]{1,0:T(8,128)(2,1)S(1)} collective-permute-done((bf16[1024,128]{1,0:T(8,128)(2,1)}, bf16[1024,128]{1,0:T(8,128)(2,1)S(1)}, u32[]{:S(2)}, u32[]{:S(2)}) %collective-permute-start.9) | collective-permute-done | bytes 262176 | tf_op jit(solution)/shard_map/ppermute | solution.py:423
  104.6 2.0 copy.23
  107.7 11.6 %propagate_2.1 = (bf16[1024,128]{1,0:T(8,128)(2,1)}, bf16[1024,128]{1,0:T(8,128)(2,1)}, bf16[1024,128]{1,0:T(8,128)(2,1)}, bf16[1024,128]{1,0:T(8,128)(2,1)}) custom-call(s32[259]{0:T(512)} %pad_add_fusion.cols, bf16[32,8,128,128]{3,2,1,0:T(8,128)(2,1)} %tiles.5, bf16[4096,128]{1,0:T(8,128)(2,1)} %get-tuple-element.79.hop, ...), custom_call_target="tpu_custom_call" | custom-call | flops 1073741824 | bytes 12582912 | tf_op jit(solution)/shard_map/propagate_2/pallas_call | solution.py:161
  119.3 1.3 collective-permute-start.12
  120.7 2.6 %collective-permute-start.13 = (bf16[1024,128]{1,0:T(8,128)(2,1)}, bf16[1024,128]{1,0:T(8,128)(2,1)S(1)}, u32[]{:S(2)}, u32[]{:S(2)}) collective-permute-start(bf16[1024,128]{1,0:T(8,128)(2,1)} %get-tuple-element.83), channel_id=1, source_target_pairs={{0,2},{1,3},{2,0},{3,1},{4,6},{5,7},{6,4},{7,5},{8,10},{9,11},{10,... | collective-permute-start | bytes 786440 | tf_op jit(solution)/shard_map/ppermute | solution.py:423
  123.9 5.6 %first_layer_early.1.refs_4_ = f32[1024,1024]{1,0:T(8,128)S(1)} custom-call(s32[3]{0:T(128)S(1)} %pad_add_fusion.1.pos, bf16[1024,128]{1,0:T(8,128)(2,1)S(1)} %get-tuple-element.54.refs_0_, bf16[1056,128]{1,0:T(8,128)(2,1)S(1)} %copy-done.5, bf16[1024,128]{1,0:T(8,128)(2,1)S(1)} %copy-done.6, bf16[1024,128]{1,0:T(8,128)(2,1)S(1)} %collective-permute-done.refs_3_.refs_1_, ...), custom_call_target="tpu_custom_call" | custom-call | flops 3221225472 | bytes 11534336 | tf_op jit(solution)/shard_map/first_layer_early/pallas_call | solution.py:274
  129.6 6.2 %collective-permute-done.13.refs_2_.refs_14_ = bf16[1024,128]{1,0:T(8,128)(2,1)S(1)} collective-permute-done((bf16[1024,128]{1,0:T(8,128)(2,1)}, bf16[1024,128]{1,0:T(8,128)(2,1)S(1)}, u32[]{:S(2)}, u32[]{:S(2)}) %collective-permute-start.13) | collective-permute-done | bytes 262176 | tf_op jit(solution)/shard_map/ppermute | solution.py:423
  135.8 14.0 %mlp.1 = (bf16[1024,1024]{1,0:T(8,128)(2,1)S(1)}, bf16[1024,1024]{1,0:T(8,128)(2,1)S(1)}, bf16[1024,256]{1,0:T(8,128)(2,1)S(1)}, bf16[1024,1024]{1,0:T(8,128)(2,1)S(1)}, bf16[1024,1024]{1,0:T(8,128)(2,1)S(1)}) custom-call(s32[3]{0:T(128)S(1)} %pad_add_fusion.1.pos, bf16[1024,128]{1,0:T(8,128)(2,1)S(1)} %copy-done.7, ...), custom_call_target="tpu_custom_call" | custom-call | flops 6442450944 | bytes 20971520 | tf_op jit(solution)/shard_map/mlp/pallas_call | solution.py:293
  149.8 5.2 %first_grads.1 = (bf16[4,4,4,16,1024]{4,3,2,1,0:T(8,128)(2,1)S(1)}, bf16[4,4,4,16,1024]{4,3,2,1,0:T(8,128)(2,1)S(1)}) custom-call(s32[3]{0:T(128)S(1)} %pad_add_fusion.1.pos, bf16[1024,128]{1,0:T(8,128)(2,1)S(1)} %get-tuple-element.54.refs_0_, bf16[1024,128]{1,0:T(8,128)(2,1)S(1)} %collective-permute-done.refs_3_.refs_1_, ...), custom_call_target="tpu_custom_call" | custom-call | flops 4294967296 | bytes 10485760 | tf_op jit(solution)/shard_map/first_grads/pallas_call | solution.py:366
  155.3 3.6 %outer_grads.1 = (bf16[4,4,4,16,640]{4,3,2,1,0:T(8,128)(2,1)S(1)}, bf16[4,4,4,16,640]{4,3,2,1,0:T(8,128)(2,1)S(1)}) custom-call(s32[3]{0:T(128)S(1)} %pad_add_fusion.1.pos, bf16[1024,1024]{1,0:T(8,128)(2,1)S(1)} %get-tuple-element.89.act1, bf16[1024,1024]{1,0:T(8,128)(2,1)S(1)} %get-tuple-element.90.act2, bf16[1024,256]{1,0:T(8,128)(2,1)S(1)} %get-tuple-element.91.gl, ...), custom_call_target="tpu_custom_call" | custom-call | flops 2684354560 | bytes 8388608 | tf_op jit(solution)/shard_map/outer_grads/pallas_call | solution.py:333
  159.4 2.7 %collective-permute-done.16 = bf16[4,4,4,16,640]{4,3,2,1,0:T(8,128)(2,1)S(1)} collective-permute-done((bf16[4,4,4,16,640]{4,3,2,1,0:T(8,128)(2,1)S(1)}, bf16[4,4,4,16,640]{4,3,2,1,0:T(8,128)(2,1)S(1)}, u32[]{:S(2)}, u32[]{:S(2)}) %collective-permute-start.16) | collective-permute-done | bytes 1310752 | tf_op jit(solution)/shard_map/ppermute | solution.py:423
  163.0 54.0 %all_to_all.20.parts = bf16[64,16,1664]{2,1,0:T(8,128)(2,1)S(1)} all-to-all(bf16[64,16,1664]{2,1,0:T(8,128)(2,1)S(1)} %join_cores.1), channel_id=1, replica_groups=mesh['y'=4,'x'=4,'core'=2,'rep'=4] {'y','x','rep'}, dimensions={0} | all-to-all | bytes 6815744 | tf_op jit(solution)/shard_map/all_to_all | solution.py:484
  (62 shorter events, 13.0 us)
Async XLA Ops:
  0.6 28.8 %copy-start.16 = (s32[32,8]{0,1:T(8,128)S(1)}, s32[32,8]{0,1:T(8,128)}, u32[]{:S(2)}) copy-start(s32[32,8]{0,1:T(8,128)} %param.12) | copy-start | bytes 3076
  1.4 30.0 %copy-start.1 = (s32[128,1]{1,0:T(8,128)}, s32[128,1]{1,0:T(8,128)S(1)}, u32[]{:S(2)}) copy-start(s32[128,1]{1,0:T(8,128)S(1)} %copy.18.brow) | copy-start | bytes 1540
  5.3 24.1 %all-to-all-start = ((bf16[16,144,128]{2,1,0:T(8,128)(2,1)}), bf16[16,144,128]{2,1,0:T(8,128)(2,1)S(1)}, u32[]{:S(2)}, u32[]{:S(2)}) async-start(bf16[16,144,128]{2,1,0:T(8,128)(2,1)} %get-tuple-element.49), calls=%async_computation | async-start | bytes 1179648 | tf_op jit(solution)/shard_map/all_to_all | solution.py:427
  12.4 10.4 %collective-permute-start = (bf16[1024,128]{1,0:T(8,128)(2,1)S(1)}, bf16[1024,128]{1,0:T(8,128)(2,1)S(1)}, u32[]{:S(2)}, u32[]{:S(2)}) collective-permute-start(bf16[1024,128]{1,0:T(8,128)(2,1)S(1)} %get-tuple-element.51), channel_id=1, source_target_pairs={{0,1},{1,2},{2,3},{3,0},{4,5},{5,6},{6,7},{7,4},{8,9},{9,10},{10,1... | collective-permute-start | bytes 786440 | tf_op jit(solution)/shard_map/ppermute | solution.py:423
  14.4 14.9 %collective-permute-start.1 = (bf16[1024,128]{1,0:T(8,128)(2,1)S(1)}, bf16[1024,128]{1,0:T(8,128)(2,1)S(1)}, u32[]{:S(2)}, u32[]{:S(2)}) collective-permute-start(bf16[1024,128]{1,0:T(8,128)(2,1)S(1)} %get-tuple-element.52), channel_id=1, source_target_pairs={{0,2},{1,3},{2,0},{3,1},{4,6},{5,7},{6,4},{7,5},{8,10},{9,11},{10,... | collective-permute-start | bytes 786440 | tf_op jit(solution)/shard_map/ppermute | solution.py:423
  18.0 11.4 %collective-permute-start.2 = (bf16[1024,128]{1,0:T(8,128)(2,1)S(1)}, bf16[1024,128]{1,0:T(8,128)(2,1)S(1)}, u32[]{:S(2)}, u32[]{:S(2)}) collective-permute-start(bf16[1024,128]{1,0:T(8,128)(2,1)S(1)} %get-tuple-element.53), channel_id=1, source_target_pairs={{0,3},{1,0},{2,1},{3,2},{4,7},{5,4},{6,5},{7,6},{8,11},{9,8},{10,9... | collective-permute-start | bytes 786440 | tf_op jit(solution)/shard_map/ppermute | solution.py:423
  29.3 2.1 copy-start.12
  29.4 2.1 collective-permute-start.3
  44.1 23.0 %all-to-all-start.1 = ((bf16[16,128,128]{2,1,0:T(8,128)(2,1)}), bf16[16,128,128]{2,1,0:T(8,128)(2,1)S(1)}, u32[]{:S(2)}, u32[]{:S(2)}) async-start(bf16[16,128,128]{2,1,0:T(8,128)(2,1)} %get-tuple-element.59), calls=%async_computation.1 | async-start | bytes 1048576 | tf_op jit(solution)/shard_map/all_to_all | solution.py:427
  51.0 10.6 %collective-permute-start.4 = (bf16[1056,128]{1,0:T(8,128)(2,1)}, bf16[1056,128]{1,0:T(8,128)(2,1)S(1)}, u32[]{:S(2)}, u32[]{:S(2)}) collective-permute-start(bf16[1056,128]{1,0:T(8,128)(2,1)} %get-tuple-element.61), channel_id=1, source_target_pairs={{0,1},{1,2},{2,3},{3,0},{4,5},{5,6},{6,7},{7,4},{8,9},{9,10},{10,1... | collective-permute-start | bytes 811016 | tf_op jit(solution)/shard_map/ppermute | solution.py:423
  52.2 14.6 %collective-permute-start.5 = (bf16[1056,128]{1,0:T(8,128)(2,1)}, bf16[1056,128]{1,0:T(8,128)(2,1)S(1)}, u32[]{:S(2)}, u32[]{:S(2)}) collective-permute-start(bf16[1056,128]{1,0:T(8,128)(2,1)} %get-tuple-element.62), channel_id=1, source_target_pairs={{0,2},{1,3},{2,0},{3,1},{4,6},{5,7},{6,4},{7,5},{8,10},{9,11},{10,... | collective-permute-start | bytes 811016 | tf_op jit(solution)/shard_map/ppermute | solution.py:423
  54.6 12.5 %collective-permute-start.6 = (bf16[1056,128]{1,0:T(8,128)(2,1)}, bf16[1056,128]{1,0:T(8,128)(2,1)S(1)}, u32[]{:S(2)}, u32[]{:S(2)}) collective-permute-start(bf16[1056,128]{1,0:T(8,128)(2,1)} %get-tuple-element.63), channel_id=1, source_target_pairs={{0,3},{1,0},{2,1},{3,2},{4,7},{5,4},{6,5},{7,6},{8,11},{9,8},{10,9... | collective-permute-start | bytes 811016 | tf_op jit(solution)/shard_map/ppermute | solution.py:423
  67.1 1.9 copy-start.13
  67.1 1.9 collective-permute-start.7
  69.8 23.6 %copy-start.5 = (bf16[1056,128]{1,0:T(8,128)(2,1)S(1)}, bf16[1056,128]{1,0:T(8,128)(2,1)}, u32[]{:S(2)}) copy-start(bf16[1056,128]{1,0:T(8,128)(2,1)} %get-tuple-element.64.lab0.refs_1_.refs_4_) | copy-start | bytes 811012
  69.8 23.6 %copy-start.8 = (s32[1,4096]{1,0:T(1,128)S(1)}, s32[1,4096]{1,0:T(1,128)}, u32[]{:S(2)}) copy-start(s32[1,4096]{1,0:T(1,128)} %param.15) | copy-start | bytes 49156
  69.8 23.6 %copy-start.9 = (s32[1,4096]{1,0:T(1,128)S(1)}, s32[1,4096]{1,0:T(1,128)}, u32[]{:S(2)}) copy-start(s32[1,4096]{1,0:T(1,128)} %param.14) | copy-start | bytes 49156
  81.6 23.0 %all-to-all-start.2 = ((bf16[16,128,128]{2,1,0:T(8,128)(2,1)}), bf16[16,128,128]{2,1,0:T(8,128)(2,1)}, u32[]{:S(2)}, u32[]{:S(2)}) async-start(bf16[16,128,128]{2,1,0:T(8,128)(2,1)} %get-tuple-element.70), calls=%async_computation.2 | async-start | bytes 1048576 | tf_op jit(solution)/shard_map/all_to_all | solution.py:427
  88.5 9.8 %collective-permute-start.8 = (bf16[1024,128]{1,0:T(8,128)(2,1)}, bf16[1024,128]{1,0:T(8,128)(2,1)S(1)}, u32[]{:S(2)}, u32[]{:S(2)}) collective-permute-start(bf16[1024,128]{1,0:T(8,128)(2,1)} %get-tuple-element.72), channel_id=1, source_target_pairs={{0,1},{1,2},{2,3},{3,0},{4,5},{5,6},{6,7},{7,4},{8,9},{9,10},{10,1... | collective-permute-start | bytes 786440 | tf_op jit(solution)/shard_map/ppermute | solution.py:423
  90.1 14.5 %collective-permute-start.9 = (bf16[1024,128]{1,0:T(8,128)(2,1)}, bf16[1024,128]{1,0:T(8,128)(2,1)S(1)}, u32[]{:S(2)}, u32[]{:S(2)}) collective-permute-start(bf16[1024,128]{1,0:T(8,128)(2,1)} %get-tuple-element.73), channel_id=1, source_target_pairs={{0,2},{1,3},{2,0},{3,1},{4,6},{5,7},{6,4},{7,5},{8,10},{9,11},{10,... | collective-permute-start | bytes 786440 | tf_op jit(solution)/shard_map/ppermute | solution.py:423
  92.7 11.9 %collective-permute-start.10 = (bf16[1024,128]{1,0:T(8,128)(2,1)}, bf16[1024,128]{1,0:T(8,128)(2,1)S(1)}, u32[]{:S(2)}, u32[]{:S(2)}) collective-permute-start(bf16[1024,128]{1,0:T(8,128)(2,1)} %get-tuple-element.74), channel_id=1, source_target_pairs={{0,3},{1,0},{2,1},{3,2},{4,7},{5,4},{6,5},{7,6},{8,11},{9,8},{10,9... | collective-permute-start | bytes 786440 | tf_op jit(solution)/shard_map/ppermute | solution.py:423
  104.6 3.1 %collective-permute-start.11 = (bf16[16,128,128]{2,1,0:T(8,128)(2,1)}, bf16[16,128,128]{2,1,0:T(8,128)(2,1)}, u32[]{:S(2)}, u32[]{:S(2)}) collective-permute-start(bf16[16,128,128]{2,1,0:T(8,128)(2,1)} %all-to-all-done.2.near), channel_id=1, source_target_pairs={{0,4},{4,0},{1,5},{5,1},{2,6},{6,2},{3,7},{7,3},{8,12},{12,8},{9,1... | collective-permute-start | bytes 1572872 | tf_op jit(solution)/shard_map/ppermute | solution.py:423
  107.7 16.2 %copy-start.3 = (bf16[4,512,1024]{2,1,0:T(8,128)(2,1)S(1)}, bf16[4,512,1024]{2,1,0:T(8,128)(2,1)}, u32[]{:S(2)}) copy-start(bf16[4,512,1024]{2,1,0:T(8,128)(2,1)} %refs_6_.1) | copy-start | bytes 12582916
  107.7 16.2 %copy-start.6 = (bf16[1024,128]{1,0:T(8,128)(2,1)S(1)}, bf16[1024,128]{1,0:T(8,128)(2,1)}, u32[]{:S(2)}) copy-start(bf16[1024,128]{1,0:T(8,128)(2,1)} %get-tuple-element.75.refs_2_.refs_8_) | copy-start | bytes 786436
  119.3 10.2 %collective-permute-start.12 = (bf16[1024,128]{1,0:T(8,128)(2,1)}, bf16[1024,128]{1,0:T(8,128)(2,1)S(1)}, u32[]{:S(2)}, u32[]{:S(2)}) collective-permute-start(bf16[1024,128]{1,0:T(8,128)(2,1)} %get-tuple-element.82), channel_id=1, source_target_pairs={{0,1},{1,2},{2,3},{3,0},{4,5},{5,6},{6,7},{7,4},{8,9},{9,10},{10,1... | collective-permute-start | bytes 786440 | tf_op jit(solution)/shard_map/ppermute | solution.py:423
  120.7 15.1 %collective-permute-start.13 = (bf16[1024,128]{1,0:T(8,128)(2,1)}, bf16[1024,128]{1,0:T(8,128)(2,1)S(1)}, u32[]{:S(2)}, u32[]{:S(2)}) collective-permute-start(bf16[1024,128]{1,0:T(8,128)(2,1)} %get-tuple-element.83), channel_id=1, source_target_pairs={{0,2},{1,3},{2,0},{3,1},{4,6},{5,7},{6,4},{7,5},{8,10},{9,11},{10,... | collective-permute-start | bytes 786440 | tf_op jit(solution)/shard_map/ppermute | solution.py:423
  123.2 12.5 %copy-start.4 = (bf16[1024,1024]{1,0:T(8,128)(2,1)S(1)}, bf16[1024,1024]{1,0:T(8,128)(2,1)}, u32[]{:S(2)}) copy-start(bf16[1024,1024]{1,0:T(8,128)(2,1)} %refs_7_.1) | copy-start | bytes 6291460
  123.2 12.5 %copy-start.7 = (bf16[1024,128]{1,0:T(8,128)(2,1)S(1)}, bf16[1024,128]{1,0:T(8,128)(2,1)}, u32[]{:S(2)}) copy-start(bf16[1024,128]{1,0:T(8,128)(2,1)} %get-tuple-element.81.refs_0_.refs_12_) | copy-start | bytes 786436
  123.2 12.5 %copy-start.11 = (f32[1024,256]{1,0:T(8,128)S(1)}, f32[1024,256]{1,0:T(8,128)}, u32[]{:S(2)}) copy-start(f32[1024,256]{1,0:T(8,128)} %copy-done.10) | copy-start | bytes 3145732
  123.2 12.5 %collective-permute-start.14 = (bf16[1024,128]{1,0:T(8,128)(2,1)}, bf16[1024,128]{1,0:T(8,128)(2,1)S(1)}, u32[]{:S(2)}, u32[]{:S(2)}) collective-permute-start(bf16[1024,128]{1,0:T(8,128)(2,1)} %get-tuple-element.84), channel_id=1, source_target_pairs={{0,3},{1,0},{2,1},{3,2},{4,7},{5,4},{6,5},{7,6},{8,11},{9,8},{10,9... | collective-permute-start | bytes 786440 | tf_op jit(solution)/shard_map/ppermute | solution.py:423
  154.9 7.2 %collective-permute-start.15 = (bf16[4,4,4,16,1024]{4,3,2,1,0:T(8,128)(2,1)S(1)}, bf16[4,4,4,16,1024]{4,3,2,1,0:T(8,128)(2,1)S(1)}, u32[]{:S(2)}, u32[]{:S(2)}) collective-permute-start(bf16[4,4,4,16,1024]{4,3,2,1,0:T(8,128)(2,1)S(1)} %get-tuple-element.88), channel_id=1, source_target_pairs={{0,4},{4,0},{1,5},{5,1},{2,6},{6,2},{3,7},{7,3},{8,12},{12,8},{9,1... | collective-permute-start | bytes 6291464 | tf_op jit(solution)/shard_map/ppermute | solution.py:423
  158.9 3.2 %collective-permute-start.16 = (bf16[4,4,4,16,640]{4,3,2,1,0:T(8,128)(2,1)S(1)}, bf16[4,4,4,16,640]{4,3,2,1,0:T(8,128)(2,1)S(1)}, u32[]{:S(2)}, u32[]{:S(2)}) collective-permute-start(bf16[4,4,4,16,640]{4,3,2,1,0:T(8,128)(2,1)S(1)} %get-tuple-element.94), channel_id=1, source_target_pairs={{0,4},{4,0},{1,5},{5,1},{2,6},{6,2},{3,7},{7,3},{8,12},{12,8},{9,1... | collective-permute-start | bytes 3932168 | tf_op jit(solution)/shard_map/ppermute | solution.py:423
  (5 other events, 4.5 us)

commit v3 on v2

--- a/solution.py
+++ b/solution.py
@@ -114,18 +114,16 @@
         at = R + t * TILE
         joined[at : at + TILE] = near[t, :TILE]
         joined[at + R // 2 : at + R // 2 + TILE] = far[t, :TILE]
-    for c in range(CUTS):
-        copies[c].wait()
-
-        @pl.loop(c * STEP, (c + 1) * STEP)
-        def _(b):
-            parts = []
-            for k in range(K):
-                at = pl.multiple_of(cols[b * K + k] * TILE, TILE)
-                parts.append(joined[pl.ds(at, TILE), :])
-            left = jnp.concatenate([held[b, k] for k in range(K)], axis=1)
-            got = dot(left, jnp.concatenate(parts, axis=0), 1, 0).astype(BF)
-            out[pl.ds(pl.multiple_of(b * TILE, TILE), TILE), :] = got
+    for b in range(NB):
+        if b % STEP == 0:
+            copies[b // STEP].wait()
+        parts = []
+        for k in range(K):
+            at = pl.multiple_of(cols[b * K + k] * TILE, TILE)
+            parts.append(joined[pl.ds(at, TILE), :])
+        left = jnp.concatenate([held[b, k] for k in range(K)], axis=1)
+        got = dot(left, jnp.concatenate(parts, axis=0), 1, 0)
+        out[b * TILE : (b + 1) * TILE, :] = got.astype(BF)
 
     if not last:
         got = export_rows(out, brow)

time: 219 us -> 207 us (0.945)
  Pallas kernels: 71.2 us -> 59.8 us
    pallas_call x3, Pallas kernels: 35.2 us -> 23.8 us  [propagate(): pl.pallas_call(functools.partial(prop_kernel, h), in_specs=[whole(pltpu.S...]
where the time goes in v3:
time: 207 us; the launch traced here: 206 us
  Pallas kernels  59.8 us (29%)
  blocking collectives  54 us (26%)
  starting transfers between devices  42.6 us (21%)
  waiting for transfers between devices  39.9 us (19%)
  local copies, waits for them, and re-layouts  8.58 us (4%)
    all_to_all x1, blocking collectives, per_device(): lax.all_to_all(parts, ('y', 'x', 'rep'), split_axis=0, concat_axis=0, til...  54 us
    ppermute x17, waiting for transfers between devices, shift(): lax.ppermute(value, axis, [(i, (i + by) % size) for i in range(size)])  39.8 us
    pallas_call x3, Pallas kernels, propagate(): pl.pallas_call(functools.partial(prop_kernel, h), in_specs=[whole(pltpu.S...  23.8 us
    ppermute x17, starting transfers between devices, shift(): lax.ppermute(value, axis, [(i, (i + by) % size) for i in range(size)])  21.6 us
    all_to_all x3, starting transfers between devices, spread(): lax.all_to_all(export, ('y', 'x'), split_axis=0, concat_axis=0, tiled=True)  20.9 us
    pallas_call x1, Pallas kernels, mlp(): pl.pallas_call(mlp_kernel, grid_spec=pltpu.PrefetchScalarGridSpec(num_sca...  14 us
    unnamed x35, local copies, waits for them, and re-layouts  6.53 us
    pallas_call x1, Pallas kernels, first_layer_early(): pl.pallas_call(early_kernel, grid_spec=pltpu.PrefetchScalarGridSpec(num_s...  5.6 us
  transfers between devices with their start and end apart: 20, of which 11 were waited for; matrix products, arithmetic and copies ran while one was open for 2% of the time, Pallas kernels for 6%

profile of v3, /device:TPU:0, one launch (start us, length us, event | category | flops | bytes accessed | tf_op | source)
XLA Modules:
  0.0 206.5 jit_solution(7251966156010468098)
XLA Ops:
  1.5 1.2 copy-done
  3.4 1.9 export_first.1
  5.3 7.1 %all-to-all-start = ((bf16[16,144,128]{2,1,0:T(8,128)(2,1)}), bf16[16,144,128]{2,1,0:T(8,128)(2,1)S(1)}, u32[]{:S(2)}, u32[]{:S(2)}) async-start(bf16[16,144,128]{2,1,0:T(8,128)(2,1)} %get-tuple-element.49), calls=%async_computation | async-start | bytes 1179648 | tf_op jit(solution)/shard_map/all_to_all | solution.py:425
  12.4 2.0 collective-permute-start
  14.4 3.6 %collective-permute-start.1 = (bf16[1024,128]{1,0:T(8,128)(2,1)S(1)}, bf16[1024,128]{1,0:T(8,128)(2,1)S(1)}, u32[]{:S(2)}, u32[]{:S(2)}) collective-permute-start(bf16[1024,128]{1,0:T(8,128)(2,1)S(1)} %get-tuple-element.52), channel_id=1, source_target_pairs={{0,2},{1,3},{2,0},{3,1},{4,6},{5,7},{6,4},{7,5},{8,10},{9,11},{10,... | collective-permute-start | bytes 786440 | tf_op jit(solution)/shard_map/ppermute | solution.py:421
  19.0 3.8 %collective-permute-done.refs_3_.refs_1_ = bf16[1024,128]{1,0:T(8,128)(2,1)S(1)} collective-permute-done((bf16[1024,128]{1,0:T(8,128)(2,1)S(1)}, bf16[1024,128]{1,0:T(8,128)(2,1)S(1)}, u32[]{:S(2)}, u32[]{:S(2)}) %collective-permute-start) | collective-permute-done | bytes 262176 | tf_op jit(solution)/shard_map/ppermute | solution.py:421
  22.8 6.5 %collective-permute-done.1.refs_6_.refs_2_ = bf16[1024,128]{1,0:T(8,128)(2,1)S(1)} collective-permute-done((bf16[1024,128]{1,0:T(8,128)(2,1)S(1)}, bf16[1024,128]{1,0:T(8,128)(2,1)S(1)}, u32[]{:S(2)}, u32[]{:S(2)}) %collective-permute-start.1) | collective-permute-done | bytes 262176 | tf_op jit(solution)/shard_map/ppermute | solution.py:421
  32.2 8.1 %propagate_0.1 = (bf16[4096,128]{1,0:T(8,128)(2,1)}, bf16[16,128,128]{2,1,0:T(8,128)(2,1)}, bf16[1056,128]{1,0:T(8,128)(2,1)}, bf16[1056,128]{1,0:T(8,128)(2,1)}...) custom-call(s32[259]{0:T(512)} %pad_add_fusion.cols, bf16[32,8,128,128]{3,2,1,0:T(8,128)(2,1)} %tiles.5, ...), custom_call_target="tpu_custom_call" | custom-call | flops 1073741824 | bytes 12582912 | tf_op jit(solution)/shard_map/propagate_0/pallas_call | solution.py:159
  40.3 6.9 %all-to-all-start.1 = ((bf16[16,128,128]{2,1,0:T(8,128)(2,1)}), bf16[16,128,128]{2,1,0:T(8,128)(2,1)S(1)}, u32[]{:S(2)}, u32[]{:S(2)}) async-start(bf16[16,128,128]{2,1,0:T(8,128)(2,1)} %get-tuple-element.59), calls=%async_computation.1 | async-start | bytes 1048576 | tf_op jit(solution)/shard_map/all_to_all | solution.py:425
  47.2 1.2 collective-permute-start.4
  48.4 2.4 %collective-permute-start.5 = (bf16[1056,128]{1,0:T(8,128)(2,1)}, bf16[1056,128]{1,0:T(8,128)(2,1)S(1)}, u32[]{:S(2)}, u32[]{:S(2)}) collective-permute-start(bf16[1056,128]{1,0:T(8,128)(2,1)} %get-tuple-element.62), channel_id=1, source_target_pairs={{0,2},{1,3},{2,0},{3,1},{4,6},{5,7},{6,4},{7,5},{8,10},{9,11},{10,... | collective-permute-start | bytes 811016 | tf_op jit(solution)/shard_map/ppermute | solution.py:421
  50.8 1.2 collective-permute-start.6
  52.1 5.7 %collective-permute-done.4.lab1.refs_4_.refs_5_ = bf16[1056,128]{1,0:T(8,128)(2,1)S(1)} collective-permute-done((bf16[1056,128]{1,0:T(8,128)(2,1)}, bf16[1056,128]{1,0:T(8,128)(2,1)S(1)}, u32[]{:S(2)}, u32[]{:S(2)}) %collective-permute-start.4) | collective-permute-done | bytes 270368 | tf_op jit(solution)/shard_map/ppermute | solution.py:421
  57.8 5.3 %collective-permute-done.5.lab2.refs_7_.refs_6_ = bf16[1056,128]{1,0:T(8,128)(2,1)S(1)} collective-permute-done((bf16[1056,128]{1,0:T(8,128)(2,1)}, bf16[1056,128]{1,0:T(8,128)(2,1)S(1)}, u32[]{:S(2)}, u32[]{:S(2)}) %collective-permute-start.5) | collective-permute-done | bytes 270368 | tf_op jit(solution)/shard_map/ppermute | solution.py:421
  63.4 1.9 collective-permute-done.7.far
  66.1 7.9 %propagate_1.1 = (bf16[4096,128]{1,0:T(8,128)(2,1)}, bf16[16,128,128]{2,1,0:T(8,128)(2,1)}, bf16[1024,128]{1,0:T(8,128)(2,1)}, bf16[1024,128]{1,0:T(8,128)(2,1)}...) custom-call(s32[259]{0:T(512)} %pad_add_fusion.cols, bf16[32,8,128,128]{3,2,1,0:T(8,128)(2,1)} %tiles.5, ...), custom_call_target="tpu_custom_call" | custom-call | flops 1073741824 | bytes 12582912 | tf_op jit(solution)/shard_map/propagate_1/pallas_call | solution.py:159
  74.0 6.9 %all-to-all-start.2 = ((bf16[16,128,128]{2,1,0:T(8,128)(2,1)}), bf16[16,128,128]{2,1,0:T(8,128)(2,1)}, u32[]{:S(2)}, u32[]{:S(2)}) async-start(bf16[16,128,128]{2,1,0:T(8,128)(2,1)} %get-tuple-element.70), calls=%async_computation.2 | async-start | bytes 1048576 | tf_op jit(solution)/shard_map/all_to_all | solution.py:425
  80.9 1.6 collective-permute-start.8
  82.5 2.6 %collective-permute-start.9 = (bf16[1024,128]{1,0:T(8,128)(2,1)}, bf16[1024,128]{1,0:T(8,128)(2,1)S(1)}, u32[]{:S(2)}, u32[]{:S(2)}) collective-permute-start(bf16[1024,128]{1,0:T(8,128)(2,1)} %get-tuple-element.73), channel_id=1, source_target_pairs={{0,2},{1,3},{2,0},{3,1},{4,6},{5,7},{6,4},{7,5},{8,10},{9,11},{10,... | collective-permute-start | bytes 786440 | tf_op jit(solution)/shard_map/ppermute | solution.py:421
  85.8 3.8 %count_labels.1.refs_5_ = f32[1024,256]{1,0:T(8,128)S(1)} custom-call(s32[3]{0:T(128)S(1)} %pad_add_fusion.1.pos, bf16[1056,128]{1,0:T(8,128)(2,1)S(1)} %copy-done.5, bf16[1056,128]{1,0:T(8,128)(2,1)S(1)} %collective-permute-done.4.lab1.refs_4_.refs_5_, bf16[1056,128]{1,0:T(8,128)(2,1)S(1)} %collective-permute-done.5.lab2.refs_7_.refs_6_, ...), custom_call_target="tpu_custom_call" | custom-call | flops 2147483648 | bytes 2097152 | tf_op jit(solution)/shard_map/count_labels/pallas_call | solution.py:206
  90.8 6.2 %collective-permute-done.9.refs_8_.refs_10_ = bf16[1024,128]{1,0:T(8,128)(2,1)S(1)} collective-permute-done((bf16[1024,128]{1,0:T(8,128)(2,1)}, bf16[1024,128]{1,0:T(8,128)(2,1)S(1)}, u32[]{:S(2)}, u32[]{:S(2)}) %collective-permute-start.9) | collective-permute-done | bytes 262176 | tf_op jit(solution)/shard_map/ppermute | solution.py:421
  97.0 2.0 copy.23
  100.1 7.8 %propagate_2.1 = (bf16[1024,128]{1,0:T(8,128)(2,1)}, bf16[1024,128]{1,0:T(8,128)(2,1)}, bf16[1024,128]{1,0:T(8,128)(2,1)}, bf16[1024,128]{1,0:T(8,128)(2,1)}) custom-call(s32[259]{0:T(512)} %pad_add_fusion.cols, bf16[32,8,128,128]{3,2,1,0:T(8,128)(2,1)} %tiles.5, bf16[4096,128]{1,0:T(8,128)(2,1)} %get-tuple-element.79.hop, ...), custom_call_target="tpu_custom_call" | custom-call | flops 1073741824 | bytes 12582912 | tf_op jit(solution)/shard_map/propagate_2/pallas_call | solution.py:159
  107.9 1.3 collective-permute-start.12
  109.3 2.6 %collective-permute-start.13 = (bf16[1024,128]{1,0:T(8,128)(2,1)}, bf16[1024,128]{1,0:T(8,128)(2,1)S(1)}, u32[]{:S(2)}, u32[]{:S(2)}) collective-permute-start(bf16[1024,128]{1,0:T(8,128)(2,1)} %get-tuple-element.83), channel_id=1, source_target_pairs={{0,2},{1,3},{2,0},{3,1},{4,6},{5,7},{6,4},{7,5},{8,10},{9,11},{10,... | collective-permute-start | bytes 786440 | tf_op jit(solution)/shard_map/ppermute | solution.py:421
  112.5 5.6 %first_layer_early.1.refs_4_ = f32[1024,1024]{1,0:T(8,128)S(1)} custom-call(s32[3]{0:T(128)S(1)} %pad_add_fusion.1.pos, bf16[1024,128]{1,0:T(8,128)(2,1)S(1)} %get-tuple-element.54.refs_0_, bf16[1056,128]{1,0:T(8,128)(2,1)S(1)} %copy-done.5, bf16[1024,128]{1,0:T(8,128)(2,1)S(1)} %copy-done.6, bf16[1024,128]{1,0:T(8,128)(2,1)S(1)} %collective-permute-done.refs_3_.refs_1_, ...), custom_call_target="tpu_custom_call" | custom-call | flops 3221225472 | bytes 11534336 | tf_op jit(solution)/shard_map/first_layer_early/pallas_call | solution.py:272
  118.2 6.2 %collective-permute-done.13.refs_2_.refs_14_ = bf16[1024,128]{1,0:T(8,128)(2,1)S(1)} collective-permute-done((bf16[1024,128]{1,0:T(8,128)(2,1)}, bf16[1024,128]{1,0:T(8,128)(2,1)S(1)}, u32[]{:S(2)}, u32[]{:S(2)}) %collective-permute-start.13) | collective-permute-done | bytes 262176 | tf_op jit(solution)/shard_map/ppermute | solution.py:421
  124.4 14.0 %mlp.1 = (bf16[1024,1024]{1,0:T(8,128)(2,1)S(1)}, bf16[1024,1024]{1,0:T(8,128)(2,1)S(1)}, bf16[1024,256]{1,0:T(8,128)(2,1)S(1)}, bf16[1024,1024]{1,0:T(8,128)(2,1)S(1)}, bf16[1024,1024]{1,0:T(8,128)(2,1)S(1)}) custom-call(s32[3]{0:T(128)S(1)} %pad_add_fusion.1.pos, bf16[1024,128]{1,0:T(8,128)(2,1)S(1)} %copy-done.7, ...), custom_call_target="tpu_custom_call" | custom-call | flops 6442450944 | bytes 20971520 | tf_op jit(solution)/shard_map/mlp/pallas_call | solution.py:291
  138.4 5.2 %first_grads.1 = (bf16[4,4,4,16,1024]{4,3,2,1,0:T(8,128)(2,1)S(1)}, bf16[4,4,4,16,1024]{4,3,2,1,0:T(8,128)(2,1)S(1)}) custom-call(s32[3]{0:T(128)S(1)} %pad_add_fusion.1.pos, bf16[1024,128]{1,0:T(8,128)(2,1)S(1)} %get-tuple-element.54.refs_0_, bf16[1024,128]{1,0:T(8,128)(2,1)S(1)} %collective-permute-done.refs_3_.refs_1_, ...), custom_call_target="tpu_custom_call" | custom-call | flops 4294967296 | bytes 10485760 | tf_op jit(solution)/shard_map/first_grads/pallas_call | solution.py:364
  143.6 3.6 %outer_grads.1 = (bf16[4,4,4,16,640]{4,3,2,1,0:T(8,128)(2,1)S(1)}, bf16[4,4,4,16,640]{4,3,2,1,0:T(8,128)(2,1)S(1)}) custom-call(s32[3]{0:T(128)S(1)} %pad_add_fusion.1.pos, bf16[1024,1024]{1,0:T(8,128)(2,1)S(1)} %get-tuple-element.89.act1, bf16[1024,1024]{1,0:T(8,128)(2,1)S(1)} %get-tuple-element.90.act2, bf16[1024,256]{1,0:T(8,128)(2,1)S(1)} %get-tuple-element.91.gl, ...), custom_call_target="tpu_custom_call" | custom-call | flops 2684354560 | bytes 8388608 | tf_op jit(solution)/shard_map/outer_grads/pallas_call | solution.py:331
  147.8 2.7 %collective-permute-done.16 = bf16[4,4,4,16,640]{4,3,2,1,0:T(8,128)(2,1)S(1)} collective-permute-done((bf16[4,4,4,16,640]{4,3,2,1,0:T(8,128)(2,1)S(1)}, bf16[4,4,4,16,640]{4,3,2,1,0:T(8,128)(2,1)S(1)}, u32[]{:S(2)}, u32[]{:S(2)}) %collective-permute-start.16) | collective-permute-done | bytes 1310752 | tf_op jit(solution)/shard_map/ppermute | solution.py:421
  151.4 54.0 %all_to_all.20.parts = bf16[64,16,1664]{2,1,0:T(8,128)(2,1)S(1)} all-to-all(bf16[64,16,1664]{2,1,0:T(8,128)(2,1)S(1)} %join_cores.1), channel_id=1, replica_groups=mesh['y'=4,'x'=4,'core'=2,'rep'=4] {'y','x','rep'}, dimensions={0} | all-to-all | bytes 6815744 | tf_op jit(solution)/shard_map/all_to_all | solution.py:482
  (62 shorter events, 12.8 us)
Async XLA Ops:
  0.6 28.8 %copy-start.16 = (s32[32,8]{0,1:T(8,128)S(1)}, s32[32,8]{0,1:T(8,128)}, u32[]{:S(2)}) copy-start(s32[32,8]{0,1:T(8,128)} %param.12) | copy-start | bytes 3076
  1.4 30.0 %copy-start.1 = (s32[128,1]{1,0:T(8,128)}, s32[128,1]{1,0:T(8,128)S(1)}, u32[]{:S(2)}) copy-start(s32[128,1]{1,0:T(8,128)S(1)} %copy.18.brow) | copy-start | bytes 1540
  5.3 24.1 %all-to-all-start = ((bf16[16,144,128]{2,1,0:T(8,128)(2,1)}), bf16[16,144,128]{2,1,0:T(8,128)(2,1)S(1)}, u32[]{:S(2)}, u32[]{:S(2)}) async-start(bf16[16,144,128]{2,1,0:T(8,128)(2,1)} %get-tuple-element.49), calls=%async_computation | async-start | bytes 1179648 | tf_op jit(solution)/shard_map/all_to_all | solution.py:425
  12.4 10.4 %collective-permute-start = (bf16[1024,128]{1,0:T(8,128)(2,1)S(1)}, bf16[1024,128]{1,0:T(8,128)(2,1)S(1)}, u32[]{:S(2)}, u32[]{:S(2)}) collective-permute-start(bf16[1024,128]{1,0:T(8,128)(2,1)S(1)} %get-tuple-element.51), channel_id=1, source_target_pairs={{0,1},{1,2},{2,3},{3,0},{4,5},{5,6},{6,7},{7,4},{8,9},{9,10},{10,1... | collective-permute-start | bytes 786440 | tf_op jit(solution)/shard_map/ppermute | solution.py:421
  14.4 14.9 %collective-permute-start.1 = (bf16[1024,128]{1,0:T(8,128)(2,1)S(1)}, bf16[1024,128]{1,0:T(8,128)(2,1)S(1)}, u32[]{:S(2)}, u32[]{:S(2)}) collective-permute-start(bf16[1024,128]{1,0:T(8,128)(2,1)S(1)} %get-tuple-element.52), channel_id=1, source_target_pairs={{0,2},{1,3},{2,0},{3,1},{4,6},{5,7},{6,4},{7,5},{8,10},{9,11},{10,... | collective-permute-start | bytes 786440 | tf_op jit(solution)/shard_map/ppermute | solution.py:421
  18.0 11.4 %collective-permute-start.2 = (bf16[1024,128]{1,0:T(8,128)(2,1)S(1)}, bf16[1024,128]{1,0:T(8,128)(2,1)S(1)}, u32[]{:S(2)}, u32[]{:S(2)}) collective-permute-start(bf16[1024,128]{1,0:T(8,128)(2,1)S(1)} %get-tuple-element.53), channel_id=1, source_target_pairs={{0,3},{1,0},{2,1},{3,2},{4,7},{5,4},{6,5},{7,6},{8,11},{9,8},{10,9... | collective-permute-start | bytes 786440 | tf_op jit(solution)/shard_map/ppermute | solution.py:421
  29.3 2.1 %copy-start.12 = (bf16[16,144,128]{2,1,0:T(8,128)(2,1)}, bf16[16,144,128]{2,1,0:T(8,128)(2,1)S(1)}, u32[]{:S(2)}) copy-start(bf16[16,144,128]{2,1,0:T(8,128)(2,1)S(1)} %all-to-all-done.near) | copy-start | bytes 1769476
  29.4 2.1 %collective-permute-start.3 = (bf16[16,144,128]{2,1,0:T(8,128)(2,1)S(1)}, bf16[16,144,128]{2,1,0:T(8,128)(2,1)S(1)}, u32[]{:S(2)}, u32[]{:S(2)}) collective-permute-start(bf16[16,144,128]{2,1,0:T(8,128)(2,1)S(1)} %all-to-all-done.near), channel_id=1, source_target_pairs={{0,4},{4,0},{1,5},{5,1},{2,6},{6,2},{3,7},{7,3},{8,12},{12,8},{9,1... | collective-permute-start | bytes 1769480 | tf_op jit(solution)/shard_map/ppermute | solution.py:421
  40.3 23.0 %all-to-all-start.1 = ((bf16[16,128,128]{2,1,0:T(8,128)(2,1)}), bf16[16,128,128]{2,1,0:T(8,128)(2,1)S(1)}, u32[]{:S(2)}, u32[]{:S(2)}) async-start(bf16[16,128,128]{2,1,0:T(8,128)(2,1)} %get-tuple-element.59), calls=%async_computation.1 | async-start | bytes 1048576 | tf_op jit(solution)/shard_map/all_to_all | solution.py:425
  47.2 10.5 %collective-permute-start.4 = (bf16[1056,128]{1,0:T(8,128)(2,1)}, bf16[1056,128]{1,0:T(8,128)(2,1)S(1)}, u32[]{:S(2)}, u32[]{:S(2)}) collective-permute-start(bf16[1056,128]{1,0:T(8,128)(2,1)} %get-tuple-element.61), channel_id=1, source_target_pairs={{0,1},{1,2},{2,3},{3,0},{4,5},{5,6},{6,7},{7,4},{8,9},{9,10},{10,1... | collective-permute-start | bytes 811016 | tf_op jit(solution)/shard_map/ppermute | solution.py:421
  48.4 14.6 %collective-permute-start.5 = (bf16[1056,128]{1,0:T(8,128)(2,1)}, bf16[1056,128]{1,0:T(8,128)(2,1)S(1)}, u32[]{:S(2)}, u32[]{:S(2)}) collective-permute-start(bf16[1056,128]{1,0:T(8,128)(2,1)} %get-tuple-element.62), channel_id=1, source_target_pairs={{0,2},{1,3},{2,0},{3,1},{4,6},{5,7},{6,4},{7,5},{8,10},{9,11},{10,... | collective-permute-start | bytes 811016 | tf_op jit(solution)/shard_map/ppermute | solution.py:421
  50.8 12.5 %collective-permute-start.6 = (bf16[1056,128]{1,0:T(8,128)(2,1)}, bf16[1056,128]{1,0:T(8,128)(2,1)S(1)}, u32[]{:S(2)}, u32[]{:S(2)}) collective-permute-start(bf16[1056,128]{1,0:T(8,128)(2,1)} %get-tuple-element.63), channel_id=1, source_target_pairs={{0,3},{1,0},{2,1},{3,2},{4,7},{5,4},{6,5},{7,6},{8,11},{9,8},{10,9... | collective-permute-start | bytes 811016 | tf_op jit(solution)/shard_map/ppermute | solution.py:421
  63.4 1.9 copy-start.13
  63.4 1.9 collective-permute-start.7
  66.1 19.7 %copy-start.5 = (bf16[1056,128]{1,0:T(8,128)(2,1)S(1)}, bf16[1056,128]{1,0:T(8,128)(2,1)}, u32[]{:S(2)}) copy-start(bf16[1056,128]{1,0:T(8,128)(2,1)} %get-tuple-element.64.lab0.refs_1_.refs_4_) | copy-start | bytes 811012
  66.1 19.7 %copy-start.8 = (s32[1,4096]{1,0:T(1,128)S(1)}, s32[1,4096]{1,0:T(1,128)}, u32[]{:S(2)}) copy-start(s32[1,4096]{1,0:T(1,128)} %param.15) | copy-start | bytes 49156
  66.1 19.7 %copy-start.9 = (s32[1,4096]{1,0:T(1,128)S(1)}, s32[1,4096]{1,0:T(1,128)}, u32[]{:S(2)}) copy-start(s32[1,4096]{1,0:T(1,128)} %param.14) | copy-start | bytes 49156
  74.0 23.0 %all-to-all-start.2 = ((bf16[16,128,128]{2,1,0:T(8,128)(2,1)}), bf16[16,128,128]{2,1,0:T(8,128)(2,1)}, u32[]{:S(2)}, u32[]{:S(2)}) async-start(bf16[16,128,128]{2,1,0:T(8,128)(2,1)} %get-tuple-element.70), calls=%async_computation.2 | async-start | bytes 1048576 | tf_op jit(solution)/shard_map/all_to_all | solution.py:425
  80.9 9.8 %collective-permute-start.8 = (bf16[1024,128]{1,0:T(8,128)(2,1)}, bf16[1024,128]{1,0:T(8,128)(2,1)S(1)}, u32[]{:S(2)}, u32[]{:S(2)}) collective-permute-start(bf16[1024,128]{1,0:T(8,128)(2,1)} %get-tuple-element.72), channel_id=1, source_target_pairs={{0,1},{1,2},{2,3},{3,0},{4,5},{5,6},{6,7},{7,4},{8,9},{9,10},{10,1... | collective-permute-start | bytes 786440 | tf_op jit(solution)/shard_map/ppermute | solution.py:421
  82.5 14.5 %collective-permute-start.9 = (bf16[1024,128]{1,0:T(8,128)(2,1)}, bf16[1024,128]{1,0:T(8,128)(2,1)S(1)}, u32[]{:S(2)}, u32[]{:S(2)}) collective-permute-start(bf16[1024,128]{1,0:T(8,128)(2,1)} %get-tuple-element.73), channel_id=1, source_target_pairs={{0,2},{1,3},{2,0},{3,1},{4,6},{5,7},{6,4},{7,5},{8,10},{9,11},{10,... | collective-permute-start | bytes 786440 | tf_op jit(solution)/shard_map/ppermute | solution.py:421
  85.1 11.9 %collective-permute-start.10 = (bf16[1024,128]{1,0:T(8,128)(2,1)}, bf16[1024,128]{1,0:T(8,128)(2,1)S(1)}, u32[]{:S(2)}, u32[]{:S(2)}) collective-permute-start(bf16[1024,128]{1,0:T(8,128)(2,1)} %get-tuple-element.74), channel_id=1, source_target_pairs={{0,3},{1,0},{2,1},{3,2},{4,7},{5,4},{6,5},{7,6},{8,11},{9,8},{10,9... | collective-permute-start | bytes 786440 | tf_op jit(solution)/shard_map/ppermute | solution.py:421
  97.0 3.1 %collective-permute-start.11 = (bf16[16,128,128]{2,1,0:T(8,128)(2,1)}, bf16[16,128,128]{2,1,0:T(8,128)(2,1)}, u32[]{:S(2)}, u32[]{:S(2)}) collective-permute-start(bf16[16,128,128]{2,1,0:T(8,128)(2,1)} %all-to-all-done.2.near), channel_id=1, source_target_pairs={{0,4},{4,0},{1,5},{5,1},{2,6},{6,2},{3,7},{7,3},{8,12},{12,8},{9,1... | collective-permute-start | bytes 1572872 | tf_op jit(solution)/shard_map/ppermute | solution.py:421
  100.1 12.4 %copy-start.3 = (bf16[4,512,1024]{2,1,0:T(8,128)(2,1)S(1)}, bf16[4,512,1024]{2,1,0:T(8,128)(2,1)}, u32[]{:S(2)}) copy-start(bf16[4,512,1024]{2,1,0:T(8,128)(2,1)} %refs_6_.1) | copy-start | bytes 12582916
  100.1 12.4 %copy-start.6 = (bf16[1024,128]{1,0:T(8,128)(2,1)S(1)}, bf16[1024,128]{1,0:T(8,128)(2,1)}, u32[]{:S(2)}) copy-start(bf16[1024,128]{1,0:T(8,128)(2,1)} %get-tuple-element.75.refs_2_.refs_8_) | copy-start | bytes 786436
  107.9 10.2 %collective-permute-start.12 = (bf16[1024,128]{1,0:T(8,128)(2,1)}, bf16[1024,128]{1,0:T(8,128)(2,1)S(1)}, u32[]{:S(2)}, u32[]{:S(2)}) collective-permute-start(bf16[1024,128]{1,0:T(8,128)(2,1)} %get-tuple-element.82), channel_id=1, source_target_pairs={{0,1},{1,2},{2,3},{3,0},{4,5},{5,6},{6,7},{7,4},{8,9},{9,10},{10,1... | collective-permute-start | bytes 786440 | tf_op jit(solution)/shard_map/ppermute | solution.py:421
  109.3 15.1 %collective-permute-start.13 = (bf16[1024,128]{1,0:T(8,128)(2,1)}, bf16[1024,128]{1,0:T(8,128)(2,1)S(1)}, u32[]{:S(2)}, u32[]{:S(2)}) collective-permute-start(bf16[1024,128]{1,0:T(8,128)(2,1)} %get-tuple-element.83), channel_id=1, source_target_pairs={{0,2},{1,3},{2,0},{3,1},{4,6},{5,7},{6,4},{7,5},{8,10},{9,11},{10,... | collective-permute-start | bytes 786440 | tf_op jit(solution)/shard_map/ppermute | solution.py:421
  111.8 12.5 %copy-start.4 = (bf16[1024,1024]{1,0:T(8,128)(2,1)S(1)}, bf16[1024,1024]{1,0:T(8,128)(2,1)}, u32[]{:S(2)}) copy-start(bf16[1024,1024]{1,0:T(8,128)(2,1)} %refs_7_.1) | copy-start | bytes 6291460
  111.8 12.5 %copy-start.7 = (bf16[1024,128]{1,0:T(8,128)(2,1)S(1)}, bf16[1024,128]{1,0:T(8,128)(2,1)}, u32[]{:S(2)}) copy-start(bf16[1024,128]{1,0:T(8,128)(2,1)} %get-tuple-element.81.refs_0_.refs_12_) | copy-start | bytes 786436
  111.9 12.5 %copy-start.11 = (f32[1024,256]{1,0:T(8,128)S(1)}, f32[1024,256]{1,0:T(8,128)}, u32[]{:S(2)}) copy-start(f32[1024,256]{1,0:T(8,128)} %copy-done.10) | copy-start | bytes 3145732
  111.9 12.5 %collective-permute-start.14 = (bf16[1024,128]{1,0:T(8,128)(2,1)}, bf16[1024,128]{1,0:T(8,128)(2,1)S(1)}, u32[]{:S(2)}, u32[]{:S(2)}) collective-permute-start(bf16[1024,128]{1,0:T(8,128)(2,1)} %get-tuple-element.84), channel_id=1, source_target_pairs={{0,3},{1,0},{2,1},{3,2},{4,7},{5,4},{6,5},{7,6},{8,11},{9,8},{10,9... | collective-permute-start | bytes 786440 | tf_op jit(solution)/shard_map/ppermute | solution.py:421
  143.5 6.9 %collective-permute-start.15 = (bf16[4,4,4,16,1024]{4,3,2,1,0:T(8,128)(2,1)S(1)}, bf16[4,4,4,16,1024]{4,3,2,1,0:T(8,128)(2,1)S(1)}, u32[]{:S(2)}, u32[]{:S(2)}) collective-permute-start(bf16[4,4,4,16,1024]{4,3,2,1,0:T(8,128)(2,1)S(1)} %get-tuple-element.88), channel_id=1, source_target_pairs={{0,4},{4,0},{1,5},{5,1},{2,6},{6,2},{3,7},{7,3},{8,12},{12,8},{9,1... | collective-permute-start | bytes 6291464 | tf_op jit(solution)/shard_map/ppermute | solution.py:421
  147.2 3.2 %collective-permute-start.16 = (bf16[4,4,4,16,640]{4,3,2,1,0:T(8,128)(2,1)S(1)}, bf16[4,4,4,16,640]{4,3,2,1,0:T(8,128)(2,1)S(1)}, u32[]{:S(2)}, u32[]{:S(2)}) collective-permute-start(bf16[4,4,4,16,640]{4,3,2,1,0:T(8,128)(2,1)S(1)} %get-tuple-element.94), channel_id=1, source_target_pairs={{0,4},{4,0},{1,5},{5,1},{2,6},{6,2},{3,7},{7,3},{8,12},{12,8},{9,1... | collective-permute-start | bytes 3932168 | tf_op jit(solution)/shard_map/ppermute | solution.py:421
  (5 other events, 4.5 us)

commit v4 on v3

--- a/solution.py
+++ b/solution.py
@@ -310,29 +310,30 @@
 
 
 WIDE = (HID + CP) // 2
+SIDE = 16
 
 
 def outer_kernel(pos, act1, act2, gl, gm, keep, send):
     own = pos[1] == 0
     width = HID // Y
-    for y in range(Y):
-        cut = slice(y * width, (y + 1) * width)
-        mid = dot(act1[:, cut], gm[...], 0, 0)
-        out = dot(act2[:, cut], gl[...], 0, 0)
+    for k in range(Y):
+        at = pl.multiple_of(lax.rem(pos[3] + k, Y) * width, width)
+        mid = dot(act1[:, pl.ds(at, width)], gm[...], 0, 0)
+        out = dot(act2[:, pl.ds(at, width)], gl[...], 0, 0)
         both = jnp.concatenate([mid, out], axis=1).reshape(X, CORE, REP, 8, HID + CP)
         both = jnp.concatenate([both[..., :WIDE], both[..., WIDE:]], axis=3)
         zero, one = both[:, 0], both[:, 1]
-        keep[y] = jnp.where(own, zero, one).astype(BF)
-        send[y] = jnp.where(own, one, zero).astype(BF)
+        shape = (SIDE, 16, WIDE)
+        keep[k] = jnp.where(own, zero, one).astype(BF).reshape(shape)
+        send[k] = jnp.where(own, one, zero).astype(BF).reshape(shape)
 
 
 def outer_grads(pos, act1, act2, gl, gm):
-    shape = (Y, X, REP, 16, WIDE)
     return pl.pallas_call(
         outer_kernel,
         in_specs=[whole(pltpu.SMEM)] + [whole()] * 4,
         out_specs=[whole()] * 2,
-        out_shape=[struct(shape)] * 2,
+        out_shape=[struct((Y, SIDE, 16, WIDE))] * 2,
         compiler_params=params(30),
         name="outer_grads",
         cost_estimate=pl.CostEstimate(
@@ -344,28 +345,24 @@
 def first_kernel(pos, *refs):
     pieces, (gf, keep, send) = refs[:16], refs[16:]
     own = pos[1] == 0
-    for d in range(REP):
-        slab = lax.rem(pos[0] + REP - d, REP)
+    for k in range(REP):
+        d = (REP - k) % REP
         for y in range(0, Y, 2):
             two = [pieces[4 * u + d][:ROWS] for u in (y, y + 1)]
             x = jnp.concatenate(two, axis=1)
-            got = dot(x, gf[...], 0, 0).reshape(2, X, CORE, 16, HID)
-            zero, one = got[:, :, 0], got[:, :, 1]
-            kept = jnp.where(own, zero, one).astype(BF)
-            sent = jnp.where(own, one, zero).astype(BF)
-            for u in range(2):
-                for v in range(X):
-                    keep[y + u, v, slab] = kept[u, v]
-                    send[y + u, v, slab] = sent[u, v]
+            got = dot(x, gf[...], 0, 0).reshape(2 * X, CORE, 16, HID)
+            zero, one = got[:, 0], got[:, 1]
+            here = slice(y * X, (y + 2) * X)
+            keep[k, here] = jnp.where(own, zero, one).astype(BF)
+            send[k, here] = jnp.where(own, one, zero).astype(BF)
 
 
 def first_grads(pos, pieces, gf):
-    shape = (Y, X, REP, 16, HID)
     return pl.pallas_call(
         first_kernel,
         in_specs=[whole(pltpu.SMEM)] + [whole()] * 17,
         out_specs=[whole()] * 2,
-        out_shape=[struct(shape)] * 2,
+        out_shape=[struct((REP, SIDE, 16, HID))] * 2,
         compiler_params=params(36),
         name="first_grads",
         cost_estimate=pl.CostEstimate(
@@ -374,46 +371,75 @@
     )(pos, *pieces, gf)
 
 
-def join_kernel(keep_f, got_f, keep_m, got_m, out):
-    out[:, :, :HID] = (keep_f[...].astype(F32) + got_f[...].astype(F32)).astype(BF)
-    out[:, :, HID:] = (keep_m[...].astype(F32) + got_m[...].astype(F32)).astype(BF)
-
-
-def join_cores(keep_f, got_f, keep_m, got_m):
-    n = Y * X * REP
-    flat = [v.reshape(n, 16, v.shape[-1]) for v in (keep_f, got_f, keep_m, got_m)]
-
-    def spec(width):
-        return pl.BlockSpec((8, 16, width), lambda i: (i, 0, 0))
-
-    return pl.pallas_call(
-        join_kernel,
-        grid=(n // 8,),
-        in_specs=[spec(v.shape[-1]) for v in flat],
-        out_specs=spec(HID + WIDE),
-        out_shape=struct((n, 16, HID + WIDE)),
-        compiler_params=params(8),
-        name="join_cores",
-    )(*flat)
-
-
-def total_kernel(parts, first, mid, out):
-    total = jnp.sum(parts[...].astype(F32), axis=0)
-    first[0] = total[:, :HID]
-    rest = jnp.concatenate([total[:8, HID:], total[8:, HID:]], axis=1)
+def plus(*values):
+    return sum(v.astype(F32) for v in values)
+
+
+def cores_kernel(keep, got, p0, p1, p3, ahead, behind):
+    half = SIDE // 2
+    p0[...] = plus(keep[0], got[0]).astype(BF)
+    p1[...] = plus(keep[1], got[1]).astype(BF)
+    p3[...] = plus(keep[3], got[3]).astype(BF)
+    ahead[...] = plus(keep[2, :half], got[2, :half]).astype(BF)
+    behind[...] = plus(keep[2, half:], got[2, half:]).astype(BF)
+
+
+def near_kernel(p1, p3, ahead, behind, q1, q3):
+    half = SIDE // 2
+    q1[:half] = plus(p1[:half], ahead[...]).astype(BF)
+    q1[half:] = p1[half:]
+    q3[:half] = p3[:half]
+    q3[half:] = plus(p3[half:], behind[...]).astype(BF)
+
+
+def own_kernel(p0, r1, r3, out):
+    out[...] = plus(p0[...], r1[...], r3[...]).astype(BF)
+
+
+def small(kernel, outs, name, *args):
+    moved = sum(a.size for a in args) * 2
+    return pl.pallas_call(
+        kernel,
+        in_specs=[whole()] * len(args),
+        out_specs=[whole()] * len(outs),
+        out_shape=[struct(s) for s in outs],
+        compiler_params=params(14),
+        name=name,
+        cost_estimate=pl.CostEstimate(
+            flops=moved, bytes_accessed=2 * moved, transcendentals=0
+        ),
+    )(*args)
+
+
+def reduce_ring(keep, send, axis, tag):
+    full = keep.shape[1:]
+    half = (SIDE // 2,) + full[1:]
+    got = shift(send, "core", 1)
+    outs = [full, full, full, half, half]
+    p0, p1, p3, ahead, behind = small(cores_kernel, outs, "cores_" + tag, keep, got)
+    ahead, behind = shift(ahead, axis, 1), shift(behind, axis, 3)
+    q1, q3 = small(near_kernel, [full, full], "near_" + tag, p1, p3, ahead, behind)
+    r1, r3 = shift(q1, axis, 1), shift(q3, axis, 3)
+    return small(own_kernel, [full], "own_" + tag, p0, r1, r3)[0]
+
+
+def total_kernel(part_f, part_m, first, mid, out):
+    first[0] = jnp.sum(part_f[...].astype(F32), axis=0)
+    total = jnp.sum(part_m[...].astype(F32), axis=0)
+    rest = jnp.concatenate([total[:8], total[8:]], axis=1)
     mid[...] = rest[:, :HID]
     out[...] = rest[:, HID : HID + C]
 
 
-def total_grads(parts):
+def total_grads(part_f, part_m):
     return pl.pallas_call(
         total_kernel,
-        in_specs=[whole()],
+        in_specs=[whole()] * 2,
         out_specs=[whole()] * 3,
         out_shape=[struct((1, 16, HID), F32), struct((8, HID), F32), struct((8, C), F32)],
-        compiler_params=params(16),
+        compiler_params=params(12),
         name="total_grads",
-    )(parts)
+    )(part_f, part_m)
 
 
 def shift(value, axis, by):
@@ -421,8 +447,8 @@
     return lax.ppermute(value, axis, [(i, (i + by) % size) for i in range(size)])
 
 
-def spread(export):
-    return lax.all_to_all(export, ("y", "x"), split_axis=0, concat_axis=0, tiled=True)
+def swap(value, axes):
+    return lax.all_to_all(value, axes, split_axis=0, concat_axis=0, tiled=True)
 
 
 def exchange(quarters):
@@ -442,7 +468,7 @@
     out_weight,
 ):
     y, x, core, rep = (lax.axis_index(a) for a in ("y", "x", "core", "rep"))
-    pos = jnp.stack([rep, core, lax.rem(rep + REP - y, REP)]).astype(jnp.int32)
+    pos = jnp.stack([rep, core, lax.rem(rep + REP - y, REP), y]).astype(jnp.int32)
 
     part = tile_columns - NB
     halo_at = NB + (part + core) % CORE * (NB // CORE) + part // CORE
@@ -459,7 +485,7 @@
             counts = count_labels(
                 pos, pieces[1], shuffle.reshape(DOM, TILE), train_rows.reshape(DOM, TILE)
             )
-        near, got, counts = lax.optimization_barrier((spread(export), got, counts))
+        near, got, counts = lax.optimization_barrier((swap(export, ("y", "x")), got, counts))
         far = shift(near, "core", 1)
         pieces.append(got)
         made = propagate(h, cols, tile_values, hop, near, far, brow)
@@ -474,13 +500,13 @@
         pos, pieces[3], early, counts, first_weight, mid_weight, w3
     )
     pieces = [v for got in pieces for v in got]
-    keep_f, send_f = first_grads(pos, pieces, gf)
-    got_f = shift(send_f, "core", 1)
     keep_m, send_m = outer_grads(pos, act1, act2, gl, gm)
-    got_m = shift(send_m, "core", 1)
-    parts = join_cores(keep_f, got_f, keep_m, got_m)
-    parts = lax.all_to_all(parts, ("y", "x", "rep"), split_axis=0, concat_axis=0, tiled=True)
-    first, mid, out = total_grads(parts)
+    keep_m, send_m, gf = lax.optimization_barrier((keep_m, send_m, gf))
+    part_m = reduce_ring(keep_m, send_m, "y", "middle")
+    part_m = swap(part_m, ("x", "rep"))
+    part_f = reduce_ring(*first_grads(pos, pieces, gf), "rep", "first")
+    part_f = swap(part_f, ("y", "x"))
+    first, mid, out = total_grads(part_f, part_m)
     return first, mid, out
 
 

time: 207 us -> 204 us (0.986)
  blocking collectives: 54 us -> 15 us
  starting transfers between devices: 42.6 us -> 62.2 us
  waiting for transfers between devices: 39.9 us -> 55.8 us
    all_to_all x1, blocking collectives: 54 us -> 15 us  [swap(): return lax.all_to_all(value, axes, split_axis=0, concat_axis=0, tiled=True)]
    ppermute x17 -> x25, starting transfers between devices: 21.6 us -> 34.8 us  [shift(): lax.ppermute(value, axis, [(i, (i + by) % size) for i in range(size)])]
    ppermute x17 -> x25, waiting for transfers between devices: 39.8 us -> 49.4 us  [shift(): lax.ppermute(value, axis, [(i, (i + by) % size) for i in range(size)])]
    all_to_all x3 -> x4, starting transfers between devices: 20.9 us -> 27.4 us  [swap(): return lax.all_to_all(value, axes, split_axis=0, concat_axis=0, tiled=True)]
    all_to_all x3 -> x4, waiting for transfers between devices: 0.01 us -> 6.41 us  [swap(): return lax.all_to_all(value, axes, split_axis=0, concat_axis=0, tiled=True)]
  transfers between devices with their start and end apart: 20 -> 29, of which waited for: 11 -> 19; matrix products, arithmetic and copies ran while one was open for 2% -> 1% of each run, Pallas kernels for 6% -> 6%
where the time goes in v4:
time: 204 us; the launch traced here: 203 us
  starting transfers between devices  62.2 us (30%)
  Pallas kernels  61.5 us (30%)
  waiting for transfers between devices  55.8 us (27%)
  blocking collectives  15 us (7%)
  local copies, waits for them, and re-layouts  6.76 us (3%)
    ppermute x25, waiting for transfers between devices, shift(): lax.ppermute(value, axis, [(i, (i + by) % size) for i in range(size)])  49.4 us
    ppermute x25, starting transfers between devices, shift(): lax.ppermute(value, axis, [(i, (i + by) % size) for i in range(size)])  34.8 us
    all_to_all x4, starting transfers between devices, swap(): return lax.all_to_all(value, axes, split_axis=0, concat_axis=0, tiled=True)  27.4 us
    pallas_call x3, Pallas kernels, propagate(): pl.pallas_call(functools.partial(prop_kernel, h), in_specs=[whole(pltpu.S...  24 us
    all_to_all x1, blocking collectives, swap(): return lax.all_to_all(value, axes, split_axis=0, concat_axis=0, tiled=True)  15 us
    pallas_call x1, Pallas kernels, mlp(): pl.pallas_call(mlp_kernel, grid_spec=pltpu.PrefetchScalarGridSpec(num_sca...  14.6 us
    all_to_all x4, waiting for transfers between devices, swap(): return lax.all_to_all(value, axes, split_axis=0, concat_axis=0, tiled=True)  6.41 us
    unnamed x35, local copies, waits for them, and re-layouts  5.75 us
  transfers between devices with their start and end apart: 29, of which 19 were waited for; matrix products, arithmetic and copies ran while one was open for 1% of the time, Pallas kernels for 6%

profile of v4, /device:TPU:0, one launch (start us, length us, event | category | flops | bytes accessed | tf_op | source)
XLA Modules:
  0.0 203.0 jit_solution(10105824640444402350)
XLA Ops:
  3.4 1.9 export_first.1
  5.3 7.1 %all-to-all-start = ((bf16[16,144,128]{2,1,0:T(8,128)(2,1)}), bf16[16,144,128]{2,1,0:T(8,128)(2,1)S(1)}, u32[]{:S(2)}, u32[]{:S(2)}) async-start(bf16[16,144,128]{2,1,0:T(8,128)(2,1)} %get-tuple-element.66), calls=%async_computation | async-start | bytes 1179648 | tf_op jit(solution)/shard_map/all_to_all | solution.py:451
  12.4 2.0 collective-permute-start
  14.4 3.6 %collective-permute-start.1 = (bf16[1024,128]{1,0:T(8,128)(2,1)S(1)}, bf16[1024,128]{1,0:T(8,128)(2,1)S(1)}, u32[]{:S(2)}, u32[]{:S(2)}) collective-permute-start(bf16[1024,128]{1,0:T(8,128)(2,1)S(1)} %get-tuple-element.69), channel_id=1, source_target_pairs={{0,2},{1,3},{2,0},{3,1},{4,6},{5,7},{6,4},{7,5},{8,10},{9,11},{10,... | collective-permute-start | bytes 786440 | tf_op jit(solution)/shard_map/ppermute | solution.py:447
  19.0 3.8 %collective-permute-done.refs_3_.refs_1_ = bf16[1024,128]{1,0:T(8,128)(2,1)S(1)} collective-permute-done((bf16[1024,128]{1,0:T(8,128)(2,1)S(1)}, bf16[1024,128]{1,0:T(8,128)(2,1)S(1)}, u32[]{:S(2)}, u32[]{:S(2)}) %collective-permute-start) | collective-permute-done | bytes 262176 | tf_op jit(solution)/shard_map/ppermute | solution.py:447
  22.8 6.5 %collective-permute-done.1.refs_6_.refs_2_ = bf16[1024,128]{1,0:T(8,128)(2,1)S(1)} collective-permute-done((bf16[1024,128]{1,0:T(8,128)(2,1)S(1)}, bf16[1024,128]{1,0:T(8,128)(2,1)S(1)}, u32[]{:S(2)}, u32[]{:S(2)}) %collective-permute-start.1) | collective-permute-done | bytes 262176 | tf_op jit(solution)/shard_map/ppermute | solution.py:447
  32.3 8.2 %propagate_0.1 = (bf16[4096,128]{1,0:T(8,128)(2,1)}, bf16[16,128,128]{2,1,0:T(8,128)(2,1)}, bf16[1056,128]{1,0:T(8,128)(2,1)}, bf16[1056,128]{1,0:T(8,128)(2,1)}...) custom-call(s32[259]{0:T(512)} %pad_add_fusion.cols, bf16[32,8,128,128]{3,2,1,0:T(8,128)(2,1)} %tiles.5, ...), custom_call_target="tpu_custom_call" | custom-call | flops 1073741824 | bytes 12582912 | tf_op jit(solution)/shard_map/propagate_0/pallas_call | solution.py:159
  40.5 6.9 %all-to-all-start.1 = ((bf16[16,128,128]{2,1,0:T(8,128)(2,1)}), bf16[16,128,128]{2,1,0:T(8,128)(2,1)S(1)}, u32[]{:S(2)}, u32[]{:S(2)}) async-start(bf16[16,128,128]{2,1,0:T(8,128)(2,1)} %get-tuple-element.76), calls=%async_computation.1 | async-start | bytes 1048576 | tf_op jit(solution)/shard_map/all_to_all | solution.py:451
  48.6 2.4 %collective-permute-start.5 = (bf16[1056,128]{1,0:T(8,128)(2,1)}, bf16[1056,128]{1,0:T(8,128)(2,1)S(1)}, u32[]{:S(2)}, u32[]{:S(2)}) collective-permute-start(bf16[1056,128]{1,0:T(8,128)(2,1)} %get-tuple-element.79), channel_id=1, source_target_pairs={{0,2},{1,3},{2,0},{3,1},{4,6},{5,7},{6,4},{7,5},{8,10},{9,11},{10,... | collective-permute-start | bytes 811016 | tf_op jit(solution)/shard_map/ppermute | solution.py:447
  52.2 5.7 %collective-permute-done.4.lab1.refs_4_.refs_5_ = bf16[1056,128]{1,0:T(8,128)(2,1)S(1)} collective-permute-done((bf16[1056,128]{1,0:T(8,128)(2,1)}, bf16[1056,128]{1,0:T(8,128)(2,1)S(1)}, u32[]{:S(2)}, u32[]{:S(2)}) %collective-permute-start.4) | collective-permute-done | bytes 270368 | tf_op jit(solution)/shard_map/ppermute | solution.py:447
  57.9 5.3 %collective-permute-done.5.lab2.refs_7_.refs_6_ = bf16[1056,128]{1,0:T(8,128)(2,1)S(1)} collective-permute-done((bf16[1056,128]{1,0:T(8,128)(2,1)}, bf16[1056,128]{1,0:T(8,128)(2,1)S(1)}, u32[]{:S(2)}, u32[]{:S(2)}) %collective-permute-start.5) | collective-permute-done | bytes 270368 | tf_op jit(solution)/shard_map/ppermute | solution.py:447
  63.5 1.9 collective-permute-done.7.far
  66.2 8.0 %propagate_1.1 = (bf16[4096,128]{1,0:T(8,128)(2,1)}, bf16[16,128,128]{2,1,0:T(8,128)(2,1)}, bf16[1024,128]{1,0:T(8,128)(2,1)}, bf16[1024,128]{1,0:T(8,128)(2,1)}...) custom-call(s32[259]{0:T(512)} %pad_add_fusion.cols, bf16[32,8,128,128]{3,2,1,0:T(8,128)(2,1)} %tiles.5, ...), custom_call_target="tpu_custom_call" | custom-call | flops 1073741824 | bytes 12582912 | tf_op jit(solution)/shard_map/propagate_1/pallas_call | solution.py:159
  74.2 6.9 %all-to-all-start.2 = ((bf16[16,128,128]{2,1,0:T(8,128)(2,1)}), bf16[16,128,128]{2,1,0:T(8,128)(2,1)}, u32[]{:S(2)}, u32[]{:S(2)}) async-start(bf16[16,128,128]{2,1,0:T(8,128)(2,1)} %get-tuple-element.87), calls=%async_computation.2 | async-start | bytes 1048576 | tf_op jit(solution)/shard_map/all_to_all | solution.py:451
  82.7 2.6 %collective-permute-start.9 = (bf16[1024,128]{1,0:T(8,128)(2,1)}, bf16[1024,128]{1,0:T(8,128)(2,1)S(1)}, u32[]{:S(2)}, u32[]{:S(2)}) collective-permute-start(bf16[1024,128]{1,0:T(8,128)(2,1)} %get-tuple-element.90), channel_id=1, source_target_pairs={{0,2},{1,3},{2,0},{3,1},{4,6},{5,7},{6,4},{7,5},{8,10},{9,11},{10,... | collective-permute-start | bytes 786440 | tf_op jit(solution)/shard_map/ppermute | solution.py:447
  86.0 3.8 %count_labels.1.refs_5_ = f32[1024,256]{1,0:T(8,128)S(1)} custom-call(s32[4]{0:T(128)S(1)} %pad_add_fusion.1.pos, bf16[1056,128]{1,0:T(8,128)(2,1)S(1)} %copy-done.5, bf16[1056,128]{1,0:T(8,128)(2,1)S(1)} %collective-permute-done.4.lab1.refs_4_.refs_5_, bf16[1056,128]{1,0:T(8,128)(2,1)S(1)} %collective-permute-done.5.lab2.refs_7_.refs_6_, ...), custom_call_target="tpu_custom_call" | custom-call | flops 2147483648 | bytes 2097152 | tf_op jit(solution)/shard_map/count_labels/pallas_call | solution.py:206
  91.0 6.2 %collective-permute-done.9.refs_8_.refs_10_ = bf16[1024,128]{1,0:T(8,128)(2,1)S(1)} collective-permute-done((bf16[1024,128]{1,0:T(8,128)(2,1)}, bf16[1024,128]{1,0:T(8,128)(2,1)S(1)}, u32[]{:S(2)}, u32[]{:S(2)}) %collective-permute-start.9) | collective-permute-done | bytes 262176 | tf_op jit(solution)/shard_map/ppermute | solution.py:447
  99.5 7.9 %propagate_2.1 = (bf16[1024,128]{1,0:T(8,128)(2,1)}, bf16[1024,128]{1,0:T(8,128)(2,1)}, bf16[1024,128]{1,0:T(8,128)(2,1)}, bf16[1024,128]{1,0:T(8,128)(2,1)}) custom-call(s32[259]{0:T(512)} %pad_add_fusion.cols, bf16[32,8,128,128]{3,2,1,0:T(8,128)(2,1)} %tiles.5, bf16[4096,128]{1,0:T(8,128)(2,1)} %get-tuple-element.96.hop, ...), custom_call_target="tpu_custom_call" | custom-call | flops 1073741824 | bytes 12582912 | tf_op jit(solution)/shard_map/propagate_2/pallas_call | solution.py:159
  108.7 2.6 %collective-permute-start.13 = (bf16[1024,128]{1,0:T(8,128)(2,1)}, bf16[1024,128]{1,0:T(8,128)(2,1)S(1)}, u32[]{:S(2)}, u32[]{:S(2)}) collective-permute-start(bf16[1024,128]{1,0:T(8,128)(2,1)} %get-tuple-element.100), channel_id=1, source_target_pairs={{0,2},{1,3},{2,0},{3,1},{4,6},{5,7},{6,4},{7,5},{8,10},{9,11},{10,... | collective-permute-start | bytes 786440 | tf_op jit(solution)/shard_map/ppermute | solution.py:447
  112.0 5.6 %first_layer_early.1.refs_4_ = f32[1024,1024]{1,0:T(8,128)S(1)} custom-call(s32[4]{0:T(128)S(1)} %pad_add_fusion.1.pos, bf16[1024,128]{1,0:T(8,128)(2,1)S(1)} %get-tuple-element.71.refs_0_, bf16[1056,128]{1,0:T(8,128)(2,1)S(1)} %copy-done.5, bf16[1024,128]{1,0:T(8,128)(2,1)S(1)} %copy-done.6, bf16[1024,128]{1,0:T(8,128)(2,1)S(1)} %collective-permute-done.refs_3_.refs_1_, ...), custom_call_target="tpu_custom_call" | custom-call | flops 3221225472 | bytes 11534336 | tf_op jit(solution)/shard_map/first_layer_early/pallas_call | solution.py:272
  117.6 5.8 %collective-permute-done.13.refs_2_.refs_14_ = bf16[1024,128]{1,0:T(8,128)(2,1)S(1)} collective-permute-done((bf16[1024,128]{1,0:T(8,128)(2,1)}, bf16[1024,128]{1,0:T(8,128)(2,1)S(1)}, u32[]{:S(2)}, u32[]{:S(2)}) %collective-permute-start.13) | collective-permute-done | bytes 262176 | tf_op jit(solution)/shard_map/ppermute | solution.py:447
  123.4 14.6 %mlp.1 = (bf16[1024,1024]{1,0:T(8,128)(2,1)S(1)}, bf16[1024,1024]{1,0:T(8,128)(2,1)S(1)}, bf16[1024,256]{1,0:T(8,128)(2,1)S(1)}, bf16[1024,1024]{1,0:T(8,128)(2,1)S(1)}, bf16[1024,1024]{1,0:T(8,128)(2,1)S(1)}) custom-call(s32[4]{0:T(128)S(1)} %pad_add_fusion.1.pos, bf16[1024,128]{1,0:T(8,128)(2,1)S(1)} %copy-done.7, ...), custom_call_target="tpu_custom_call" | custom-call | flops 6442450944 | bytes 20971520 | tf_op jit(solution)/shard_map/mlp/pallas_call | solution.py:291
  138.0 3.6 %outer_grads.1 = (bf16[4,16,16,640]{3,2,1,0:T(8,128)(2,1)S(1)}, bf16[4,16,16,640]{3,2,1,0:T(8,128)(2,1)S(1)}) custom-call(s32[4]{0:T(128)S(1)} %pad_add_fusion.1.pos, bf16[1024,1024]{1,0:T(8,128)(2,1)S(1)} %get-tuple-element.103.act1, bf16[1024,1024]{1,0:T(8,128)(2,1)S(1)} %get-tuple-element.104.act2, bf16[1024,256]{1,0:T(8,128)(2,1)S(1)} %get-tuple-element.105.gl, ...), custom_call_target="tpu_custom_call" | custom-call | flops 2684354560 | bytes 8388608 | tf_op jit(solution)/shard_map/outer_grads/pallas_call | solution.py:332
  141.7 5.2 %first_grads.1 = (bf16[4,16,16,1024]{3,2,1,0:T(8,128)(2,1)S(1)}, bf16[4,16,16,1024]{3,2,1,0:T(8,128)(2,1)S(1)}) custom-call(s32[4]{0:T(128)S(1)} %pad_add_fusion.1.pos, bf16[1024,128]{1,0:T(8,128)(2,1)S(1)} %get-tuple-element.71.refs_0_, bf16[1024,128]{1,0:T(8,128)(2,1)S(1)} %collective-permute-done.refs_3_.refs_1_, ...), custom_call_target="tpu_custom_call" | custom-call | flops 4294967296 | bytes 10485760 | tf_op jit(solution)/shard_map/first_grads/pallas_call | solution.py:361
  147.4 5.5 %collective-permute-done.20.got = bf16[4,16,16,640]{3,2,1,0:T(8,128)(2,1)S(1)} collective-permute-done((bf16[4,16,16,640]{3,2,1,0:T(8,128)(2,1)S(1)}, bf16[4,16,16,640]{3,2,1,0:T(8,128)(2,1)S(1)}, u32[]{:S(2)}, u32[]{:S(2)}) %collective-permute-start.20) | collective-permute-done | bytes 1310752 | tf_op jit(solution)/shard_map/ppermute | solution.py:447
  158.4 2.0 collective-permute-start.17
  164.2 2.0 collective-permute-done.16.ahead
  167.3 2.4 %collective-permute-start.19 = (bf16[16,16,1024]{2,1,0:T(8,128)(2,1)S(1)}, bf16[16,16,1024]{2,1,0:T(8,128)(2,1)S(1)}, u32[]{:S(2)}, u32[]{:S(2)}) collective-permute-start(bf16[16,16,1024]{2,1,0:T(8,128)(2,1)S(1)} %get-tuple-element.119), channel_id=1, source_target_pairs={{0,3},{1,0},{2,1},{3,2},{4,7},{5,4},{6,5},{7,6},{8,11},{9,8},{10,9... | collective-permute-start | bytes 1572872 | tf_op jit(solution)/shard_map/ppermute | solution.py:447
  171.9 6.5 %all-to-all-start.4 = ((bf16[16,16,640]{2,1,0:T(8,128)(2,1)}), bf16[16,16,640]{2,1,0:T(8,128)(2,1)S(1)}, u32[]{:S(2)}, u32[]{:S(2)}) async-start(bf16[16,16,640]{2,1,0:T(8,128)(2,1)} %own_middle.1), calls=%async_computation.4 | async-start | bytes 655360 | tf_op jit(solution)/shard_map/all_to_all | solution.py:451
  178.4 1.9 collective-permute-done.18.r1
  180.8 6.4 %all-to-all-done.4.part_m = bf16[16,16,640]{2,1,0:T(8,128)(2,1)S(1)} async-done(((bf16[16,16,640]{2,1,0:T(8,128)(2,1)}), bf16[16,16,640]{2,1,0:T(8,128)(2,1)S(1)}, u32[]{:S(2)}, u32[]{:S(2)}) %all-to-all-start.4) | async-done | bytes 327712 | tf_op jit(solution)/shard_map/all_to_all | solution.py:451
  187.2 15.0 %all_to_all.25.part_f = bf16[16,16,1024]{2,1,0:T(8,128)(2,1)S(1)} all-to-all(bf16[16,16,1024]{2,1,0:T(8,128)(2,1)S(1)} %own_first.1), channel_id=1, replica_groups=mesh['y'=4,'x'=4,'core'=2,'rep'=4] {'y','x'}, dimensions={0} | all-to-all | bytes 1048576 | tf_op jit(solution)/shard_map/all_to_all | solution.py:451
  (85 shorter events, 32.3 us)
Async XLA Ops:
  0.6 28.8 %copy-start.16 = (s32[32,8]{0,1:T(8,128)S(1)}, s32[32,8]{0,1:T(8,128)}, u32[]{:S(2)}) copy-start(s32[32,8]{0,1:T(8,128)} %param.12) | copy-start | bytes 3076
  1.4 30.0 %copy-start.1 = (s32[128,1]{1,0:T(8,128)}, s32[128,1]{1,0:T(8,128)S(1)}, u32[]{:S(2)}) copy-start(s32[128,1]{1,0:T(8,128)S(1)} %copy.18.brow) | copy-start | bytes 1540
  5.3 24.1 %all-to-all-start = ((bf16[16,144,128]{2,1,0:T(8,128)(2,1)}), bf16[16,144,128]{2,1,0:T(8,128)(2,1)S(1)}, u32[]{:S(2)}, u32[]{:S(2)}) async-start(bf16[16,144,128]{2,1,0:T(8,128)(2,1)} %get-tuple-element.66), calls=%async_computation | async-start | bytes 1179648 | tf_op jit(solution)/shard_map/all_to_all | solution.py:451
  12.4 10.4 %collective-permute-start = (bf16[1024,128]{1,0:T(8,128)(2,1)S(1)}, bf16[1024,128]{1,0:T(8,128)(2,1)S(1)}, u32[]{:S(2)}, u32[]{:S(2)}) collective-permute-start(bf16[1024,128]{1,0:T(8,128)(2,1)S(1)} %get-tuple-element.68), channel_id=1, source_target_pairs={{0,1},{1,2},{2,3},{3,0},{4,5},{5,6},{6,7},{7,4},{8,9},{9,10},{10,1... | collective-permute-start | bytes 786440 | tf_op jit(solution)/shard_map/ppermute | solution.py:447
  14.4 14.9 %collective-permute-start.1 = (bf16[1024,128]{1,0:T(8,128)(2,1)S(1)}, bf16[1024,128]{1,0:T(8,128)(2,1)S(1)}, u32[]{:S(2)}, u32[]{:S(2)}) collective-permute-start(bf16[1024,128]{1,0:T(8,128)(2,1)S(1)} %get-tuple-element.69), channel_id=1, source_target_pairs={{0,2},{1,3},{2,0},{3,1},{4,6},{5,7},{6,4},{7,5},{8,10},{9,11},{10,... | collective-permute-start | bytes 786440 | tf_op jit(solution)/shard_map/ppermute | solution.py:447
  18.0 11.4 %collective-permute-start.2 = (bf16[1024,128]{1,0:T(8,128)(2,1)S(1)}, bf16[1024,128]{1,0:T(8,128)(2,1)S(1)}, u32[]{:S(2)}, u32[]{:S(2)}) collective-permute-start(bf16[1024,128]{1,0:T(8,128)(2,1)S(1)} %get-tuple-element.70), channel_id=1, source_target_pairs={{0,3},{1,0},{2,1},{3,2},{4,7},{5,4},{6,5},{7,6},{8,11},{9,8},{10,9... | collective-permute-start | bytes 786440 | tf_op jit(solution)/shard_map/ppermute | solution.py:447
  29.4 2.1 %collective-permute-start.3 = (bf16[16,144,128]{2,1,0:T(8,128)(2,1)S(1)}, bf16[16,144,128]{2,1,0:T(8,128)(2,1)S(1)}, u32[]{:S(2)}, u32[]{:S(2)}) collective-permute-start(bf16[16,144,128]{2,1,0:T(8,128)(2,1)S(1)} %all-to-all-done.near), channel_id=1, source_target_pairs={{0,4},{4,0},{1,5},{5,1},{2,6},{6,2},{3,7},{7,3},{8,12},{12,8},{9,1... | collective-permute-start | bytes 1769480 | tf_op jit(solution)/shard_map/ppermute | solution.py:447
  40.5 23.0 %all-to-all-start.1 = ((bf16[16,128,128]{2,1,0:T(8,128)(2,1)}), bf16[16,128,128]{2,1,0:T(8,128)(2,1)S(1)}, u32[]{:S(2)}, u32[]{:S(2)}) async-start(bf16[16,128,128]{2,1,0:T(8,128)(2,1)} %get-tuple-element.76), calls=%async_computation.1 | async-start | bytes 1048576 | tf_op jit(solution)/shard_map/all_to_all | solution.py:451
  47.4 10.5 %collective-permute-start.4 = (bf16[1056,128]{1,0:T(8,128)(2,1)}, bf16[1056,128]{1,0:T(8,128)(2,1)S(1)}, u32[]{:S(2)}, u32[]{:S(2)}) collective-permute-start(bf16[1056,128]{1,0:T(8,128)(2,1)} %get-tuple-element.78), channel_id=1, source_target_pairs={{0,1},{1,2},{2,3},{3,0},{4,5},{5,6},{6,7},{7,4},{8,9},{9,10},{10,1... | collective-permute-start | bytes 811016 | tf_op jit(solution)/shard_map/ppermute | solution.py:447
  48.6 14.6 %collective-permute-start.5 = (bf16[1056,128]{1,0:T(8,128)(2,1)}, bf16[1056,128]{1,0:T(8,128)(2,1)S(1)}, u32[]{:S(2)}, u32[]{:S(2)}) collective-permute-start(bf16[1056,128]{1,0:T(8,128)(2,1)} %get-tuple-element.79), channel_id=1, source_target_pairs={{0,2},{1,3},{2,0},{3,1},{4,6},{5,7},{6,4},{7,5},{8,10},{9,11},{10,... | collective-permute-start | bytes 811016 | tf_op jit(solution)/shard_map/ppermute | solution.py:447
  51.0 12.5 %collective-permute-start.6 = (bf16[1056,128]{1,0:T(8,128)(2,1)}, bf16[1056,128]{1,0:T(8,128)(2,1)S(1)}, u32[]{:S(2)}, u32[]{:S(2)}) collective-permute-start(bf16[1056,128]{1,0:T(8,128)(2,1)} %get-tuple-element.80), channel_id=1, source_target_pairs={{0,3},{1,0},{2,1},{3,2},{4,7},{5,4},{6,5},{7,6},{8,11},{9,8},{10,9... | collective-permute-start | bytes 811016 | tf_op jit(solution)/shard_map/ppermute | solution.py:447
  63.5 1.9 collective-permute-start.7
  66.2 19.8 %copy-start.9 = (s32[1,4096]{1,0:T(1,128)S(1)}, s32[1,4096]{1,0:T(1,128)}, u32[]{:S(2)}) copy-start(s32[1,4096]{1,0:T(1,128)} %param.14) | copy-start | bytes 49156
  74.2 23.0 %all-to-all-start.2 = ((bf16[16,128,128]{2,1,0:T(8,128)(2,1)}), bf16[16,128,128]{2,1,0:T(8,128)(2,1)}, u32[]{:S(2)}, u32[]{:S(2)}) async-start(bf16[16,128,128]{2,1,0:T(8,128)(2,1)} %get-tuple-element.87), calls=%async_computation.2 | async-start | bytes 1048576 | tf_op jit(solution)/shard_map/all_to_all | solution.py:451
  81.2 9.8 %collective-permute-start.8 = (bf16[1024,128]{1,0:T(8,128)(2,1)}, bf16[1024,128]{1,0:T(8,128)(2,1)S(1)}, u32[]{:S(2)}, u32[]{:S(2)}) collective-permute-start(bf16[1024,128]{1,0:T(8,128)(2,1)} %get-tuple-element.89), channel_id=1, source_target_pairs={{0,1},{1,2},{2,3},{3,0},{4,5},{5,6},{6,7},{7,4},{8,9},{9,10},{10,1... | collective-permute-start | bytes 786440 | tf_op jit(solution)/shard_map/ppermute | solution.py:447
  82.7 14.5 %collective-permute-start.9 = (bf16[1024,128]{1,0:T(8,128)(2,1)}, bf16[1024,128]{1,0:T(8,128)(2,1)S(1)}, u32[]{:S(2)}, u32[]{:S(2)}) collective-permute-start(bf16[1024,128]{1,0:T(8,128)(2,1)} %get-tuple-element.90), channel_id=1, source_target_pairs={{0,2},{1,3},{2,0},{3,1},{4,6},{5,7},{6,4},{7,5},{8,10},{9,11},{10,... | collective-permute-start | bytes 786440 | tf_op jit(solution)/shard_map/ppermute | solution.py:447
  85.3 11.9 %collective-permute-start.10 = (bf16[1024,128]{1,0:T(8,128)(2,1)}, bf16[1024,128]{1,0:T(8,128)(2,1)S(1)}, u32[]{:S(2)}, u32[]{:S(2)}) collective-permute-start(bf16[1024,128]{1,0:T(8,128)(2,1)} %get-tuple-element.91), channel_id=1, source_target_pairs={{0,3},{1,0},{2,1},{3,2},{4,7},{5,4},{6,5},{7,6},{8,11},{9,8},{10,9... | collective-permute-start | bytes 786440 | tf_op jit(solution)/shard_map/ppermute | solution.py:447
  97.2 2.3 %collective-permute-start.11 = (bf16[16,128,128]{2,1,0:T(8,128)(2,1)}, bf16[16,128,128]{2,1,0:T(8,128)(2,1)}, u32[]{:S(2)}, u32[]{:S(2)}) collective-permute-start(bf16[16,128,128]{2,1,0:T(8,128)(2,1)} %all-to-all-done.2.near), channel_id=1, source_target_pairs={{0,4},{4,0},{1,5},{5,1},{2,6},{6,2},{3,7},{7,3},{8,12},{12,8},{9,1... | collective-permute-start | bytes 1572872 | tf_op jit(solution)/shard_map/ppermute | solution.py:447
  107.3 10.2 %collective-permute-start.12 = (bf16[1024,128]{1,0:T(8,128)(2,1)}, bf16[1024,128]{1,0:T(8,128)(2,1)S(1)}, u32[]{:S(2)}, u32[]{:S(2)}) collective-permute-start(bf16[1024,128]{1,0:T(8,128)(2,1)} %get-tuple-element.99), channel_id=1, source_target_pairs={{0,1},{1,2},{2,3},{3,0},{4,5},{5,6},{6,7},{7,4},{8,9},{9,10},{10,1... | collective-permute-start | bytes 786440 | tf_op jit(solution)/shard_map/ppermute | solution.py:447
  108.7 14.7 %collective-permute-start.13 = (bf16[1024,128]{1,0:T(8,128)(2,1)}, bf16[1024,128]{1,0:T(8,128)(2,1)S(1)}, u32[]{:S(2)}, u32[]{:S(2)}) collective-permute-start(bf16[1024,128]{1,0:T(8,128)(2,1)} %get-tuple-element.100), channel_id=1, source_target_pairs={{0,2},{1,3},{2,0},{3,1},{4,6},{5,7},{6,4},{7,5},{8,10},{9,11},{10,... | collective-permute-start | bytes 786440 | tf_op jit(solution)/shard_map/ppermute | solution.py:447
  111.3 12.1 %collective-permute-start.14 = (bf16[1024,128]{1,0:T(8,128)(2,1)}, bf16[1024,128]{1,0:T(8,128)(2,1)S(1)}, u32[]{:S(2)}, u32[]{:S(2)}) collective-permute-start(bf16[1024,128]{1,0:T(8,128)(2,1)} %get-tuple-element.101), channel_id=1, source_target_pairs={{0,3},{1,0},{2,1},{3,2},{4,7},{5,4},{6,5},{7,6},{8,11},{9,8},{10,9... | collective-permute-start | bytes 786440 | tf_op jit(solution)/shard_map/ppermute | solution.py:447
  146.8 9.7 %collective-permute-start.15 = (bf16[4,16,16,1024]{3,2,1,0:T(8,128)(2,1)S(1)}, bf16[4,16,16,1024]{3,2,1,0:T(8,128)(2,1)S(1)}, u32[]{:S(2)}, u32[]{:S(2)}) collective-permute-start(bf16[4,16,16,1024]{3,2,1,0:T(8,128)(2,1)S(1)} %get-tuple-element.112), channel_id=1, source_target_pairs={{0,4},{4,0},{1,5},{5,1},{2,6},{6,2},{3,7},{7,3},{8,12},{12,8},{9,1... | collective-permute-start | bytes 6291464 | tf_op jit(solution)/shard_map/ppermute | solution.py:447
  146.9 6.0 %collective-permute-start.20 = (bf16[4,16,16,640]{3,2,1,0:T(8,128)(2,1)S(1)}, bf16[4,16,16,640]{3,2,1,0:T(8,128)(2,1)S(1)}, u32[]{:S(2)}, u32[]{:S(2)}) collective-permute-start(bf16[4,16,16,640]{3,2,1,0:T(8,128)(2,1)S(1)} %get-tuple-element.121), channel_id=1, source_target_pairs={{0,4},{4,0},{1,5},{5,1},{2,6},{6,2},{3,7},{7,3},{8,12},{12,8},{9,1... | collective-permute-start | bytes 3932168 | tf_op jit(solution)/shard_map/ppermute | solution.py:447
  153.3 7.5 %collective-permute-start.21 = (bf16[8,16,640]{2,1,0:T(8,128)(2,1)S(1)}, bf16[8,16,640]{2,1,0:T(8,128)(2,1)S(1)}, u32[]{:S(2)}, u32[]{:S(2)}) collective-permute-start(bf16[8,16,640]{2,1,0:T(8,128)(2,1)S(1)} %get-tuple-element.125), channel_id=1, source_target_pairs={{0,32},{32,64},{64,96},{96,0},{1,33},{33,65},{65,97},{97,1},{2,34}... | collective-permute-start | bytes 491528 | tf_op jit(solution)/shard_map/ppermute | solution.py:447
  154.9 6.0 %collective-permute-start.22 = (bf16[8,16,640]{2,1,0:T(8,128)(2,1)S(1)}, bf16[8,16,640]{2,1,0:T(8,128)(2,1)S(1)}, u32[]{:S(2)}, u32[]{:S(2)}) collective-permute-start(bf16[8,16,640]{2,1,0:T(8,128)(2,1)S(1)} %get-tuple-element.126), channel_id=1, source_target_pairs={{0,96},{32,0},{64,32},{96,64},{1,97},{33,1},{65,33},{97,65},{2,98}... | collective-permute-start | bytes 491528 | tf_op jit(solution)/shard_map/ppermute | solution.py:447
  157.0 9.2 %collective-permute-start.16 = (bf16[8,16,1024]{2,1,0:T(8,128)(2,1)S(1)}, bf16[8,16,1024]{2,1,0:T(8,128)(2,1)S(1)}, u32[]{:S(2)}, u32[]{:S(2)}) collective-permute-start(bf16[8,16,1024]{2,1,0:T(8,128)(2,1)S(1)} %get-tuple-element.116), channel_id=1, source_target_pairs={{0,1},{1,2},{2,3},{3,0},{4,5},{5,6},{6,7},{7,4},{8,9},{9,10},{10,1... | collective-permute-start | bytes 786440 | tf_op jit(solution)/shard_map/ppermute | solution.py:447
  158.4 7.9 %collective-permute-start.17 = (bf16[8,16,1024]{2,1,0:T(8,128)(2,1)S(1)}, bf16[8,16,1024]{2,1,0:T(8,128)(2,1)S(1)}, u32[]{:S(2)}, u32[]{:S(2)}) collective-permute-start(bf16[8,16,1024]{2,1,0:T(8,128)(2,1)S(1)} %get-tuple-element.117), channel_id=1, source_target_pairs={{0,3},{1,0},{2,1},{3,2},{4,7},{5,4},{6,5},{7,6},{8,11},{9,8},{10,9... | collective-permute-start | bytes 786440 | tf_op jit(solution)/shard_map/ppermute | solution.py:447
  160.9 10.2 %collective-permute-start.23 = (bf16[16,16,640]{2,1,0:T(8,128)(2,1)S(1)}, bf16[16,16,640]{2,1,0:T(8,128)(2,1)S(1)}, u32[]{:S(2)}, u32[]{:S(2)}) collective-permute-start(bf16[16,16,640]{2,1,0:T(8,128)(2,1)S(1)} %get-tuple-element.127), channel_id=1, source_target_pairs={{0,32},{32,64},{64,96},{96,0},{1,33},{33,65},{65,97},{97,1},{2,34}... | collective-permute-start | bytes 983048 | tf_op jit(solution)/shard_map/ppermute | solution.py:447
  162.4 8.7 %collective-permute-start.24 = (bf16[16,16,640]{2,1,0:T(8,128)(2,1)S(1)}, bf16[16,16,640]{2,1,0:T(8,128)(2,1)S(1)}, u32[]{:S(2)}, u32[]{:S(2)}) collective-permute-start(bf16[16,16,640]{2,1,0:T(8,128)(2,1)S(1)} %get-tuple-element.128), channel_id=1, source_target_pairs={{0,96},{32,0},{64,32},{96,64},{1,97},{33,1},{65,33},{97,65},{2,98}... | collective-permute-start | bytes 983048 | tf_op jit(solution)/shard_map/ppermute | solution.py:447
  166.4 13.9 %collective-permute-start.18 = (bf16[16,16,1024]{2,1,0:T(8,128)(2,1)S(1)}, bf16[16,16,1024]{2,1,0:T(8,128)(2,1)S(1)}, u32[]{:S(2)}, u32[]{:S(2)}) collective-permute-start(bf16[16,16,1024]{2,1,0:T(8,128)(2,1)S(1)} %get-tuple-element.118), channel_id=1, source_target_pairs={{0,1},{1,2},{2,3},{3,0},{4,5},{5,6},{6,7},{7,4},{8,9},{9,10},{10,1... | collective-permute-start | bytes 1572872 | tf_op jit(solution)/shard_map/ppermute | solution.py:447
  167.3 13.4 %collective-permute-start.19 = (bf16[16,16,1024]{2,1,0:T(8,128)(2,1)S(1)}, bf16[16,16,1024]{2,1,0:T(8,128)(2,1)S(1)}, u32[]{:S(2)}, u32[]{:S(2)}) collective-permute-start(bf16[16,16,1024]{2,1,0:T(8,128)(2,1)S(1)} %get-tuple-element.119), channel_id=1, source_target_pairs={{0,3},{1,0},{2,1},{3,2},{4,7},{5,4},{6,5},{7,6},{8,11},{9,8},{10,9... | collective-permute-start | bytes 1572872 | tf_op jit(solution)/shard_map/ppermute | solution.py:447
  171.9 15.3 %all-to-all-start.4 = ((bf16[16,16,640]{2,1,0:T(8,128)(2,1)}), bf16[16,16,640]{2,1,0:T(8,128)(2,1)S(1)}, u32[]{:S(2)}, u32[]{:S(2)}) async-start(bf16[16,16,640]{2,1,0:T(8,128)(2,1)} %own_middle.1), calls=%async_computation.4 | async-start | bytes 655360 | tf_op jit(solution)/shard_map/all_to_all | solution.py:451
  (14 other events, 109.6 us)
